TPU v7x, 1024 devices: a whole 4x8x16 slice. The times are simulated.
1024 devices in a mesh: section: 2 (over y_lo), scene: 32 (over z, core), mp: 16 (over x, y_hi).
Axes of the slice: x: 4, y: 8 (y_hi: 4, y_lo: 2; y = y_hi * 2 + y_lo), z: 16, core: 2. Of those that a mesh axis runs over, the one named last changes fastest.
Arguments:
- dec_grad: bfloat16 [32, 32, 256, 4096], P('scene', ('section', 'mp')), may hold values from -1.0546875 to 1.0546875
- agent_queries: bfloat16 [32, 256, 4096], P('scene', None, ('section', 'mp')), as said below
- map_keys: bfloat16 [32, 1024, 4096], P('scene', None, ('section', 'mp')), as said below
- map_values: bfloat16 [32, 1024, 4096], P('scene', None, ('section', 'mp')), may hold values from -6 to 6
- w_out: bfloat16 [4096, 4096], P(('section', 'mp'), 'scene'), may hold values from -0.09375 to 0.09375
- block_mask: int32 [32, 2, 8], P('scene'), may hold values from 0 to 1, as said below
- agent_count: int32 [32], P('scene'), may hold values from 64 to 256
Outputs:
- d_queries: bfloat16 [32, 256, 4096], P('scene', None, ('section', 'mp'))
- d_keys: bfloat16 [32, 1024, 4096], P('scene', None, ('section', 'mp'))
- d_values: bfloat16 [32, 1024, 4096], P('scene', None, ('section', 'mp'))
- d_wout: float32 [4096, 4096], P(('section', 'mp'), 'scene')
Inputs may be any that keep to these rules, and one draw needn't show every extreme that they name: `block_mask`: every agent block of a scene sees map block 0. In each scene at most 4 map blocks are seen by some agent block, and some scene reaches 4. `agent_queries`: entries are finite and of moderate size. `map_keys`: entries are finite and of moderate size.
All inputs are finite; a program needn't handle non-finite values.
Results may differ from a plain program's by a relative error of at most 0.04.
Values may be sent and summed in bfloat16 or wider, within the bound.
No kernel may reach another device: no remote copies, remote signals or barrier semaphores. Data moves between devices by JAX's collectives and lax.ppermute only.
A program may use at most 32 MiB of HBM per device.

v0:
```python
import math

import jax
import jax.numpy as jnp
from jax import lax
from jax.sharding import PartitionSpec as P

HEAD_DIM = 128


def attend_forward(query_heads, key_heads, value_heads, visible, scaling):
    scores = (
        jnp.einsum("qhd,khd->hqk", query_heads, key_heads, preferred_element_type=jnp.float32)
        * scaling
    )
    scores = jnp.where(visible[None], scores, -1e30)
    largest = jnp.max(scores, axis=-1, keepdims=True)
    exponent = jnp.exp(scores - largest)
    probs = exponent / jnp.sum(exponent, axis=-1, keepdims=True)
    weights = probs.astype(jnp.bfloat16)
    attended = jnp.einsum("hqk,khd->qhd", weights, value_heads, preferred_element_type=jnp.float32)
    return (probs, weights, attended)


def attend_backward(
    query_heads, key_heads, value_heads, grad_heads, probs, weights, attended, scaling
):
    delta = jnp.sum(grad_heads.astype(jnp.float32) * attended, axis=-1)
    d_values = jnp.einsum(
        "hqk,qhd->khd", weights, grad_heads, preferred_element_type=jnp.float32
    ).astype(jnp.bfloat16)
    d_probs = jnp.einsum(
        "qhd,khd->hqk", grad_heads, value_heads, preferred_element_type=jnp.float32
    )
    score_grads = (probs * (d_probs - delta.T[:, :, None])).astype(jnp.bfloat16)
    d_queries = (
        scaling
        * jnp.einsum("hqk,khd->qhd", score_grads, key_heads, preferred_element_type=jnp.float32)
    ).astype(jnp.bfloat16)
    d_keys = (
        scaling
        * jnp.einsum("hqk,qhd->khd", score_grads, query_heads, preferred_element_type=jnp.float32)
    ).astype(jnp.bfloat16)
    return (d_queries, d_keys, d_values)


def reduce_weights(attended_rounded, upstream):
    term = jnp.einsum("qh,qd->hd", attended_rounded, upstream, preferred_element_type=jnp.float32)
    return lax.psum_scatter(term, "scene", scatter_dimension=1, tiled=True)


def shards(dec_grad, agent_queries, map_keys, map_values, w_out, block_mask, agent_count):
    scaling = 1.0 / math.sqrt(HEAD_DIM)
    partial_sum = jnp.sum(dec_grad[0].astype(jnp.float32), axis=0).astype(jnp.bfloat16)
    agent_total = agent_count[0]
    token_rows = partial_sum.shape[0]
    summed = lax.psum(partial_sum, ("section", "mp")).astype(jnp.float32)
    row_keep = jnp.arange(token_rows) < agent_total
    upstream = jnp.where(row_keep[:, None], summed, 0.0).astype(jnp.bfloat16)
    proj_width = w_out.shape[0]
    d_attn = jnp.einsum(
        "td,hd->th",
        upstream,
        lax.all_gather(w_out, "scene", axis=1, tiled=True),
        preferred_element_type=jnp.float32,
    ).astype(jnp.bfloat16)
    head_count = proj_width // HEAD_DIM
    query_heads = agent_queries[0].reshape(token_rows, head_count, HEAD_DIM)
    grad_heads = d_attn.reshape(token_rows, head_count, HEAD_DIM)
    key_rows = map_keys[0]
    value_rows = map_values[0]
    mask_rows = block_mask[0]
    map_blocks = mask_rows.shape[1]
    block_size = key_rows.shape[0] // map_blocks
    visible = jnp.repeat(jnp.repeat(mask_rows == 1, block_size, axis=0), block_size, axis=1)
    key_heads = key_rows.reshape(-1, head_count, HEAD_DIM)
    value_heads = value_rows.reshape(-1, head_count, HEAD_DIM)
    probs, weights, attended = attend_forward(query_heads, key_heads, value_heads, visible, scaling)
    attended_rounded = attended.astype(jnp.bfloat16).reshape(token_rows, proj_width)
    d_queries, d_keys, d_values = attend_backward(
        query_heads, key_heads, value_heads, grad_heads, probs, weights, attended, scaling
    )
    d_wout = reduce_weights(attended_rounded, upstream)
    d_keys_out = d_keys.reshape(-1, proj_width)
    d_values_out = d_values.reshape(-1, proj_width)
    return (
        d_queries.reshape(token_rows, proj_width)[None],
        d_keys_out[None],
        d_values_out[None],
        d_wout,
    )


def solution(mesh):
    return jax.shard_map(
        shards,
        mesh=mesh,
        in_specs=(
            P("scene", ("section", "mp"), None, None),
            P("scene", None, ("section", "mp")),
            P("scene", None, ("section", "mp")),
            P("scene", None, ("section", "mp")),
            P(("section", "mp"), "scene"),
            P("scene", None, None),
            P("scene"),
        ),
        out_specs=(
            P("scene", None, ("section", "mp")),
            P("scene", None, ("section", "mp")),
            P("scene", None, ("section", "mp")),
            P(("section", "mp"), "scene"),
        ),
        check_vma=False,
    )
```

profile of v0, /device:TPU:4, one launch (start us, length us, event | category | flops | bytes accessed | tf_op | source)
XLA Modules:
  0.0 332.5 jit_solution(12409818577832359672)
XLA Ops:
  8.0 0.0 copy-start
  8.0 0.0 copy-start.4
  8.0 0.0 copy-start.3
  8.0 0.0 copy-start.2
  8.0 0.0 all-gather.2.cloned.1.call-start
  8.1 0.7 all-gather.2.cloned.1.call-update
  8.8 0.0 all-reduce.2.cloned.1.call-start
  8.8 0.5 all-reduce.2.cloned.1.call-update
  9.4 0.0 reduce-scatter.2.cloned.1.call-start
  10.1 0.0 copy-done.4
  10.1 0.3 broadcast_in_dim.26
  10.4 0.0 copy-done.3
  10.5 0.0 copy-done.2
  10.5 0.4 fusion.24
  10.9 0.3 fusion.9
  11.2 0.3 fusion.8
  11.5 82.0 %all-gather.2.cloned.1.call-done = bf16[128,4096]{1,0:T(8,128)(2,1)} async-done(((bf16[128,128]{1,0:T(8,128)(2,1)}), bf16[128,4096]{1,0:T(8,128)(2,1)}) %all-gather.2.cloned.1.call-update) | async-done | bytes 1048592 | tf_op jit(solution)/shard_map/all_gather | solution.py:64
  93.5 112.8 %all-reduce.2.cloned.1.call-done = bf16[256,4096]{1,0:T(8,128)(2,1)} async-done(((bf16[256,4096]{1,0:T(8,128)(2,1)}), bf16[256,4096]{1,0:T(8,128)(2,1)}) %all-reduce.2.cloned.1.call-update) | async-done | bytes 2097168 | tf_op jit(solution)/shard_map/psum | solution.py:57
  206.3 0.0 copy-start.1
  206.3 2.9 convolution_convert_fusion.1
  209.2 0.0 copy-done
  209.2 0.3 fusion.17
  209.6 0.0 copy-done.1
  209.6 1.9 fusion.10
  211.4 0.0 reduce-scatter.2.cloned.1.call-update
  211.5 0.2 fusion.5
  211.7 0.8 copy.11
  212.6 0.3 fusion.2
  212.9 1.1 fusion.4
  213.9 0.9 fusion.7
  214.9 110.2 %reduce-scatter.2.cloned.1.call-done = f32[128,128]{1,0:T(8,128)} async-done(((f32[128,4096]{1,0:T(8,128)}), f32[128,128]{1,0:T(8,128)}) %reduce-scatter.2.cloned.1.call-update) | async-done | bytes 65552 | tf_op jit(solution)/shard_map/reduce_scatter | solution.py:49
  (3 shorter events, 0.0 us)
Async XLA Ops:
  8.0 201.2 %copy-start = (bf16[1,1024,128]{2,1,0:T(8,128)(2,1)S(1)}, bf16[1,1024,128]{2,1,0:T(8,128)(2,1)}, u32[]{:S(2)}) copy-start(bf16[1,1024,128]{2,1,0:T(8,128)(2,1)} %param.10) | copy-start | bytes 786436
  8.0 2.1 copy-start.4
  8.0 2.4 copy-start.3
  8.0 2.4 copy-start.2
  8.0 85.4 %all-gather.2.cloned.1.call-start = ((), (), s32[]{:S(2)}) async-start(), calls=%async_computation.2 | async-start | bytes 1081344 | tf_op jit(solution)/shard_map/all_gather | solution.py:64
  8.8 197.5 %all-reduce.2.cloned.1.call-start = ((), (), s32[]{:S(2)}) async-start(), calls=%async_computation.1 | async-start | bytes 4194304 | tf_op jit(solution)/shard_map/psum | solution.py:57
  9.4 315.7 %reduce-scatter.2.cloned.1.call-start = ((), (), s32[]{:S(2)}) async-start(), calls=%async_computation.3 | async-start | bytes 2162688 | tf_op jit(solution)/shard_map/reduce_scatter | solution.py:49
  206.3 3.3 copy-start.1
Sparse Core Ops, SparseCore 0:
  11.5 81.9 all-gather.1
  211.6 113.3 reduce-scatter.1
Sparse Core Ops, SparseCore 1:
  12.8 193.5 all-reduce.1
where the time goes:
time: 333 us; the launch traced here: 332 us
  waiting for transfers between devices  306 us (92%)
  between operations  16.3 us (5%)
  matrix products  8.08 us (2%)
    psum x1, waiting for transfers between devices, shards(): summed = lax.psum(partial_sum, ('section', 'mp')).astype(jnp.float32)  113 us
    reduce_scatter x1, waiting for transfers between devices, reduce_weights(): return lax.psum_scatter(term, 'scene', scatter_dimension=1, tiled=True)  110 us
    all_gather x1, waiting for transfers between devices, shards(): lax.all_gather(w_out, 'scene', axis=1, tiled=True)  82 us
  transfers between devices with their start and end apart: 3, of which 3 were waited for; matrix products, arithmetic and copies ran while one was open for 1% of the time, Pallas kernels for 0%

commit v1 on v0

v1 whole, which is shorter than its diff:
```python
import math

import jax
import jax.numpy as jnp
from jax import lax
from jax.experimental import pallas as pl
from jax.experimental.pallas import tpu as pltpu
from jax.sharding import PartitionSpec as P

HEAD_DIM = 128
XY = ("section", "mp")
X, YH, YL = 4, 4, 2
ZH, ZL, CORES = 4, 4, 2


def xy_index(x, y):
    return (y % YL) * (X * YH) + x * YH + y // YL


def scene_index(zh, zl, core):
    return (zh * ZL + zl) * CORES + core


def shift_x(k):
    return [(x * YH + y, ((x + k) % X) * YH + y) for x in range(X) for y in range(YH)]


def shift_zl(k):
    return [
        (scene_index(a, b, c), scene_index(a, (b + k) % ZL, c))
        for a in range(ZH)
        for b in range(ZL)
        for c in range(CORES)
    ]


def shift_zh(k):
    return [
        (scene_index(a, b, c), scene_index((a + k) % ZH, b, c))
        for a in range(ZH)
        for b in range(ZL)
        for c in range(CORES)
    ]


def other_core():
    return [(s, s ^ 1) for s in range(ZH * ZL * CORES)]


def y_groups():
    return [[xy_index(x, y) for y in range(YH * YL)] for x in range(X)]


def z_groups():
    return [[z * CORES + c for z in range(ZH * ZL)] for c in range(CORES)]


def attend_forward(queries, keys, values, visible, scaling):
    scores = jnp.einsum("qd,kd->qk", queries, keys, preferred_element_type=jnp.float32) * scaling
    scores = jnp.where(visible, scores, -1e30)
    largest = jnp.max(scores, axis=-1, keepdims=True)
    exponent = jnp.exp(scores - largest)
    probs = exponent / jnp.sum(exponent, axis=-1, keepdims=True)
    weights = probs.astype(jnp.bfloat16)
    attended = jnp.einsum("qk,kd->qd", weights, values, preferred_element_type=jnp.float32)
    return probs, weights, attended


def attend_backward(queries, keys, values, grads, probs, weights, attended, scaling):
    delta = jnp.sum(grads.astype(jnp.float32) * attended, axis=-1)
    d_values = jnp.einsum("qk,qd->kd", weights, grads, preferred_element_type=jnp.float32)
    d_probs = jnp.einsum("qd,kd->qk", grads, values, preferred_element_type=jnp.float32)
    score_grads = (probs * (d_probs - delta[:, None])).astype(jnp.bfloat16)
    d_queries = scaling * jnp.einsum(
        "qk,kd->qd", score_grads, keys, preferred_element_type=jnp.float32
    )
    d_keys = scaling * jnp.einsum(
        "qk,qd->kd", score_grads, queries, preferred_element_type=jnp.float32
    )
    return [g.astype(jnp.bfloat16) for g in (d_queries, d_keys, d_values)]


def weight_terms_kernel(core_ref, attended_ref, *refs):
    blocks, (send_ref, keep_ref) = refs[:X], refs[X:]
    first = core_ref[0] == 0
    for k in range(X):
        term = lax.dot_general(
            attended_ref[...],
            blocks[k][...],
            (((0,), (0,)), ((), ())),
            preferred_element_type=jnp.float32,
        )
        for b in range(ZL):
            left = b * CORES * HEAD_DIM
            low = term[:, left : left + HEAD_DIM]
            high = term[:, left + HEAD_DIM : left + 2 * HEAD_DIM]
            send_ref[b, k] = jnp.where(first, high, low).astype(jnp.bfloat16)
            keep_ref[b, k] = jnp.where(first, low, high)


def weight_terms(core, attended, blocks):
    rows, width = blocks[0].shape
    shape = (ZL, X, HEAD_DIM, HEAD_DIM)
    vmem = pl.BlockSpec(memory_space=pltpu.VMEM)
    return pl.pallas_call(
        weight_terms_kernel,
        out_shape=(
            jax.ShapeDtypeStruct(shape, jnp.bfloat16),
            jax.ShapeDtypeStruct(shape, jnp.float32),
        ),
        in_specs=[pl.BlockSpec(memory_space=pltpu.SMEM)] + [vmem] * (1 + X),
        out_specs=(vmem, vmem),
        compiler_params=pltpu.CompilerParams(vmem_limit_bytes=24 << 20),
        cost_estimate=pl.CostEstimate(
            flops=2 * rows * width * X * HEAD_DIM,
            bytes_accessed=2 * rows * width * X + 6 * width * X * HEAD_DIM // 2,
            transcendentals=0,
        ),
        name="weight_terms",
    )(core.reshape(1), attended, *blocks)


def shift_right(number, size):
    return lax.shift_right_logical(number, size.bit_length() - 1)


def sum_f32(parts):
    total = parts[0].astype(jnp.float32)
    for part in parts[1:]:
        total = total + part.astype(jnp.float32)
    return total


def shards(dec_grad, agent_queries, map_keys, map_values, w_out, block_mask, agent_count):
    scaling = 1.0 / math.sqrt(HEAD_DIM)
    section, mp, scene = (lax.axis_index(name) for name in ("section", "mp", "scene"))
    x, y = shift_right(mp, YH), (mp & (YH - 1)) * YL + section
    zh, zl = shift_right(scene, ZL * CORES), shift_right(scene, CORES) & (ZL - 1)
    core = scene & (CORES - 1)
    sample = dec_grad[0, 0]
    tokens, model = sample.shape
    width = model // X

    with jax.named_scope("gather_projection"):
        w_other = lax.ppermute(w_out, "scene", other_core())
        w_chip = jnp.concatenate(
            [jnp.where(core == 0, w_out, w_other), jnp.where(core == 0, w_other, w_out)], axis=1
        )
        w_full = lax.all_gather(w_chip, "scene", axis=1, tiled=True, axis_index_groups=z_groups())

    with jax.named_scope("sum_over_x"):
        pieces = [
            lax.dynamic_slice(sample, (0, ((x + k) & (X - 1)) * width), (tokens, width))
            for k in range(X)
        ]
        arrived = [lax.ppermute(pieces[k], "mp", shift_x(k)) for k in range(1, X)]
        partial = sum_f32([pieces[0]] + arrived).astype(jnp.bfloat16)

    queries, keys, values = agent_queries[0], map_keys[0], map_values[0]
    mask_rows = block_mask[0]
    agent_block, map_block = tokens // mask_rows.shape[0], keys.shape[0] // mask_rows.shape[1]
    visible = jnp.repeat(jnp.repeat(mask_rows == 1, agent_block, axis=0), map_block, axis=1)
    probs, weights, attended = attend_forward(queries, keys, values, visible, scaling)
    attended_rounded = attended.astype(jnp.bfloat16)

    with jax.named_scope("sum_over_y"):
        rows = tokens // (YH * YL)
        lines = lax.all_to_all(
            partial.reshape(YH * YL, rows, width), XY, 0, 0, axis_index_groups=y_groups()
        )
        summed = jnp.sum(lines.astype(jnp.float32), axis=0)
        row_keep = y * rows + jnp.arange(rows) < agent_count[0]
        own = jnp.where(row_keep[:, None], summed, 0.0).astype(jnp.bfloat16)

    with jax.named_scope("gather_over_y"):
        spread = jnp.broadcast_to(own[None], (YH * YL, rows, width))
        block = lax.all_to_all(spread, XY, 0, 0, axis_index_groups=y_groups())
        block = block.reshape(tokens, width)

    with jax.named_scope("gather_over_x"):
        upstream = [block] + [lax.ppermute(block, "mp", shift_x(-k)) for k in range(1, X)]

    with jax.named_scope("weight_terms"):
        send, keep = weight_terms(core, attended_rounded, upstream)

    with jax.named_scope("sum_over_core"):
        pair = sum_f32([keep, lax.ppermute(send, "scene", other_core())]).astype(jnp.bfloat16)

    with jax.named_scope("sum_over_z_lo"):
        parts = [
            lax.dynamic_index_in_dim(pair, (zl + k) & (ZL - 1), 0, keepdims=False) for k in range(ZL)
        ]
        near = sum_f32(
            parts[:1] + [lax.ppermute(parts[k], "scene", shift_zl(k)) for k in range(1, ZL)]
        ).astype(jnp.bfloat16)

    with jax.named_scope("sum_over_z_hi"):
        parts = [
            lax.dynamic_index_in_dim(near, (zh + k - x) & (X - 1), 0, keepdims=False)
            for k in range(ZH)
        ]
        d_wout = sum_f32(
            parts[:1] + [lax.ppermute(parts[k], "scene", shift_zh(k)) for k in range(1, ZH)]
        )

    with jax.named_scope("head_gradients"):
        upstream, w_full, _ = lax.optimization_barrier((upstream, w_full, pair))
        d_attn = sum(
            jnp.einsum(
                "td,hd->th",
                upstream[k],
                lax.dynamic_slice(w_full, (0, ((x + k) & (X - 1)) * width), (HEAD_DIM, width)),
                preferred_element_type=jnp.float32,
            )
            for k in range(X)
        ).astype(jnp.bfloat16)
        d_queries, d_keys, d_values = attend_backward(
            queries, keys, values, d_attn, probs, weights, attended, scaling
        )
    return d_queries[None], d_keys[None], d_values[None], d_wout


def solution(mesh):
    heads = P("scene", None, XY)
    return jax.shard_map(
        shards,
        mesh=mesh,
        in_specs=(
            P("scene", XY, None, None),
            heads,
            heads,
            heads,
            P(XY, "scene"),
            P("scene", None, None),
            P("scene"),
        ),
        out_specs=(heads, heads, heads, P(XY, "scene")),
        check_vma=False,
    )
```

time: 333 us -> 205 us (0.62)
  the two profiles are of different devices: /device:TPU:4 before, /device:TPU:12 now
where the time goes in v1:
time: 205 us; the launch traced here: 204 us
  waiting for transfers between devices  97.4 us (48%)
  starting transfers between devices  68.1 us (33%)
  between operations  15.1 us (7%)
  matrix products  10.2 us (5%)
  other arithmetic  6.61 us (3%)
  local copies, waits for them, and re-layouts  5.4 us (3%)
    all_gather x1, waiting for transfers between devices, shards(): lax.all_gather(w_chip, 'scene', axis=1, tiled=True, axis_index_groups=z_g...  22.9 us
    ppermute x3, waiting for transfers between devices, shards(): arrived = [lax.ppermute(pieces[k], 'mp', shift_x(k)) for k in range(1, X)]  21.6 us
    ppermute x3, waiting for transfers between devices, shards(): lax.ppermute(block, 'mp', shift_x(-k))  18.7 us
    ppermute x3, starting transfers between devices, shards(): lax.ppermute(parts[k], 'scene', shift_zh(k))  18 us
    all_to_all x1, waiting for transfers between devices, shards(): block = lax.all_to_all(spread, XY, 0, 0, axis_index_groups=y_groups())  12.6 us
    all_to_all x1, waiting for transfers between devices, shards(): lax.all_to_all(partial.reshape(YH * YL, rows, width), XY, 0, 0, axis_inde...  12.6 us
    ppermute x3, starting transfers between devices, shards(): lax.ppermute(parts[k], 'scene', shift_zl(k))  12.4 us
    ppermute x3, starting transfers between devices, shards(): lax.ppermute(block, 'mp', shift_x(-k))  12.3 us
  transfers between devices with their start and end apart: 17, of which 10 were waited for; matrix products, arithmetic and copies ran while one was open for 7% of the time, Pallas kernels for 1%

profile of v1, /device:TPU:12, one launch (start us, length us, event | category | flops | bytes accessed | tf_op | source)
XLA Modules:
  0.0 204.0 jit_solution(13853791199942012984)
XLA Ops:
  7.2 1.5 dynamic-slice_bitcast_fusion.2
  8.7 3.1 %collective-permute-start = (bf16[256,1024]{1,0:T(8,128)(2,1)S(1)}, bf16[256,1024]{1,0:T(8,128)(2,1)S(1)}, u32[]{:S(2)}, u32[]{:S(2)}) collective-permute-start(bf16[256,1024]{1,0:T(8,128)(2,1)S(1)} %get-tuple-element.18), channel_id=1, source_target_pairs={{0,4},{1,5},{2,6},{3,7},{4,8},{5,9},{6,10},{7,11},{8,12},{9,13},{1... | collective-permute-start | bytes 1572872 | tf_op jit(solution)/shard_map/sum_over_x/ppermute | solution.py:156
  11.8 2.7 %collective-permute-start.1 = (bf16[256,1024]{1,0:T(8,128)(2,1)S(1)}, bf16[256,1024]{1,0:T(8,128)(2,1)S(1)}, u32[]{:S(2)}, u32[]{:S(2)}) collective-permute-start(bf16[256,1024]{1,0:T(8,128)(2,1)S(1)} %get-tuple-element.20), channel_id=1, source_target_pairs={{0,8},{1,9},{2,10},{3,11},{4,12},{5,13},{6,14},{7,15},{8,0},{9,1},... | collective-permute-start | bytes 1572872 | tf_op jit(solution)/shard_map/sum_over_x/ppermute | solution.py:156
  14.6 3.0 %collective-permute-start.2 = (bf16[256,1024]{1,0:T(8,128)(2,1)S(1)}, bf16[256,1024]{1,0:T(8,128)(2,1)S(1)}, u32[]{:S(2)}, u32[]{:S(2)}) collective-permute-start(bf16[256,1024]{1,0:T(8,128)(2,1)S(1)} %get-tuple-element.19), channel_id=1, source_target_pairs={{0,12},{1,13},{2,14},{3,15},{4,0},{5,1},{6,2},{7,3},{8,4},{9,5},{1... | collective-permute-start | bytes 1572872 | tf_op jit(solution)/shard_map/sum_over_x/ppermute | solution.py:156
  17.6 7.8 %collective-permute-done = bf16[256,1024]{1,0:T(8,128)(2,1)S(1)} collective-permute-done((bf16[256,1024]{1,0:T(8,128)(2,1)S(1)}, bf16[256,1024]{1,0:T(8,128)(2,1)S(1)}, u32[]{:S(2)}, u32[]{:S(2)}) %collective-permute-start) | collective-permute-done | bytes 524320 | tf_op jit(solution)/shard_map/sum_over_x/ppermute | solution.py:156
  25.4 10.1 %collective-permute-done.1 = bf16[256,1024]{1,0:T(8,128)(2,1)S(1)} collective-permute-done((bf16[256,1024]{1,0:T(8,128)(2,1)S(1)}, bf16[256,1024]{1,0:T(8,128)(2,1)S(1)}, u32[]{:S(2)}, u32[]{:S(2)}) %collective-permute-start.1) | collective-permute-done | bytes 524320 | tf_op jit(solution)/shard_map/sum_over_x/ppermute | solution.py:156
  35.5 3.7 %collective-permute-done.2 = bf16[256,1024]{1,0:T(8,128)(2,1)S(1)} collective-permute-done((bf16[256,1024]{1,0:T(8,128)(2,1)S(1)}, bf16[256,1024]{1,0:T(8,128)(2,1)S(1)}, u32[]{:S(2)}, u32[]{:S(2)}) %collective-permute-start.2) | collective-permute-done | bytes 524320 | tf_op jit(solution)/shard_map/sum_over_x/ppermute | solution.py:156
  39.3 2.2 %fusion.13 = bf16[256,1024]{1,0:T(8,128)(2,1)} fusion(bf16[256,1024]{1,0:T(8,128)(2,1)S(1)} %collective-permute-done.2, bf16[256,1024]{1,0:T(8,128)(2,1)S(1)} %collective-permute-done.1, bf16[256,1024]{1,0:T(8,128)(2,1)S(1)} %collective-permute-done, bf16[1,1,256,4096]{3,2,1,0:T(8,128)(2,1)} %param.7, s32[]{:T(128)S(6)} %select_n.67), kind=kLoop, calls=%fused_computation.20 | loop fusion | flops 2097152 | bytes 2621444 | tf_op jit(solution)/shard_map/sum_over_x/convert_element_type | solution.py:157
  41.5 7.7 %all-to-all-start = ((bf16[8,32,1024]{2,1,0:T(8,128)(2,1)}), bf16[8,32,1024]{2,1,0:T(8,128)(2,1)S(1)}, u32[]{:S(2)}, u32[]{:S(2)}) async-start(bf16[8,32,1024]{2,1,0:T(8,128)(2,1)} %bitcast.9), calls=%async_computation | async-start | bytes 1048576 | tf_op jit(solution)/shard_map/sum_over_y/all_to_all | solution.py:168
  49.2 1.9 collective-permute-start.6
  51.8 12.6 %all-to-all-done = bf16[8,32,1024]{2,1,0:T(8,128)(2,1)S(1)} async-done(((bf16[8,32,1024]{2,1,0:T(8,128)(2,1)}), bf16[8,32,1024]{2,1,0:T(8,128)(2,1)S(1)}, u32[]{:S(2)}, u32[]{:S(2)}) %all-to-all-start) | async-done | bytes 524320 | tf_op jit(solution)/shard_map/sum_over_y/all_to_all | solution.py:168
  64.5 0.9 broadcast_in_dim.46
  65.4 4.9 %all-to-all-start.1 = ((bf16[8,32,1024]{2,1,0:T(8,128)(2,1)}), bf16[8,32,1024]{2,1,0:T(8,128)(2,1)S(1)}, u32[]{:S(2)}, u32[]{:S(2)}) async-start(bf16[8,32,1024]{2,1,0:T(8,128)(2,1)} %broadcast_in_dim.46), calls=%async_computation.1 | async-start | bytes 1048576 | tf_op jit(solution)/shard_map/gather_over_y/all_to_all | solution.py:177
  70.2 0.6 pad_maximum_fusion
  71.0 0.3 broadcast_in_dim.42
  71.3 0.4 fusion.41
  72.1 12.6 %all-to-all-done.1 = bf16[8,32,1024]{2,1,0:T(8,128)(2,1)S(1)} async-done(((bf16[8,32,1024]{2,1,0:T(8,128)(2,1)}), bf16[8,32,1024]{2,1,0:T(8,128)(2,1)S(1)}, u32[]{:S(2)}, u32[]{:S(2)}) %all-to-all-start.1) | async-done | bytes 524320 | tf_op jit(solution)/shard_map/gather_over_y/all_to_all | solution.py:177
  84.7 6.4 %collective-permute-start.3 = (bf16[256,1024]{1,0:T(8,128)(2,1)S(1)}, bf16[256,1024]{1,0:T(8,128)(2,1)S(1)}, u32[]{:S(2)}, u32[]{:S(2)}) collective-permute-start(bf16[256,1024]{1,0:T(8,128)(2,1)S(1)} %bitcast.71), channel_id=1, source_target_pairs={{0,12},{1,13},{2,14},{3,15},{4,0},{5,1},{6,2},{7,3},{8,4},{9,5},{1... | collective-permute-start | bytes 1572872 | tf_op jit(solution)/shard_map/gather_over_x/ppermute | solution.py:181
  91.1 3.6 %collective-permute-start.4 = (bf16[256,1024]{1,0:T(8,128)(2,1)S(1)}, bf16[256,1024]{1,0:T(8,128)(2,1)S(1)}, u32[]{:S(2)}, u32[]{:S(2)}) collective-permute-start(bf16[256,1024]{1,0:T(8,128)(2,1)S(1)} %bitcast.72), channel_id=1, source_target_pairs={{0,8},{1,9},{2,10},{3,11},{4,12},{5,13},{6,14},{7,15},{8,0},{9,1},... | collective-permute-start | bytes 1572872 | tf_op jit(solution)/shard_map/gather_over_x/ppermute | solution.py:181
  94.7 2.3 %collective-permute-start.5 = (bf16[256,1024]{1,0:T(8,128)(2,1)S(1)}, bf16[256,1024]{1,0:T(8,128)(2,1)S(1)}, u32[]{:S(2)}, u32[]{:S(2)}) collective-permute-start(bf16[256,1024]{1,0:T(8,128)(2,1)S(1)} %bitcast.73), channel_id=1, source_target_pairs={{0,4},{1,5},{2,6},{3,7},{4,8},{5,9},{6,10},{7,11},{8,12},{9,13},{1... | collective-permute-start | bytes 1572872 | tf_op jit(solution)/shard_map/gather_over_x/ppermute | solution.py:181
  97.3 0.9 copy-done.1
  98.3 1.3 fusion.20
  99.7 13.1 %collective-permute-done.3.refs_1_ = bf16[256,1024]{1,0:T(8,128)(2,1)S(1)} collective-permute-done((bf16[256,1024]{1,0:T(8,128)(2,1)S(1)}, bf16[256,1024]{1,0:T(8,128)(2,1)S(1)}, u32[]{:S(2)}, u32[]{:S(2)}) %collective-permute-start.3) | collective-permute-done | bytes 524320 | tf_op jit(solution)/shard_map/gather_over_x/ppermute | solution.py:181
  112.7 5.6 %collective-permute-done.5.refs_3_ = bf16[256,1024]{1,0:T(8,128)(2,1)S(1)} collective-permute-done((bf16[256,1024]{1,0:T(8,128)(2,1)S(1)}, bf16[256,1024]{1,0:T(8,128)(2,1)S(1)}, u32[]{:S(2)}, u32[]{:S(2)}) %collective-permute-start.5) | collective-permute-done | bytes 524320 | tf_op jit(solution)/shard_map/gather_over_x/ppermute | solution.py:181
  118.3 1.3 weight_terms.1
  119.6 2.0 collective-permute-start.7
  121.6 2.1 %collective-permute-done.7 = bf16[4,4,128,128]{3,2,1,0:T(8,128)(2,1)} collective-permute-done((bf16[4,4,128,128]{3,2,1,0:T(8,128)(2,1)}, bf16[4,4,128,128]{3,2,1,0:T(8,128)(2,1)}, u32[]{:S(2)}, u32[]{:S(2)}) %collective-permute-start.7) | collective-permute-done | bytes 524320 | tf_op jit(solution)/shard_map/sum_over_core/ppermute | solution.py:187
  123.7 1.2 add_convert_fusion
  124.9 0.8 copy-done.3
  125.7 0.7 dynamic-slice_bitcast_fusion.5
  126.5 8.0 %collective-permute-start.10 = (bf16[4,128,128]{2,1,0:T(8,128)(2,1)}, bf16[4,128,128]{2,1,0:T(8,128)(2,1)}, u32[]{:S(2)}, u32[]{:S(2)}) collective-permute-start(bf16[4,128,128]{2,1,0:T(8,128)(2,1)} %get-tuple-element.22), channel_id=1, source_target_pairs={{0,96},{16,112},{32,0},{48,16},{64,32},{80,48},{96,64},{112,80},{1... | collective-permute-start | bytes 393224 | tf_op jit(solution)/shard_map/sum_over_z_lo/ppermute | solution.py:194
  134.5 1.9 collective-permute-start.8
  136.4 2.5 %collective-permute-start.9 = (bf16[4,128,128]{2,1,0:T(8,128)(2,1)}, bf16[4,128,128]{2,1,0:T(8,128)(2,1)}, u32[]{:S(2)}, u32[]{:S(2)}) collective-permute-start(bf16[4,128,128]{2,1,0:T(8,128)(2,1)} %get-tuple-element.23), channel_id=1, source_target_pairs={{0,64},{16,80},{32,96},{48,112},{64,0},{80,16},{96,32},{112,48},{1... | collective-permute-start | bytes 393224 | tf_op jit(solution)/shard_map/sum_over_z_lo/ppermute | solution.py:194
  138.9 22.9 %all-gather.2.cloned.1.call-done = bf16[128,4096]{1,0:T(8,128)(2,1)} async-done(((bf16[128,256]{1,0:T(8,128)(2,1)}), bf16[128,4096]{1,0:T(8,128)(2,1)}) %all-gather.2.cloned.1.call-update) | async-done | bytes 1048592 | tf_op jit(solution)/shard_map/gather_projection/all_gather | solution.py:149
  161.8 1.3 fusion.28
  163.1 1.3 fusion.26
  164.4 1.3 fusion.24
  165.7 1.3 multiply_reduce_fusion
  167.0 1.1 fusion.5
  168.0 0.3 fusion.2
  168.4 0.9 fusion.10
  169.3 1.2 fusion.18
  170.5 4.5 %collective-permute-start.11 = (bf16[128,128]{1,0:T(8,128)(2,1)S(1)}, bf16[128,128]{1,0:T(8,128)(2,1)S(1)}, u32[]{:S(2)}, u32[]{:S(2)}) collective-permute-start(bf16[128,128]{1,0:T(8,128)(2,1)S(1)} %get-tuple-element.24), channel_id=1, source_target_pairs={{0,128},{16,144},{32,160},{48,176},{64,192},{80,208},{96,224},{112... | collective-permute-start | bytes 98312 | tf_op jit(solution)/shard_map/sum_over_z_hi/ppermute | solution.py:203
  175.0 11.6 %collective-permute-start.12 = (bf16[128,128]{1,0:T(8,128)(2,1)S(1)}, bf16[128,128]{1,0:T(8,128)(2,1)S(1)}, u32[]{:S(2)}, u32[]{:S(2)}) collective-permute-start(bf16[128,128]{1,0:T(8,128)(2,1)S(1)} %get-tuple-element.26), channel_id=1, source_target_pairs={{0,256},{16,272},{32,288},{48,304},{64,320},{80,336},{96,352},{112... | collective-permute-start | bytes 98312 | tf_op jit(solution)/shard_map/sum_over_z_hi/ppermute | solution.py:203
  186.6 1.9 collective-permute-start.13
  188.6 1.1 fusion.4
  189.6 6.9 %collective-permute-done.13 = bf16[128,128]{1,0:T(8,128)(2,1)S(1)} collective-permute-done((bf16[128,128]{1,0:T(8,128)(2,1)S(1)}, bf16[128,128]{1,0:T(8,128)(2,1)S(1)}, u32[]{:S(2)}, u32[]{:S(2)}) %collective-permute-start.13) | collective-permute-done | bytes 32800 | tf_op jit(solution)/shard_map/sum_over_z_hi/ppermute | solution.py:203
  196.5 0.6 fusion.34
  (39 shorter events, 1.0 us)
Async XLA Ops:
  7.2 64.1 %copy-start = (bf16[1,1024,128]{2,1,0:T(8,128)(2,1)S(1)}, bf16[1,1024,128]{2,1,0:T(8,128)(2,1)}, u32[]{:S(2)}) copy-start(bf16[1,1024,128]{2,1,0:T(8,128)(2,1)} %param.9) | copy-start | bytes 786436
  8.7 40.5 %copy-start.9 = (bf16[128,128]{1,0:T(8,128)(2,1)S(1)}, bf16[128,128]{1,0:T(8,128)(2,1)}, u32[]{:S(2)}) copy-start(bf16[128,128]{1,0:T(8,128)(2,1)} %param.11) | copy-start | bytes 98308
  8.7 16.7 %collective-permute-start = (bf16[256,1024]{1,0:T(8,128)(2,1)S(1)}, bf16[256,1024]{1,0:T(8,128)(2,1)S(1)}, u32[]{:S(2)}, u32[]{:S(2)}) collective-permute-start(bf16[256,1024]{1,0:T(8,128)(2,1)S(1)} %get-tuple-element.18), channel_id=1, source_target_pairs={{0,4},{1,5},{2,6},{3,7},{4,8},{5,9},{6,10},{7,11},{8,12},{9,13},{1... | collective-permute-start | bytes 1572872 | tf_op jit(solution)/shard_map/sum_over_x/ppermute | solution.py:156
  11.8 23.7 %collective-permute-start.1 = (bf16[256,1024]{1,0:T(8,128)(2,1)S(1)}, bf16[256,1024]{1,0:T(8,128)(2,1)S(1)}, u32[]{:S(2)}, u32[]{:S(2)}) collective-permute-start(bf16[256,1024]{1,0:T(8,128)(2,1)S(1)} %get-tuple-element.20), channel_id=1, source_target_pairs={{0,8},{1,9},{2,10},{3,11},{4,12},{5,13},{6,14},{7,15},{8,0},{9,1},... | collective-permute-start | bytes 1572872 | tf_op jit(solution)/shard_map/sum_over_x/ppermute | solution.py:156
  14.6 24.7 %collective-permute-start.2 = (bf16[256,1024]{1,0:T(8,128)(2,1)S(1)}, bf16[256,1024]{1,0:T(8,128)(2,1)S(1)}, u32[]{:S(2)}, u32[]{:S(2)}) collective-permute-start(bf16[256,1024]{1,0:T(8,128)(2,1)S(1)} %get-tuple-element.19), channel_id=1, source_target_pairs={{0,12},{1,13},{2,14},{3,15},{4,0},{5,1},{6,2},{7,3},{8,4},{9,5},{1... | collective-permute-start | bytes 1572872 | tf_op jit(solution)/shard_map/sum_over_x/ppermute | solution.py:156
  41.5 29.4 %copy-start.10 = (s32[1,2,8]{2,1,0:T(2,128)S(1)}, s32[1,2,8]{2,1,0:T(2,128)}, u32[]{:S(2)}) copy-start(s32[1,2,8]{2,1,0:T(2,128)} %param.12) | copy-start | bytes 196
  41.5 29.8 %copy-start.7 = (bf16[1,256,128]{2,1,0:T(8,128)(2,1)S(1)}, bf16[1,256,128]{2,1,0:T(8,128)(2,1)}, u32[]{:S(2)}) copy-start(bf16[1,256,128]{2,1,0:T(8,128)(2,1)} %param.8) | copy-start | bytes 196612
  41.5 22.8 %all-to-all-start = ((bf16[8,32,1024]{2,1,0:T(8,128)(2,1)}), bf16[8,32,1024]{2,1,0:T(8,128)(2,1)S(1)}, u32[]{:S(2)}, u32[]{:S(2)}) async-start(bf16[8,32,1024]{2,1,0:T(8,128)(2,1)} %bitcast.9), calls=%async_computation | async-start | bytes 1048576 | tf_op jit(solution)/shard_map/sum_over_y/all_to_all | solution.py:168
  49.2 21.0 %collective-permute-start.6 = (bf16[128,128]{1,0:T(8,128)(2,1)S(1)}, bf16[128,128]{1,0:T(8,128)(2,1)S(1)}, u32[]{:S(2)}, u32[]{:S(2)}) collective-permute-start(bf16[128,128]{1,0:T(8,128)(2,1)S(1)} %copy-done.9), channel_id=1, source_target_pairs={{0,16},{16,0},{32,48},{48,32},{64,80},{80,64},{96,112},{112,96},{1... | collective-permute-start | bytes 98312 | tf_op jit(solution)/shard_map/gather_projection/ppermute | solution.py:145
  65.4 19.3 %all-to-all-start.1 = ((bf16[8,32,1024]{2,1,0:T(8,128)(2,1)}), bf16[8,32,1024]{2,1,0:T(8,128)(2,1)S(1)}, u32[]{:S(2)}, u32[]{:S(2)}) async-start(bf16[8,32,1024]{2,1,0:T(8,128)(2,1)} %broadcast_in_dim.46), calls=%async_computation.1 | async-start | bytes 1048576 | tf_op jit(solution)/shard_map/gather_over_y/all_to_all | solution.py:177
  70.2 91.6 %all-gather.2.cloned.1.call-start = ((), (), s32[]{:S(2)}) async-start(), calls=%async_computation.2 | async-start | bytes 1114112 | tf_op jit(solution)/shard_map/gather_projection/all_gather | solution.py:149
  84.7 28.0 %collective-permute-start.3 = (bf16[256,1024]{1,0:T(8,128)(2,1)S(1)}, bf16[256,1024]{1,0:T(8,128)(2,1)S(1)}, u32[]{:S(2)}, u32[]{:S(2)}) collective-permute-start(bf16[256,1024]{1,0:T(8,128)(2,1)S(1)} %bitcast.71), channel_id=1, source_target_pairs={{0,12},{1,13},{2,14},{3,15},{4,0},{5,1},{6,2},{7,3},{8,4},{9,5},{1... | collective-permute-start | bytes 1572872 | tf_op jit(solution)/shard_map/gather_over_x/ppermute | solution.py:181
  91.1 21.6 %collective-permute-start.4 = (bf16[256,1024]{1,0:T(8,128)(2,1)S(1)}, bf16[256,1024]{1,0:T(8,128)(2,1)S(1)}, u32[]{:S(2)}, u32[]{:S(2)}) collective-permute-start(bf16[256,1024]{1,0:T(8,128)(2,1)S(1)} %bitcast.72), channel_id=1, source_target_pairs={{0,8},{1,9},{2,10},{3,11},{4,12},{5,13},{6,14},{7,15},{8,0},{9,1},... | collective-permute-start | bytes 1572872 | tf_op jit(solution)/shard_map/gather_over_x/ppermute | solution.py:181
  94.7 23.6 %collective-permute-start.5 = (bf16[256,1024]{1,0:T(8,128)(2,1)S(1)}, bf16[256,1024]{1,0:T(8,128)(2,1)S(1)}, u32[]{:S(2)}, u32[]{:S(2)}) collective-permute-start(bf16[256,1024]{1,0:T(8,128)(2,1)S(1)} %bitcast.73), channel_id=1, source_target_pairs={{0,4},{1,5},{2,6},{3,7},{4,8},{5,9},{6,10},{7,11},{8,12},{9,13},{1... | collective-permute-start | bytes 1572872 | tf_op jit(solution)/shard_map/gather_over_x/ppermute | solution.py:181
  97.3 0.9 copy-start.1
  99.5 18.8 %copy-start.4 = (f32[256,128]{0,1:T(8,128)}, f32[256,128]{0,1:T(8,128)S(1)}, u32[]{:S(2)}) copy-start(f32[256,128]{0,1:T(8,128)S(1)} %fusion.20) | copy-start | bytes 393220
  119.6 4.1 %collective-permute-start.7 = (bf16[4,4,128,128]{3,2,1,0:T(8,128)(2,1)}, bf16[4,4,128,128]{3,2,1,0:T(8,128)(2,1)}, u32[]{:S(2)}, u32[]{:S(2)}) collective-permute-start(bf16[4,4,128,128]{3,2,1,0:T(8,128)(2,1)} %get-tuple-element.12), channel_id=1, source_target_pairs={{0,16},{16,0},{32,48},{48,32},{64,80},{80,64},{96,112},{112,96},{1... | collective-permute-start | bytes 1572872 | tf_op jit(solution)/shard_map/sum_over_core/ppermute | solution.py:187
  124.9 0.8 copy-start.3
  125.7 40.0 %copy-start.5 = (f32[256,128]{0,1:T(8,128)S(1)}, f32[256,128]{0,1:T(8,128)}, u32[]{:S(2)}) copy-start(f32[256,128]{0,1:T(8,128)} %copy-done.4) | copy-start | bytes 393220
  126.5 40.5 %copy-start.2 = (f32[256,1024]{1,0:T(8,128)S(1)}, f32[256,1024]{1,0:T(8,128)}, u32[]{:S(2)}) copy-start(f32[256,1024]{1,0:T(8,128)} %copy-done.1) | copy-start | bytes 3145732
  126.5 42.8 %collective-permute-start.10 = (bf16[4,128,128]{2,1,0:T(8,128)(2,1)}, bf16[4,128,128]{2,1,0:T(8,128)(2,1)}, u32[]{:S(2)}, u32[]{:S(2)}) collective-permute-start(bf16[4,128,128]{2,1,0:T(8,128)(2,1)} %get-tuple-element.22), channel_id=1, source_target_pairs={{0,96},{16,112},{32,0},{48,16},{64,32},{80,48},{96,64},{112,80},{1... | collective-permute-start | bytes 393224 | tf_op jit(solution)/shard_map/sum_over_z_lo/ppermute | solution.py:194
  134.5 34.8 %collective-permute-start.8 = (bf16[4,128,128]{2,1,0:T(8,128)(2,1)}, bf16[4,128,128]{2,1,0:T(8,128)(2,1)}, u32[]{:S(2)}, u32[]{:S(2)}) collective-permute-start(bf16[4,128,128]{2,1,0:T(8,128)(2,1)} %get-tuple-element.21), channel_id=1, source_target_pairs={{0,32},{16,48},{32,64},{48,80},{64,96},{80,112},{96,0},{112,16},{1... | collective-permute-start | bytes 393224 | tf_op jit(solution)/shard_map/sum_over_z_lo/ppermute | solution.py:194
  136.4 32.9 %collective-permute-start.9 = (bf16[4,128,128]{2,1,0:T(8,128)(2,1)}, bf16[4,128,128]{2,1,0:T(8,128)(2,1)}, u32[]{:S(2)}, u32[]{:S(2)}) collective-permute-start(bf16[4,128,128]{2,1,0:T(8,128)(2,1)} %get-tuple-element.23), channel_id=1, source_target_pairs={{0,64},{16,80},{32,96},{48,112},{64,0},{80,16},{96,32},{112,48},{1... | collective-permute-start | bytes 393224 | tf_op jit(solution)/shard_map/sum_over_z_lo/ppermute | solution.py:194
  163.1 5.0 %copy-start.6 = (bf16[1,1024,128]{2,1,0:T(8,128)(2,1)S(1)}, bf16[1,1024,128]{2,1,0:T(8,128)(2,1)}, u32[]{:S(2)}) copy-start(bf16[1,1024,128]{2,1,0:T(8,128)(2,1)} %param.10) | copy-start | bytes 786436
  168.0 20.5 %copy-start.8 = (bf16[1,256,128]{2,1,0:T(8,128)(2,1)S(1)}, bf16[1,256,128]{2,1,0:T(8,128)(2,1)}, u32[]{:S(2)}) copy-start(bf16[1,256,128]{2,1,0:T(8,128)(2,1)} %param.8) | copy-start | bytes 196612
  170.5 19.1 %collective-permute-start.11 = (bf16[128,128]{1,0:T(8,128)(2,1)S(1)}, bf16[128,128]{1,0:T(8,128)(2,1)S(1)}, u32[]{:S(2)}, u32[]{:S(2)}) collective-permute-start(bf16[128,128]{1,0:T(8,128)(2,1)S(1)} %get-tuple-element.24), channel_id=1, source_target_pairs={{0,128},{16,144},{32,160},{48,176},{64,192},{80,208},{96,224},{112... | collective-permute-start | bytes 98312 | tf_op jit(solution)/shard_map/sum_over_z_hi/ppermute | solution.py:203
  175.0 14.6 %collective-permute-start.12 = (bf16[128,128]{1,0:T(8,128)(2,1)S(1)}, bf16[128,128]{1,0:T(8,128)(2,1)S(1)}, u32[]{:S(2)}, u32[]{:S(2)}) collective-permute-start(bf16[128,128]{1,0:T(8,128)(2,1)S(1)} %get-tuple-element.26), channel_id=1, source_target_pairs={{0,256},{16,272},{32,288},{48,304},{64,320},{80,336},{96,352},{112... | collective-permute-start | bytes 98312 | tf_op jit(solution)/shard_map/sum_over_z_hi/ppermute | solution.py:203
  186.6 9.9 %collective-permute-start.13 = (bf16[128,128]{1,0:T(8,128)(2,1)S(1)}, bf16[128,128]{1,0:T(8,128)(2,1)S(1)}, u32[]{:S(2)}, u32[]{:S(2)}) collective-permute-start(bf16[128,128]{1,0:T(8,128)(2,1)S(1)} %get-tuple-element.25), channel_id=1, source_target_pairs={{0,384},{16,400},{32,416},{48,432},{64,448},{80,464},{96,480},{112... | collective-permute-start | bytes 98312 | tf_op jit(solution)/shard_map/sum_over_z_hi/ppermute | solution.py:203
Sparse Core Ops, SparseCore 0:
  74.2 87.5 all-gather.1

commit v2 on v1

--- a/solution.py
+++ b/solution.py
@@ -43,16 +43,24 @@
     ]
 
 
+def swap_x_zh():
+    pairs = []
+    for a in range(ZH):
+        for rest in range(ZL * CORES):
+            for x in range(X):
+                for yh in range(YH):
+                    here = ((a * ZL * CORES + rest) * X + x) * YH + yh
+                    there = ((x * ZL * CORES + rest) * X + a) * YH + yh
+                    pairs.append((here, there))
+    return pairs
+
+
 def other_core():
     return [(s, s ^ 1) for s in range(ZH * ZL * CORES)]
 
 
 def y_groups():
     return [[xy_index(x, y) for y in range(YH * YL)] for x in range(X)]
-
-
-def z_groups():
-    return [[z * CORES + c for z in range(ZH * ZL)] for c in range(CORES)]
 
 
 def attend_forward(queries, keys, values, visible, scaling):
@@ -80,13 +88,13 @@
     return [g.astype(jnp.bfloat16) for g in (d_queries, d_keys, d_values)]
 
 
-def weight_terms_kernel(core_ref, attended_ref, *refs):
-    blocks, (send_ref, keep_ref) = refs[:X], refs[X:]
+def weight_terms_kernel(core_ref, block_ref, *refs):
+    attended, (send_ref, keep_ref) = refs[:X], refs[X:]
     first = core_ref[0] == 0
     for k in range(X):
         term = lax.dot_general(
-            attended_ref[...],
-            blocks[k][...],
+            attended[k][...],
+            block_ref[...],
             (((0,), (0,)), ((), ())),
             preferred_element_type=jnp.float32,
         )
@@ -98,8 +106,8 @@
             keep_ref[b, k] = jnp.where(first, low, high)
 
 
-def weight_terms(core, attended, blocks):
-    rows, width = blocks[0].shape
+def weight_terms(core, block, attended):
+    rows, width = block.shape
     shape = (ZL, X, HEAD_DIM, HEAD_DIM)
     vmem = pl.BlockSpec(memory_space=pltpu.VMEM)
     return pl.pallas_call(
@@ -113,11 +121,47 @@
         compiler_params=pltpu.CompilerParams(vmem_limit_bytes=24 << 20),
         cost_estimate=pl.CostEstimate(
             flops=2 * rows * width * X * HEAD_DIM,
-            bytes_accessed=2 * rows * width * X + 6 * width * X * HEAD_DIM // 2,
+            bytes_accessed=2 * rows * (width + X * HEAD_DIM) + 3 * width * X * HEAD_DIM,
             transcendentals=0,
         ),
         name="weight_terms",
-    )(core.reshape(1), attended, *blocks)
+    )(core.reshape(1), block, *attended)
+
+
+def head_grad_kernel(place_ref, *refs):
+    blocks, weights, out_ref = refs[:X], refs[X : X + ZL], refs[X + ZL]
+    x, zh, zl = place_ref[0], place_ref[1], place_ref[2]
+    wide = CORES * HEAD_DIM
+    total = jnp.zeros(out_ref.shape, jnp.float32)
+    for k in range(X):
+        far = (x + k - zh) & (ZH - 1)
+        for i in range(ZL):
+            left = pl.multiple_of(((zl + i) & (ZL - 1)) * wide, wide)
+            total += lax.dot_general(
+                blocks[k][:, pl.ds(left, wide)],
+                weights[i][far],
+                (((1,), (1,)), ((), ())),
+                preferred_element_type=jnp.float32,
+            )
+    out_ref[...] = total.astype(out_ref.dtype)
+
+
+def head_grad(place, blocks, weights):
+    rows, width = blocks[0].shape
+    vmem = pl.BlockSpec(memory_space=pltpu.VMEM)
+    return pl.pallas_call(
+        head_grad_kernel,
+        out_shape=jax.ShapeDtypeStruct((rows, HEAD_DIM), jnp.bfloat16),
+        in_specs=[pl.BlockSpec(memory_space=pltpu.SMEM)] + [vmem] * (X + ZL),
+        out_specs=vmem,
+        compiler_params=pltpu.CompilerParams(vmem_limit_bytes=24 << 20),
+        cost_estimate=pl.CostEstimate(
+            flops=2 * rows * width * X * HEAD_DIM,
+            bytes_accessed=2 * (rows + HEAD_DIM) * width * X,
+            transcendentals=0,
+        ),
+        name="head_grad",
+    )(place, *blocks, *weights)
 
 
 def shift_right(number, size):
@@ -141,20 +185,22 @@
     tokens, model = sample.shape
     width = model // X
 
+    with jax.named_scope("sum_over_x"):
+        pieces = [
+            lax.dynamic_slice(sample, (0, ((x + k) & (X - 1)) * width), (tokens, width))
+            for k in range(X)
+        ]
+        arrived = [lax.ppermute(pieces[k], "mp", shift_x(k)) for k in range(1, X)]
+        partial = sum_f32([pieces[0]] + arrived).astype(jnp.bfloat16)
+
     with jax.named_scope("gather_projection"):
         w_other = lax.ppermute(w_out, "scene", other_core())
         w_chip = jnp.concatenate(
             [jnp.where(core == 0, w_out, w_other), jnp.where(core == 0, w_other, w_out)], axis=1
         )
-        w_full = lax.all_gather(w_chip, "scene", axis=1, tiled=True, axis_index_groups=z_groups())
-
-    with jax.named_scope("sum_over_x"):
-        pieces = [
-            lax.dynamic_slice(sample, (0, ((x + k) & (X - 1)) * width), (tokens, width))
-            for k in range(X)
-        ]
-        arrived = [lax.ppermute(pieces[k], "mp", shift_x(k)) for k in range(1, X)]
-        partial = sum_f32([pieces[0]] + arrived).astype(jnp.bfloat16)
+        w_far = jnp.stack(
+            [w_chip] + [lax.ppermute(w_chip, "scene", shift_zh(-k)) for k in range(1, ZH)]
+        )
 
     queries, keys, values = agent_queries[0], map_keys[0], map_values[0]
     mask_rows = block_mask[0]
@@ -163,6 +209,7 @@
     probs, weights, attended = attend_forward(queries, keys, values, visible, scaling)
     attended_rounded = attended.astype(jnp.bfloat16)
 
+    partial, w_far, attended_rounded = lax.optimization_barrier((partial, w_far, attended_rounded))
     with jax.named_scope("sum_over_y"):
         rows = tokens // (YH * YL)
         lines = lax.all_to_all(
@@ -171,49 +218,51 @@
         summed = jnp.sum(lines.astype(jnp.float32), axis=0)
         row_keep = y * rows + jnp.arange(rows) < agent_count[0]
         own = jnp.where(row_keep[:, None], summed, 0.0).astype(jnp.bfloat16)
-
+    with jax.named_scope("gather_attended"):
+        attended_near = [attended_rounded] + [
+            lax.ppermute(attended_rounded, "mp", shift_x(-k)) for k in range(1, X)
+        ]
+
+    own, attended_near, w_far = lax.optimization_barrier((own, attended_near, w_far))
     with jax.named_scope("gather_over_y"):
         spread = jnp.broadcast_to(own[None], (YH * YL, rows, width))
         block = lax.all_to_all(spread, XY, 0, 0, axis_index_groups=y_groups())
         block = block.reshape(tokens, width)
+    with jax.named_scope("gather_projection"):
+        w_near = [w_far] + [lax.ppermute(w_far, "scene", shift_zl(-k)) for k in range(1, ZL)]
+
+    block, w_near = lax.optimization_barrier((block, w_near))
+    with jax.named_scope("weight_terms"):
+        send, keep = weight_terms(core, block, attended_near)
+
+    with jax.named_scope("sum_over_core"):
+        pair = sum_f32([keep, lax.ppermute(send, "scene", other_core())]).astype(jnp.bfloat16)
 
     with jax.named_scope("gather_over_x"):
         upstream = [block] + [lax.ppermute(block, "mp", shift_x(-k)) for k in range(1, X)]
 
-    with jax.named_scope("weight_terms"):
-        send, keep = weight_terms(core, attended_rounded, upstream)
-
-    with jax.named_scope("sum_over_core"):
-        pair = sum_f32([keep, lax.ppermute(send, "scene", other_core())]).astype(jnp.bfloat16)
-
     with jax.named_scope("sum_over_z_lo"):
         parts = [
-            lax.dynamic_index_in_dim(pair, (zl + k) & (ZL - 1), 0, keepdims=False) for k in range(ZL)
+            lax.dynamic_index_in_dim(pair, (zl + k) & (ZL - 1), 0, keepdims=False)
+            for k in range(ZL)
         ]
         near = sum_f32(
             parts[:1] + [lax.ppermute(parts[k], "scene", shift_zl(k)) for k in range(1, ZL)]
         ).astype(jnp.bfloat16)
 
+    near, upstream, w_near = lax.optimization_barrier((near, upstream, w_near))
     with jax.named_scope("sum_over_z_hi"):
         parts = [
             lax.dynamic_index_in_dim(near, (zh + k - x) & (X - 1), 0, keepdims=False)
             for k in range(ZH)
         ]
-        d_wout = sum_f32(
+        summed_block = sum_f32(
             parts[:1] + [lax.ppermute(parts[k], "scene", shift_zh(k)) for k in range(1, ZH)]
         )
+        d_wout = lax.ppermute(summed_block, ("scene", "mp"), swap_x_zh())
 
     with jax.named_scope("head_gradients"):
-        upstream, w_full, _ = lax.optimization_barrier((upstream, w_full, pair))
-        d_attn = sum(
-            jnp.einsum(
-                "td,hd->th",
-                upstream[k],
-                lax.dynamic_slice(w_full, (0, ((x + k) & (X - 1)) * width), (HEAD_DIM, width)),
-                preferred_element_type=jnp.float32,
-            )
-            for k in range(X)
-        ).astype(jnp.bfloat16)
+        d_attn = head_grad(jnp.stack([x, zh, zl]), upstream, w_near)
         d_queries, d_keys, d_values = attend_backward(
             queries, keys, values, d_attn, probs, weights, attended, scaling
         )

time: 205 us -> 193 us (0.941)
  the two profiles are of different devices: /device:TPU:12 before, /device:TPU:76 now
where the time goes in v2:
time: 193 us; the launch traced here: 192 us
  starting transfers between devices  128 us (66%)
  waiting for transfers between devices  40.8 us (21%)
  local copies, waits for them, and re-layouts  8.31 us (4%)
  other arithmetic  6.03 us (3%)
  matrix products  4.08 us (2%)
  Pallas kernels  3.04 us (2%)
    ppermute x3, starting transfers between devices, shards(): lax.ppermute(w_chip, 'scene', shift_zh(-k))  26.3 us
    ppermute x3, starting transfers between devices, shards(): lax.ppermute(parts[k], 'scene', shift_zh(k))  19.4 us
    ppermute x3, starting transfers between devices, shards(): lax.ppermute(w_far, 'scene', shift_zl(-k))  14.8 us
    ppermute x3, starting transfers between devices, shards(): lax.ppermute(parts[k], 'scene', shift_zl(k))  14.3 us
    ppermute x3, waiting for transfers between devices, shards(): lax.ppermute(w_far, 'scene', shift_zl(-k))  12.9 us
    ppermute x1, waiting for transfers between devices, shards(): d_wout = lax.ppermute(summed_block, ('scene', 'mp'), swap_x_zh())  11.4 us
    ppermute x3, starting transfers between devices, shards(): lax.ppermute(block, 'mp', shift_x(-k))  11.4 us
    ppermute x3, starting transfers between devices, shards(): lax.ppermute(attended_rounded, 'mp', shift_x(-k))  10.7 us
  transfers between devices with their start and end apart: 26, of which 7 were waited for; matrix products, arithmetic and copies ran while one was open for 4% of the time, Pallas kernels for 1%

profile of v2, /device:TPU:76, one launch (start us, length us, event | category | flops | bytes accessed | tf_op | source)
XLA Modules:
  0.0 192.3 jit_solution(13575194947457066865)
XLA Ops:
  0.7 1.6 dynamic-slice_bitcast_fusion.2
  2.3 3.1 %collective-permute-start = (bf16[256,1024]{1,0:T(8,128)(2,1)S(1)}, bf16[256,1024]{1,0:T(8,128)(2,1)}, u32[]{:S(2)}, u32[]{:S(2)}) collective-permute-start(bf16[256,1024]{1,0:T(8,128)(2,1)S(1)} %get-tuple-element.54), channel_id=1, source_target_pairs={{0,4},{1,5},{2,6},{3,7},{4,8},{5,9},{6,10},{7,11},{8,12},{9,13},{1... | collective-permute-start | bytes 1572872 | tf_op jit(solution)/shard_map/sum_over_x/ppermute | solution.py:193
  5.4 2.7 %collective-permute-start.1 = (bf16[256,1024]{1,0:T(8,128)(2,1)S(1)}, bf16[256,1024]{1,0:T(8,128)(2,1)}, u32[]{:S(2)}, u32[]{:S(2)}) collective-permute-start(bf16[256,1024]{1,0:T(8,128)(2,1)S(1)} %get-tuple-element.56), channel_id=1, source_target_pairs={{0,8},{1,9},{2,10},{3,11},{4,12},{5,13},{6,14},{7,15},{8,0},{9,1},... | collective-permute-start | bytes 1572872 | tf_op jit(solution)/shard_map/sum_over_x/ppermute | solution.py:193
  8.1 3.0 %collective-permute-start.2 = (bf16[256,1024]{1,0:T(8,128)(2,1)S(1)}, bf16[256,1024]{1,0:T(8,128)(2,1)}, u32[]{:S(2)}, u32[]{:S(2)}) collective-permute-start(bf16[256,1024]{1,0:T(8,128)(2,1)S(1)} %get-tuple-element.55), channel_id=1, source_target_pairs={{0,12},{1,13},{2,14},{3,15},{4,0},{5,1},{6,2},{7,3},{8,4},{9,5},{1... | collective-permute-start | bytes 1572872 | tf_op jit(solution)/shard_map/sum_over_x/ppermute | solution.py:193
  11.2 1.9 collective-permute-start.3
  14.3 17.3 %collective-permute-start.4 = (bf16[128,256]{1,0:T(8,128)(2,1)S(1)}, bf16[128,256]{1,0:T(8,128)(2,1)S(1)}, u32[]{:S(2)}, u32[]{:S(2)}) collective-permute-start(bf16[128,256]{1,0:T(8,128)(2,1)S(1)} %get-tuple-element.64), channel_id=1, source_target_pairs={{0,384},{16,400},{32,416},{48,432},{64,448},{80,464},{96,480},{112... | collective-permute-start | bytes 196616 | tf_op jit(solution)/shard_map/gather_projection/ppermute | solution.py:202
  31.9 3.1 %collective-permute-start.5 = (bf16[128,256]{1,0:T(8,128)(2,1)S(1)}, bf16[128,256]{1,0:T(8,128)(2,1)S(1)}, u32[]{:S(2)}, u32[]{:S(2)}) collective-permute-start(bf16[128,256]{1,0:T(8,128)(2,1)S(1)} %get-tuple-element.64), channel_id=1, source_target_pairs={{0,256},{16,272},{32,288},{48,304},{64,320},{80,336},{96,352},{112... | collective-permute-start | bytes 196616 | tf_op jit(solution)/shard_map/gather_projection/ppermute | solution.py:202
  35.0 1.9 collective-permute-done.4
  36.9 6.0 %collective-permute-start.6 = (bf16[128,256]{1,0:T(8,128)(2,1)S(1)}, bf16[128,256]{1,0:T(8,128)(2,1)S(1)}, u32[]{:S(2)}, u32[]{:S(2)}) collective-permute-start(bf16[128,256]{1,0:T(8,128)(2,1)S(1)} %get-tuple-element.64), channel_id=1, source_target_pairs={{0,128},{16,144},{32,160},{48,176},{64,192},{80,208},{96,224},{112... | collective-permute-start | bytes 196616 | tf_op jit(solution)/shard_map/gather_projection/ppermute | solution.py:202
  43.2 5.2 %collective-permute-done.5 = bf16[128,256]{1,0:T(8,128)(2,1)S(1)} collective-permute-done((bf16[128,256]{1,0:T(8,128)(2,1)S(1)}, bf16[128,256]{1,0:T(8,128)(2,1)S(1)}, u32[]{:S(2)}, u32[]{:S(2)}) %collective-permute-start.5) | collective-permute-done | bytes 65568 | tf_op jit(solution)/shard_map/gather_projection/ppermute | solution.py:202
  48.4 2.7 %fusion.10 = bf16[256,1024]{1,0:T(8,128)(2,1)} fusion(bf16[256,1024]{1,0:T(8,128)(2,1)} %collective-permute-done.2, bf16[256,1024]{1,0:T(8,128)(2,1)} %collective-permute-done.1, bf16[256,1024]{1,0:T(8,128)(2,1)} %collective-permute-done, bf16[1,1,256,4096]{3,2,1,0:T(8,128)(2,1)} %param.7, s32[]{:T(128)S(6)} %select_n.59), kind=kLoop, calls=%fused_computation.16 | loop fusion | flops 2097152 | bytes 2621444 | tf_op jit(solution)/shard_map/sum_over_x/convert_element_type | solution.py:194
  51.1 8.2 %all-to-all-start = ((bf16[8,32,1024]{2,1,0:T(8,128)(2,1)}), bf16[8,32,1024]{2,1,0:T(8,128)(2,1)S(1)}, u32[]{:S(2)}, u32[]{:S(2)}) async-start(bf16[8,32,1024]{2,1,0:T(8,128)(2,1)} %bitcast.18), calls=%async_computation | async-start | bytes 1048576 | tf_op jit(solution)/shard_map/sum_over_y/all_to_all | solution.py:215
  60.0 3.4 %collective-permute-start.7 = (bf16[256,128]{1,0:T(8,128)(2,1)S(1)}, bf16[256,128]{1,0:T(8,128)(2,1)S(1)}, u32[]{:S(2)}, u32[]{:S(2)}) collective-permute-start(bf16[256,128]{1,0:T(8,128)(2,1)S(1)} %get-tuple-element.35.refs_0_), channel_id=1, source_target_pairs={{0,12},{1,13},{2,14},{3,15},{4,0},{5,1},{6,2},{7,3},{8,4},{9,5},{1... | collective-permute-start | bytes 196616 | tf_op jit(solution)/shard_map/gather_attended/ppermute | solution.py:223
  63.4 2.8 %collective-permute-start.8 = (bf16[256,128]{1,0:T(8,128)(2,1)S(1)}, bf16[256,128]{1,0:T(8,128)(2,1)S(1)}, u32[]{:S(2)}, u32[]{:S(2)}) collective-permute-start(bf16[256,128]{1,0:T(8,128)(2,1)S(1)} %get-tuple-element.35.refs_0_), channel_id=1, source_target_pairs={{0,8},{1,9},{2,10},{3,11},{4,12},{5,13},{6,14},{7,15},{8,0},{9,1},... | collective-permute-start | bytes 196616 | tf_op jit(solution)/shard_map/gather_attended/ppermute | solution.py:223
  66.2 4.5 %collective-permute-start.9 = (bf16[256,128]{1,0:T(8,128)(2,1)S(1)}, bf16[256,128]{1,0:T(8,128)(2,1)S(1)}, u32[]{:S(2)}, u32[]{:S(2)}) collective-permute-start(bf16[256,128]{1,0:T(8,128)(2,1)S(1)} %get-tuple-element.35.refs_0_), channel_id=1, source_target_pairs={{0,4},{1,5},{2,6},{3,7},{4,8},{5,9},{6,10},{7,11},{8,12},{9,13},{1... | collective-permute-start | bytes 196616 | tf_op jit(solution)/shard_map/gather_attended/ppermute | solution.py:223
  70.7 5.1 %all-to-all-done = bf16[8,32,1024]{2,1,0:T(8,128)(2,1)S(1)} async-done(((bf16[8,32,1024]{2,1,0:T(8,128)(2,1)}), bf16[8,32,1024]{2,1,0:T(8,128)(2,1)S(1)}, u32[]{:S(2)}, u32[]{:S(2)}) %all-to-all-start) | async-done | bytes 524320 | tf_op jit(solution)/shard_map/sum_over_y/all_to_all | solution.py:215
  76.0 0.9 broadcast_in_dim.46
  76.9 4.8 %all-to-all-start.1 = ((bf16[8,32,1024]{2,1,0:T(8,128)(2,1)}), bf16[8,32,1024]{2,1,0:T(8,128)(2,1)S(1)}, u32[]{:S(2)}, u32[]{:S(2)}) async-start(bf16[8,32,1024]{2,1,0:T(8,128)(2,1)} %broadcast_in_dim.46), calls=%async_computation.1 | async-start | bytes 1048576 | tf_op jit(solution)/shard_map/gather_over_y/all_to_all | solution.py:229
  81.7 9.5 %collective-permute-start.10 = (bf16[4,128,256]{2,1,0:T(8,128)(2,1)S(1)}, bf16[4,128,256]{2,1,0:T(8,128)(2,1)S(1)}, u32[]{:S(2)}, u32[]{:S(2)}) collective-permute-start(bf16[4,128,256]{2,1,0:T(8,128)(2,1)S(1)} %pad_maximum_fusion.refs_4_), channel_id=1, source_target_pairs={{0,96},{16,112},{32,0},{48,16},{64,32},{80,48},{96,64},{112,80},{1... | collective-permute-start | bytes 786440 | tf_op jit(solution)/shard_map/gather_projection/ppermute | solution.py:232
  91.2 1.9 collective-permute-start.11
  93.1 3.4 %collective-permute-start.12 = (bf16[4,128,256]{2,1,0:T(8,128)(2,1)S(1)}, bf16[4,128,256]{2,1,0:T(8,128)(2,1)S(1)}, u32[]{:S(2)}, u32[]{:S(2)}) collective-permute-start(bf16[4,128,256]{2,1,0:T(8,128)(2,1)S(1)} %pad_maximum_fusion.refs_4_), channel_id=1, source_target_pairs={{0,32},{16,48},{32,64},{48,80},{64,96},{80,112},{96,0},{112,16},{1... | collective-permute-start | bytes 786440 | tf_op jit(solution)/shard_map/gather_projection/ppermute | solution.py:232
  96.5 8.1 %collective-permute-done.11.refs_6_ = bf16[4,128,256]{2,1,0:T(8,128)(2,1)S(1)} collective-permute-done((bf16[4,128,256]{2,1,0:T(8,128)(2,1)S(1)}, bf16[4,128,256]{2,1,0:T(8,128)(2,1)S(1)}, u32[]{:S(2)}, u32[]{:S(2)}) %collective-permute-start.11) | collective-permute-done | bytes 262176 | tf_op jit(solution)/shard_map/gather_projection/ppermute | solution.py:232
  104.6 0.7 copy-done.1
  105.3 4.8 %collective-permute-done.12.refs_7_ = bf16[4,128,256]{2,1,0:T(8,128)(2,1)S(1)} collective-permute-done((bf16[4,128,256]{2,1,0:T(8,128)(2,1)S(1)}, bf16[4,128,256]{2,1,0:T(8,128)(2,1)S(1)}, u32[]{:S(2)}, u32[]{:S(2)}) %collective-permute-start.12) | collective-permute-done | bytes 262176 | tf_op jit(solution)/shard_map/gather_projection/ppermute | solution.py:232
  110.9 1.3 weight_terms.1
  112.1 1.9 collective-permute-start.13
  114.1 4.0 %collective-permute-start.17 = (bf16[256,1024]{1,0:T(8,128)(2,1)S(1)}, bf16[256,1024]{1,0:T(8,128)(2,1)S(1)}, u32[]{:S(2)}, u32[]{:S(2)}) collective-permute-start(bf16[256,1024]{1,0:T(8,128)(2,1)S(1)} %bitcast.78), channel_id=1, source_target_pairs={{0,12},{1,13},{2,14},{3,15},{4,0},{5,1},{6,2},{7,3},{8,4},{9,5},{1... | collective-permute-start | bytes 1572872 | tf_op jit(solution)/shard_map/gather_over_x/ppermute | solution.py:242
  118.0 2.9 %collective-permute-start.18 = (bf16[256,1024]{1,0:T(8,128)(2,1)S(1)}, bf16[256,1024]{1,0:T(8,128)(2,1)S(1)}, u32[]{:S(2)}, u32[]{:S(2)}) collective-permute-start(bf16[256,1024]{1,0:T(8,128)(2,1)S(1)} %bitcast.79), channel_id=1, source_target_pairs={{0,8},{1,9},{2,10},{3,11},{4,12},{5,13},{6,14},{7,15},{8,0},{9,1},... | collective-permute-start | bytes 1572872 | tf_op jit(solution)/shard_map/gather_over_x/ppermute | solution.py:242
  120.9 4.5 %collective-permute-start.19 = (bf16[256,1024]{1,0:T(8,128)(2,1)S(1)}, bf16[256,1024]{1,0:T(8,128)(2,1)}, u32[]{:S(2)}, u32[]{:S(2)}) collective-permute-start(bf16[256,1024]{1,0:T(8,128)(2,1)S(1)} %bitcast.80), channel_id=1, source_target_pairs={{0,4},{1,5},{2,6},{3,7},{4,8},{5,9},{6,10},{7,11},{8,12},{9,13},{1... | collective-permute-start | bytes 1572872 | tf_op jit(solution)/shard_map/gather_over_x/ppermute | solution.py:242
  125.5 1.2 add_convert_fusion
  126.7 0.8 copy-done.7
  127.5 0.7 dynamic-slice_bitcast_fusion.5
  128.2 4.4 %collective-permute-start.14 = (bf16[4,128,128]{2,1,0:T(8,128)(2,1)S(1)}, bf16[4,128,128]{2,1,0:T(8,128)(2,1)}, u32[]{:S(2)}, u32[]{:S(2)}) collective-permute-start(bf16[4,128,128]{2,1,0:T(8,128)(2,1)S(1)} %get-tuple-element.57), channel_id=1, source_target_pairs={{0,32},{16,48},{32,64},{48,80},{64,96},{80,112},{96,0},{112,16},{1... | collective-permute-start | bytes 393224 | tf_op jit(solution)/shard_map/sum_over_z_lo/ppermute | solution.py:250
  132.6 4.6 %collective-permute-start.15 = (bf16[4,128,128]{2,1,0:T(8,128)(2,1)}, bf16[4,128,128]{2,1,0:T(8,128)(2,1)}, u32[]{:S(2)}, u32[]{:S(2)}) collective-permute-start(bf16[4,128,128]{2,1,0:T(8,128)(2,1)} %get-tuple-element.59), channel_id=1, source_target_pairs={{0,64},{16,80},{32,96},{48,112},{64,0},{80,16},{96,32},{112,48},{1... | collective-permute-start | bytes 393224 | tf_op jit(solution)/shard_map/sum_over_z_lo/ppermute | solution.py:250
  137.2 5.3 %collective-permute-start.16 = (bf16[4,128,128]{2,1,0:T(8,128)(2,1)}, bf16[4,128,128]{2,1,0:T(8,128)(2,1)}, u32[]{:S(2)}, u32[]{:S(2)}) collective-permute-start(bf16[4,128,128]{2,1,0:T(8,128)(2,1)} %get-tuple-element.58), channel_id=1, source_target_pairs={{0,96},{16,112},{32,0},{48,16},{64,32},{80,48},{96,64},{112,80},{1... | collective-permute-start | bytes 393224 | tf_op jit(solution)/shard_map/sum_over_z_lo/ppermute | solution.py:250
  142.7 4.2 %collective-permute-done.16 = bf16[4,128,128]{2,1,0:T(8,128)(2,1)} collective-permute-done((bf16[4,128,128]{2,1,0:T(8,128)(2,1)}, bf16[4,128,128]{2,1,0:T(8,128)(2,1)}, u32[]{:S(2)}, u32[]{:S(2)}) %collective-permute-start.16) | collective-permute-done | bytes 131104 | tf_op jit(solution)/shard_map/sum_over_z_lo/ppermute | solution.py:250
  146.9 1.2 fusion.15
  148.1 5.9 %collective-permute-start.20 = (bf16[128,128]{1,0:T(8,128)(2,1)S(1)}, bf16[128,128]{1,0:T(8,128)(2,1)S(1)}, u32[]{:S(2)}, u32[]{:S(2)}) collective-permute-start(bf16[128,128]{1,0:T(8,128)(2,1)S(1)} %get-tuple-element.60), channel_id=1, source_target_pairs={{0,128},{16,144},{32,160},{48,176},{64,192},{80,208},{96,224},{112... | collective-permute-start | bytes 98312 | tf_op jit(solution)/shard_map/sum_over_z_hi/ppermute | solution.py:260
  154.0 8.8 %collective-permute-start.21 = (bf16[128,128]{1,0:T(8,128)(2,1)S(1)}, bf16[128,128]{1,0:T(8,128)(2,1)S(1)}, u32[]{:S(2)}, u32[]{:S(2)}) collective-permute-start(bf16[128,128]{1,0:T(8,128)(2,1)S(1)} %get-tuple-element.62), channel_id=1, source_target_pairs={{0,256},{16,272},{32,288},{48,304},{64,320},{80,336},{96,352},{112... | collective-permute-start | bytes 98312 | tf_op jit(solution)/shard_map/sum_over_z_hi/ppermute | solution.py:260
  162.8 4.7 %collective-permute-start.22 = (bf16[128,128]{1,0:T(8,128)(2,1)S(1)}, bf16[128,128]{1,0:T(8,128)(2,1)S(1)}, u32[]{:S(2)}, u32[]{:S(2)}) collective-permute-start(bf16[128,128]{1,0:T(8,128)(2,1)S(1)} %get-tuple-element.61), channel_id=1, source_target_pairs={{0,384},{16,400},{32,416},{48,432},{64,448},{80,464},{96,480},{112... | collective-permute-start | bytes 98312 | tf_op jit(solution)/shard_map/sum_over_z_hi/ppermute | solution.py:260
  167.5 0.9 copy-done.2
  168.4 0.9 copy-done.4
  169.4 1.8 head_grad.1
  171.2 1.1 fusion.5
  172.7 0.9 fusion.7
  173.7 5.5 %collective-permute-start.23 = (f32[128,128]{1,0:T(8,128)S(1)}, f32[128,128]{1,0:T(8,128)S(1)}, u32[]{:S(2)}, u32[]{:S(2)}) collective-permute-start(f32[128,128]{1,0:T(8,128)S(1)} %fusion.24), channel_id=1, source_target_pairs={{0,0},{1,1},{2,2},{3,3},{4,128},{5,129},{6,130},{7,131},{8,256},{9... | collective-permute-start | bytes 196616 | tf_op jit(solution)/shard_map/sum_over_z_hi/ppermute | solution.py:262
  179.2 1.1 fusion.4
  180.2 11.4 %collective-permute-done.23 = f32[128,128]{1,0:T(8,128)S(1)} collective-permute-done((f32[128,128]{1,0:T(8,128)S(1)}, f32[128,128]{1,0:T(8,128)S(1)}, u32[]{:S(2)}, u32[]{:S(2)}) %collective-permute-start.23) | collective-permute-done | bytes 65568 | tf_op jit(solution)/shard_map/sum_over_z_hi/ppermute | solution.py:262
  (62 shorter events, 3.9 us)
Async XLA Ops:
  0.6 42.2 %copy-start = (bf16[1,1024,128]{2,1,0:T(8,128)(2,1)S(1)}, bf16[1,1024,128]{2,1,0:T(8,128)(2,1)}, u32[]{:S(2)}) copy-start(bf16[1,1024,128]{2,1,0:T(8,128)(2,1)} %param.10) | copy-start | bytes 786436
  0.6 10.5 %copy-start.12 = (bf16[128,128]{1,0:T(8,128)(2,1)S(1)}, bf16[128,128]{1,0:T(8,128)(2,1)}, u32[]{:S(2)}) copy-start(bf16[128,128]{1,0:T(8,128)(2,1)} %param.11) | copy-start | bytes 98308
  0.7 12.4 %copy-start.13 = (s32[1,2,8]{2,1,0:T(2,128)S(1)}, s32[1,2,8]{2,1,0:T(2,128)}, u32[]{:S(2)}) copy-start(s32[1,2,8]{2,1,0:T(2,128)} %param.12) | copy-start | bytes 196
  0.7 12.8 %copy-start.10 = (bf16[1,256,128]{2,1,0:T(8,128)(2,1)S(1)}, bf16[1,256,128]{2,1,0:T(8,128)(2,1)}, u32[]{:S(2)}) copy-start(bf16[1,256,128]{2,1,0:T(8,128)(2,1)} %param.8) | copy-start | bytes 196612
  0.7 12.8 %copy-start.8 = (bf16[1,1024,128]{2,1,0:T(8,128)(2,1)S(1)}, bf16[1,1024,128]{2,1,0:T(8,128)(2,1)}, u32[]{:S(2)}) copy-start(bf16[1,1024,128]{2,1,0:T(8,128)(2,1)} %param.9) | copy-start | bytes 786436
  2.3 46.2 %collective-permute-start = (bf16[256,1024]{1,0:T(8,128)(2,1)S(1)}, bf16[256,1024]{1,0:T(8,128)(2,1)}, u32[]{:S(2)}, u32[]{:S(2)}) collective-permute-start(bf16[256,1024]{1,0:T(8,128)(2,1)S(1)} %get-tuple-element.54), channel_id=1, source_target_pairs={{0,4},{1,5},{2,6},{3,7},{4,8},{5,9},{6,10},{7,11},{8,12},{9,13},{1... | collective-permute-start | bytes 1572872 | tf_op jit(solution)/shard_map/sum_over_x/ppermute | solution.py:193
  5.4 43.0 %collective-permute-start.1 = (bf16[256,1024]{1,0:T(8,128)(2,1)S(1)}, bf16[256,1024]{1,0:T(8,128)(2,1)}, u32[]{:S(2)}, u32[]{:S(2)}) collective-permute-start(bf16[256,1024]{1,0:T(8,128)(2,1)S(1)} %get-tuple-element.56), channel_id=1, source_target_pairs={{0,8},{1,9},{2,10},{3,11},{4,12},{5,13},{6,14},{7,15},{8,0},{9,1},... | collective-permute-start | bytes 1572872 | tf_op jit(solution)/shard_map/sum_over_x/ppermute | solution.py:193
  8.1 40.3 %collective-permute-start.2 = (bf16[256,1024]{1,0:T(8,128)(2,1)S(1)}, bf16[256,1024]{1,0:T(8,128)(2,1)}, u32[]{:S(2)}, u32[]{:S(2)}) collective-permute-start(bf16[256,1024]{1,0:T(8,128)(2,1)S(1)} %get-tuple-element.55), channel_id=1, source_target_pairs={{0,12},{1,13},{2,14},{3,15},{4,0},{5,1},{6,2},{7,3},{8,4},{9,5},{1... | collective-permute-start | bytes 1572872 | tf_op jit(solution)/shard_map/sum_over_x/ppermute | solution.py:193
  11.2 3.1 %collective-permute-start.3 = (bf16[128,128]{1,0:T(8,128)(2,1)S(1)}, bf16[128,128]{1,0:T(8,128)(2,1)S(1)}, u32[]{:S(2)}, u32[]{:S(2)}) collective-permute-start(bf16[128,128]{1,0:T(8,128)(2,1)S(1)} %copy-done.12), channel_id=1, source_target_pairs={{0,16},{16,0},{32,48},{48,32},{64,80},{80,64},{96,112},{112,96},{1... | collective-permute-start | bytes 98312 | tf_op jit(solution)/shard_map/gather_projection/ppermute | solution.py:197
  14.3 22.6 %collective-permute-start.4 = (bf16[128,256]{1,0:T(8,128)(2,1)S(1)}, bf16[128,256]{1,0:T(8,128)(2,1)S(1)}, u32[]{:S(2)}, u32[]{:S(2)}) collective-permute-start(bf16[128,256]{1,0:T(8,128)(2,1)S(1)} %get-tuple-element.64), channel_id=1, source_target_pairs={{0,384},{16,400},{32,416},{48,432},{64,448},{80,464},{96,480},{112... | collective-permute-start | bytes 196616 | tf_op jit(solution)/shard_map/gather_projection/ppermute | solution.py:202
  31.9 11.0 %copy-start.5 = (f32[256,1024]{1,0:T(8,128)}, f32[256,1024]{1,0:T(8,128)S(1)}, u32[]{:S(2)}) copy-start(f32[256,1024]{1,0:T(8,128)S(1)} %fusion.11) | copy-start | bytes 3145732
  31.9 16.5 %collective-permute-start.5 = (bf16[128,256]{1,0:T(8,128)(2,1)S(1)}, bf16[128,256]{1,0:T(8,128)(2,1)S(1)}, u32[]{:S(2)}, u32[]{:S(2)}) collective-permute-start(bf16[128,256]{1,0:T(8,128)(2,1)S(1)} %get-tuple-element.64), channel_id=1, source_target_pairs={{0,256},{16,272},{32,288},{48,304},{64,320},{80,336},{96,352},{112... | collective-permute-start | bytes 196616 | tf_op jit(solution)/shard_map/gather_projection/ppermute | solution.py:202
  36.9 11.5 %collective-permute-start.6 = (bf16[128,256]{1,0:T(8,128)(2,1)S(1)}, bf16[128,256]{1,0:T(8,128)(2,1)S(1)}, u32[]{:S(2)}, u32[]{:S(2)}) collective-permute-start(bf16[128,256]{1,0:T(8,128)(2,1)S(1)} %get-tuple-element.64), channel_id=1, source_target_pairs={{0,128},{16,144},{32,160},{48,176},{64,192},{80,208},{96,224},{112... | collective-permute-start | bytes 196616 | tf_op jit(solution)/shard_map/gather_projection/ppermute | solution.py:202
  51.1 24.7 %all-to-all-start = ((bf16[8,32,1024]{2,1,0:T(8,128)(2,1)}), bf16[8,32,1024]{2,1,0:T(8,128)(2,1)S(1)}, u32[]{:S(2)}, u32[]{:S(2)}) async-start(bf16[8,32,1024]{2,1,0:T(8,128)(2,1)} %bitcast.18), calls=%async_computation | async-start | bytes 1048576 | tf_op jit(solution)/shard_map/sum_over_y/all_to_all | solution.py:215
  60.0 16.0 %collective-permute-start.7 = (bf16[256,128]{1,0:T(8,128)(2,1)S(1)}, bf16[256,128]{1,0:T(8,128)(2,1)S(1)}, u32[]{:S(2)}, u32[]{:S(2)}) collective-permute-start(bf16[256,128]{1,0:T(8,128)(2,1)S(1)} %get-tuple-element.35.refs_0_), channel_id=1, source_target_pairs={{0,12},{1,13},{2,14},{3,15},{4,0},{5,1},{6,2},{7,3},{8,4},{9,5},{1... | collective-permute-start | bytes 196616 | tf_op jit(solution)/shard_map/gather_attended/ppermute | solution.py:223
  63.4 12.6 %collective-permute-start.8 = (bf16[256,128]{1,0:T(8,128)(2,1)S(1)}, bf16[256,128]{1,0:T(8,128)(2,1)S(1)}, u32[]{:S(2)}, u32[]{:S(2)}) collective-permute-start(bf16[256,128]{1,0:T(8,128)(2,1)S(1)} %get-tuple-element.35.refs_0_), channel_id=1, source_target_pairs={{0,8},{1,9},{2,10},{3,11},{4,12},{5,13},{6,14},{7,15},{8,0},{9,1},... | collective-permute-start | bytes 196616 | tf_op jit(solution)/shard_map/gather_attended/ppermute | solution.py:223
  66.2 9.8 %collective-permute-start.9 = (bf16[256,128]{1,0:T(8,128)(2,1)S(1)}, bf16[256,128]{1,0:T(8,128)(2,1)S(1)}, u32[]{:S(2)}, u32[]{:S(2)}) collective-permute-start(bf16[256,128]{1,0:T(8,128)(2,1)S(1)} %get-tuple-element.35.refs_0_), channel_id=1, source_target_pairs={{0,4},{1,5},{2,6},{3,7},{4,8},{5,9},{6,10},{7,11},{8,12},{9,13},{1... | collective-permute-start | bytes 196616 | tf_op jit(solution)/shard_map/gather_attended/ppermute | solution.py:223
  76.9 34.0 %all-to-all-start.1 = ((bf16[8,32,1024]{2,1,0:T(8,128)(2,1)}), bf16[8,32,1024]{2,1,0:T(8,128)(2,1)S(1)}, u32[]{:S(2)}, u32[]{:S(2)}) async-start(bf16[8,32,1024]{2,1,0:T(8,128)(2,1)} %broadcast_in_dim.46), calls=%async_computation.1 | async-start | bytes 1048576 | tf_op jit(solution)/shard_map/gather_over_y/all_to_all | solution.py:229
  81.7 14.8 %collective-permute-start.10 = (bf16[4,128,256]{2,1,0:T(8,128)(2,1)S(1)}, bf16[4,128,256]{2,1,0:T(8,128)(2,1)S(1)}, u32[]{:S(2)}, u32[]{:S(2)}) collective-permute-start(bf16[4,128,256]{2,1,0:T(8,128)(2,1)S(1)} %pad_maximum_fusion.refs_4_), channel_id=1, source_target_pairs={{0,96},{16,112},{32,0},{48,16},{64,32},{80,48},{96,64},{112,80},{1... | collective-permute-start | bytes 786440 | tf_op jit(solution)/shard_map/gather_projection/ppermute | solution.py:232
  91.2 13.4 %collective-permute-start.11 = (bf16[4,128,256]{2,1,0:T(8,128)(2,1)S(1)}, bf16[4,128,256]{2,1,0:T(8,128)(2,1)S(1)}, u32[]{:S(2)}, u32[]{:S(2)}) collective-permute-start(bf16[4,128,256]{2,1,0:T(8,128)(2,1)S(1)} %pad_maximum_fusion.refs_4_), channel_id=1, source_target_pairs={{0,64},{16,80},{32,96},{48,112},{64,0},{80,16},{96,32},{112,48},{1... | collective-permute-start | bytes 786440 | tf_op jit(solution)/shard_map/gather_projection/ppermute | solution.py:232
  93.1 17.0 %collective-permute-start.12 = (bf16[4,128,256]{2,1,0:T(8,128)(2,1)S(1)}, bf16[4,128,256]{2,1,0:T(8,128)(2,1)S(1)}, u32[]{:S(2)}, u32[]{:S(2)}) collective-permute-start(bf16[4,128,256]{2,1,0:T(8,128)(2,1)S(1)} %pad_maximum_fusion.refs_4_), channel_id=1, source_target_pairs={{0,32},{16,48},{32,64},{48,80},{64,96},{80,112},{96,0},{112,16},{1... | collective-permute-start | bytes 786440 | tf_op jit(solution)/shard_map/gather_projection/ppermute | solution.py:232
  104.6 0.7 copy-start.1
  110.2 0.7 copy-start.3
  112.1 13.3 %collective-permute-start.13 = (bf16[4,4,128,128]{3,2,1,0:T(8,128)(2,1)}, bf16[4,4,128,128]{3,2,1,0:T(8,128)(2,1)}, u32[]{:S(2)}, u32[]{:S(2)}) collective-permute-start(bf16[4,4,128,128]{3,2,1,0:T(8,128)(2,1)} %get-tuple-element.40), channel_id=1, source_target_pairs={{0,16},{16,0},{32,48},{48,32},{64,80},{80,64},{96,112},{112,96},{1... | collective-permute-start | bytes 1572872 | tf_op jit(solution)/shard_map/sum_over_core/ppermute | solution.py:239
  114.1 34.0 %collective-permute-start.17 = (bf16[256,1024]{1,0:T(8,128)(2,1)S(1)}, bf16[256,1024]{1,0:T(8,128)(2,1)S(1)}, u32[]{:S(2)}, u32[]{:S(2)}) collective-permute-start(bf16[256,1024]{1,0:T(8,128)(2,1)S(1)} %bitcast.78), channel_id=1, source_target_pairs={{0,12},{1,13},{2,14},{3,15},{4,0},{5,1},{6,2},{7,3},{8,4},{9,5},{1... | collective-permute-start | bytes 1572872 | tf_op jit(solution)/shard_map/gather_over_x/ppermute | solution.py:242
  118.0 30.0 %collective-permute-start.18 = (bf16[256,1024]{1,0:T(8,128)(2,1)S(1)}, bf16[256,1024]{1,0:T(8,128)(2,1)S(1)}, u32[]{:S(2)}, u32[]{:S(2)}) collective-permute-start(bf16[256,1024]{1,0:T(8,128)(2,1)S(1)} %bitcast.79), channel_id=1, source_target_pairs={{0,8},{1,9},{2,10},{3,11},{4,12},{5,13},{6,14},{7,15},{8,0},{9,1},... | collective-permute-start | bytes 1572872 | tf_op jit(solution)/shard_map/gather_over_x/ppermute | solution.py:242
  120.9 27.1 %collective-permute-start.19 = (bf16[256,1024]{1,0:T(8,128)(2,1)S(1)}, bf16[256,1024]{1,0:T(8,128)(2,1)}, u32[]{:S(2)}, u32[]{:S(2)}) collective-permute-start(bf16[256,1024]{1,0:T(8,128)(2,1)S(1)} %bitcast.80), channel_id=1, source_target_pairs={{0,4},{1,5},{2,6},{3,7},{4,8},{5,9},{6,10},{7,11},{8,12},{9,13},{1... | collective-permute-start | bytes 1572872 | tf_op jit(solution)/shard_map/gather_over_x/ppermute | solution.py:242
  126.7 0.8 copy-start.7
  127.5 43.7 %copy-start.6 = (f32[256,1024]{1,0:T(8,128)S(1)}, f32[256,1024]{1,0:T(8,128)}, u32[]{:S(2)}) copy-start(f32[256,1024]{1,0:T(8,128)} %copy-done.5) | copy-start | bytes 3145732
  128.2 9.0 %collective-permute-start.14 = (bf16[4,128,128]{2,1,0:T(8,128)(2,1)S(1)}, bf16[4,128,128]{2,1,0:T(8,128)(2,1)}, u32[]{:S(2)}, u32[]{:S(2)}) collective-permute-start(bf16[4,128,128]{2,1,0:T(8,128)(2,1)S(1)} %get-tuple-element.57), channel_id=1, source_target_pairs={{0,32},{16,48},{32,64},{48,80},{64,96},{80,112},{96,0},{112,16},{1... | collective-permute-start | bytes 393224 | tf_op jit(solution)/shard_map/sum_over_z_lo/ppermute | solution.py:250
  132.6 10.1 %collective-permute-start.15 = (bf16[4,128,128]{2,1,0:T(8,128)(2,1)}, bf16[4,128,128]{2,1,0:T(8,128)(2,1)}, u32[]{:S(2)}, u32[]{:S(2)}) collective-permute-start(bf16[4,128,128]{2,1,0:T(8,128)(2,1)} %get-tuple-element.59), channel_id=1, source_target_pairs={{0,64},{16,80},{32,96},{48,112},{64,0},{80,16},{96,32},{112,48},{1... | collective-permute-start | bytes 393224 | tf_op jit(solution)/shard_map/sum_over_z_lo/ppermute | solution.py:250
  137.2 9.7 %collective-permute-start.16 = (bf16[4,128,128]{2,1,0:T(8,128)(2,1)}, bf16[4,128,128]{2,1,0:T(8,128)(2,1)}, u32[]{:S(2)}, u32[]{:S(2)}) collective-permute-start(bf16[4,128,128]{2,1,0:T(8,128)(2,1)} %get-tuple-element.58), channel_id=1, source_target_pairs={{0,96},{16,112},{32,0},{48,16},{64,32},{80,48},{96,64},{112,80},{1... | collective-permute-start | bytes 393224 | tf_op jit(solution)/shard_map/sum_over_z_lo/ppermute | solution.py:250
  148.1 25.5 %collective-permute-start.20 = (bf16[128,128]{1,0:T(8,128)(2,1)S(1)}, bf16[128,128]{1,0:T(8,128)(2,1)S(1)}, u32[]{:S(2)}, u32[]{:S(2)}) collective-permute-start(bf16[128,128]{1,0:T(8,128)(2,1)S(1)} %get-tuple-element.60), channel_id=1, source_target_pairs={{0,128},{16,144},{32,160},{48,176},{64,192},{80,208},{96,224},{112... | collective-permute-start | bytes 98312 | tf_op jit(solution)/shard_map/sum_over_z_hi/ppermute | solution.py:260
  154.0 19.6 %collective-permute-start.21 = (bf16[128,128]{1,0:T(8,128)(2,1)S(1)}, bf16[128,128]{1,0:T(8,128)(2,1)S(1)}, u32[]{:S(2)}, u32[]{:S(2)}) collective-permute-start(bf16[128,128]{1,0:T(8,128)(2,1)S(1)} %get-tuple-element.62), channel_id=1, source_target_pairs={{0,256},{16,272},{32,288},{48,304},{64,320},{80,336},{96,352},{112... | collective-permute-start | bytes 98312 | tf_op jit(solution)/shard_map/sum_over_z_hi/ppermute | solution.py:260
  162.8 10.8 %collective-permute-start.22 = (bf16[128,128]{1,0:T(8,128)(2,1)S(1)}, bf16[128,128]{1,0:T(8,128)(2,1)S(1)}, u32[]{:S(2)}, u32[]{:S(2)}) collective-permute-start(bf16[128,128]{1,0:T(8,128)(2,1)S(1)} %get-tuple-element.61), channel_id=1, source_target_pairs={{0,384},{16,400},{32,416},{48,432},{64,448},{80,464},{96,480},{112... | collective-permute-start | bytes 98312 | tf_op jit(solution)/shard_map/sum_over_z_hi/ppermute | solution.py:260
  167.5 1.0 copy-start.2
  168.4 0.9 copy-start.4
  171.2 1.5 copy-start.9
  171.2 8.0 %copy-start.11 = (bf16[1,256,128]{2,1,0:T(8,128)(2,1)S(1)}, bf16[1,256,128]{2,1,0:T(8,128)(2,1)}, u32[]{:S(2)}) copy-start(bf16[1,256,128]{2,1,0:T(8,128)(2,1)} %param.8) | copy-start | bytes 196612
  173.7 18.0 %collective-permute-start.23 = (f32[128,128]{1,0:T(8,128)S(1)}, f32[128,128]{1,0:T(8,128)S(1)}, u32[]{:S(2)}, u32[]{:S(2)}) collective-permute-start(f32[128,128]{1,0:T(8,128)S(1)} %fusion.24), channel_id=1, source_target_pairs={{0,0},{1,1},{2,2},{3,3},{4,128},{5,129},{6,130},{7,131},{8,256},{9... | collective-permute-start | bytes 196616 | tf_op jit(solution)/shard_map/sum_over_z_hi/ppermute | solution.py:262

commit v3 on v1

v3 whole, which is shorter than its diff:
```python
import math

import jax
import jax.numpy as jnp
from jax import lax
from jax.experimental import pallas as pl
from jax.experimental.pallas import tpu as pltpu
from jax.sharding import PartitionSpec as P

HEAD_DIM = 128
XY = ("section", "mp")
X, YH, YL = 4, 4, 2
ZH, ZL, CORES = 4, 4, 2


def xy_index(x, y):
    return (y % YL) * (X * YH) + x * YH + y // YL


def scene_index(zh, zl, core):
    return (zh * ZL + zl) * CORES + core


def shift_x(k):
    return [(x * YH + y, ((x + k) % X) * YH + y) for x in range(X) for y in range(YH)]


def shift_zl(k):
    return [
        (scene_index(a, b, c), scene_index(a, (b + k) % ZL, c))
        for a in range(ZH)
        for b in range(ZL)
        for c in range(CORES)
    ]


def shift_zh(k):
    return [
        (scene_index(a, b, c), scene_index((a + k) % ZH, b, c))
        for a in range(ZH)
        for b in range(ZL)
        for c in range(CORES)
    ]


def y_groups():
    return [[xy_index(x, y) for y in range(YH * YL)] for x in range(X)]


def z_hi_groups():
    return [
        [scene_index(a, b, c) for a in range(ZH)] for b in range(ZL) for c in range(CORES)
    ]


def other_core():
    return [(s, s ^ 1) for s in range(ZH * ZL * CORES)]


def swap_head_and_scene():
    def index(head, scene):
        x, yh, yl = head
        return (yl * ZH * ZL * CORES + scene_index(*scene)) * X * YH + x * YH + yh

    heads = [(x, yh, yl) for x in range(X) for yh in range(YH) for yl in range(YL)]
    return [(index(h, s), index(s, h)) for h in heads for s in heads]


def exchange(blocks, axis, groups):
    return lax.all_to_all(blocks, axis, 0, 0, axis_index_groups=groups)


def gather(block, axis, groups):
    return exchange(jnp.broadcast_to(block[None], (len(groups[0]), *block.shape)), axis, groups)


def ring_gather(block, axis, shift, size):
    return [block] + [lax.ppermute(block, axis, shift(-k)) for k in range(1, size)]


def ring_exchange(blocks, axis, shift):
    return blocks[:1] + [lax.ppermute(b, axis, shift(k)) for k, b in enumerate(blocks) if k]


def attend_forward(queries, keys, values, visible, scaling):
    scores = jnp.einsum("qd,kd->qk", queries, keys, preferred_element_type=jnp.float32) * scaling
    scores = jnp.where(visible, scores, -1e30)
    largest = jnp.max(scores, axis=-1, keepdims=True)
    exponent = jnp.exp(scores - largest)
    probs = exponent / jnp.sum(exponent, axis=-1, keepdims=True)
    weights = probs.astype(jnp.bfloat16)
    attended = jnp.einsum("qk,kd->qd", weights, values, preferred_element_type=jnp.float32)
    return probs, weights, attended


def attend_backward(queries, keys, values, grads, probs, weights, attended, scaling):
    delta = jnp.sum(grads.astype(jnp.float32) * attended, axis=-1)
    d_values = jnp.einsum("qk,qd->kd", weights, grads, preferred_element_type=jnp.float32)
    d_probs = jnp.einsum("qd,kd->qk", grads, values, preferred_element_type=jnp.float32)
    score_grads = (probs * (d_probs - delta[:, None])).astype(jnp.bfloat16)
    d_queries = scaling * jnp.einsum(
        "qk,kd->qd", score_grads, keys, preferred_element_type=jnp.float32
    )
    d_keys = scaling * jnp.einsum(
        "qk,qd->kd", score_grads, queries, preferred_element_type=jnp.float32
    )
    return [g.astype(jnp.bfloat16) for g in (d_queries, d_keys, d_values)]


VMEM = pl.BlockSpec(memory_space=pltpu.VMEM)
SMEM = pl.BlockSpec(memory_space=pltpu.SMEM)


def cost(flops, count):
    return pl.CostEstimate(flops=flops, bytes_accessed=count, transcendentals=0)


def split_sum_kernel(*refs):
    *part_refs, out_ref = refs
    for y in range(YH * YL):
        left = y * HEAD_DIM
        total = part_refs[0][:, left : left + HEAD_DIM].astype(jnp.float32)
        for part_ref in part_refs[1:]:
            total += part_ref[:, left : left + HEAD_DIM].astype(jnp.float32)
        out_ref[y] = total.astype(out_ref.dtype)


def split_sum(parts):
    tokens = parts[0].shape[0]
    return pl.pallas_call(
        split_sum_kernel,
        out_shape=jax.ShapeDtypeStruct((YH * YL, tokens, HEAD_DIM), jnp.bfloat16),
        in_specs=[VMEM] * len(parts),
        out_specs=VMEM,
        compiler_params=pltpu.CompilerParams(vmem_limit_bytes=16 << 20),
        cost_estimate=cost(parts[0].size * len(parts), 2 * parts[0].size * (len(parts) + 1)),
        name="split_sum",
    )(*parts)


def weight_terms_kernel(place_ref, own_ref, *refs):
    attended_refs, (send_ref, keep_ref) = refs[:X], refs[X:]
    first = place_ref[0] == 0
    for k in range(X):
        x = (place_ref[1] + k) & (X - 1)
        for yh in range(YH):
            low, high = [
                jnp.dot(
                    attended_refs[k][yh * YL + yl],
                    own_ref[...],
                    preferred_element_type=jnp.float32,
                )
                for yl in range(YL)
            ]
            send_ref[yh, x] = jnp.where(first, high, low).astype(jnp.bfloat16)
            keep_ref[yh, x] = jnp.where(first, low, high)


def weight_terms(place, attended, own):
    tokens, columns = own.shape
    shape = (YH, X, HEAD_DIM, columns)
    size = attended[0].size * X
    return pl.pallas_call(
        weight_terms_kernel,
        out_shape=(
            jax.ShapeDtypeStruct(shape, jnp.bfloat16),
            jax.ShapeDtypeStruct(shape, jnp.float32),
        ),
        in_specs=[SMEM] + [VMEM] * (1 + X),
        out_specs=(VMEM, VMEM),
        compiler_params=pltpu.CompilerParams(vmem_limit_bytes=24 << 20),
        cost_estimate=cost(2 * size * columns, 2 * size + 6 * YH * X * HEAD_DIM * columns),
        name="weight_terms",
    )(place, own, *attended)


def head_grad_kernel(place_ref, w_own_ref, w_other_ref, *refs):
    *upstream_refs, out_ref = refs
    core, x, zh, zl = [place_ref[i] for i in range(4)]
    total = jnp.zeros(out_ref.shape, jnp.float32)
    for k in range(X):
        far = (x + k - zh) & (ZH - 1)
        for b in range(ZL):
            near = (b - zl) & (ZL - 1)
            for w_ref, c in ((w_own_ref, core), (w_other_ref, 1 - core)):
                total += lax.dot_general(
                    upstream_refs[k][b * CORES + c],
                    w_ref[near, far],
                    (((1,), (1,)), ((), ())),
                    preferred_element_type=jnp.float32,
                )
    out_ref[...] = total.astype(out_ref.dtype)


def head_grad(place, upstream, w_own, w_other):
    tokens = upstream[0].shape[1]
    size = upstream[0].size * X
    return pl.pallas_call(
        head_grad_kernel,
        out_shape=jax.ShapeDtypeStruct((tokens, HEAD_DIM), jnp.bfloat16),
        in_specs=[SMEM] + [VMEM] * (2 + X),
        out_specs=VMEM,
        compiler_params=pltpu.CompilerParams(vmem_limit_bytes=24 << 20),
        cost_estimate=cost(2 * size * HEAD_DIM, 2 * (size + 2 * w_own.size)),
        name="head_grad",
    )(place, w_own, w_other, *upstream)


def shift_right(number, size):
    return lax.shift_right_logical(number, size.bit_length() - 1)


def sum_f32(parts):
    total = parts[0].astype(jnp.float32)
    for k in range(1, len(parts)):
        total = total + parts[k].astype(jnp.float32)
    return total


def shards(dec_grad, agent_queries, map_keys, map_values, w_out, block_mask, agent_count):
    scaling = 1.0 / math.sqrt(HEAD_DIM)
    mp, scene = lax.axis_index("mp"), lax.axis_index("scene")
    x, core = shift_right(mp, YH), scene & (CORES - 1)
    zh, zl = shift_right(scene, ZL * CORES), shift_right(scene, CORES) & (ZL - 1)
    place = jnp.stack([core, x, zh, zl])
    sample = dec_grad[0, 0]
    tokens, model = sample.shape
    width = model // X

    with jax.named_scope("sum_over_x"):
        pieces = [
            lax.dynamic_slice(sample, (0, ((x + k) & (X - 1)) * width), (tokens, width))
            for k in range(X)
        ]
        partial = split_sum(ring_exchange(pieces, "mp", shift_x))

    with jax.named_scope("gather_projection"):
        w_far = jnp.stack(ring_gather(w_out, "scene", shift_zh, ZH))

    queries, keys, values = agent_queries[0], map_keys[0], map_values[0]
    mask_rows = block_mask[0]
    agent_block, map_block = tokens // mask_rows.shape[0], keys.shape[0] // mask_rows.shape[1]
    visible = jnp.repeat(jnp.repeat(mask_rows == 1, agent_block, axis=0), map_block, axis=1)
    probs, weights, attended = attend_forward(queries, keys, values, visible, scaling)
    with jax.named_scope("gather_attended"):
        attended_near = gather(attended.astype(jnp.bfloat16).T, XY, y_groups())

    partial, attended_near = lax.optimization_barrier((partial, attended_near))
    with jax.named_scope("sum_over_y"):
        summed = sum_f32(exchange(partial, XY, y_groups()))
        row_keep = jnp.arange(tokens) < agent_count[0]
        own = jnp.where(row_keep[:, None], summed, 0.0).astype(jnp.bfloat16)
    with jax.named_scope("gather_attended"):
        attended_all = ring_gather(attended_near, "mp", shift_x, X)
    with jax.named_scope("gather_projection"):
        w_near = jnp.stack(ring_gather(w_far, "scene", shift_zl, ZL))

    own, attended_all, w_far = lax.optimization_barrier((own, attended_all, w_far))
    with jax.named_scope("weight_terms"):
        send, keep = weight_terms(place, attended_all, own)
    with jax.named_scope("sum_over_core"):
        pair = (keep + lax.ppermute(send, "scene", other_core())).astype(jnp.bfloat16)
    with jax.named_scope("gather_over_y"):
        block = gather(own, XY, y_groups())
    pair, w_near = lax.optimization_barrier((pair, w_near))
    with jax.named_scope("gather_projection"):
        w_other = lax.ppermute(w_near, "scene", other_core())
    with jax.named_scope("sum_over_z_lo"):
        parts = [
            lax.dynamic_index_in_dim(pair, (zl + k) & (ZL - 1), 0, keepdims=False)
            for k in range(ZL)
        ]
        near = sum_f32(ring_exchange(parts, "scene", shift_zl)).astype(jnp.bfloat16)

    near, block, w_other = lax.optimization_barrier((near, block, w_other))
    with jax.named_scope("sum_over_z_hi"):
        total = sum_f32(exchange(near, "scene", z_hi_groups()))
        d_wout = lax.ppermute(total, ("section", "scene", "mp"), swap_head_and_scene())
    with jax.named_scope("gather_over_x"):
        upstream = ring_gather(block, "mp", shift_x, X)

    with jax.named_scope("head_gradients"):
        d_attn = head_grad(place, upstream, w_near, w_other)
        d_queries, d_keys, d_values = attend_backward(
            queries, keys, values, d_attn, probs, weights, attended, scaling
        )
    return d_queries[None], d_keys[None], d_values[None], d_wout


def solution(mesh):
    heads = P("scene", None, XY)
    return jax.shard_map(
        shards,
        mesh=mesh,
        in_specs=(
            P("scene", XY, None, None),
            heads,
            heads,
            heads,
            P(XY, "scene"),
            P("scene", None, None),
            P("scene"),
        ),
        out_specs=(heads, heads, heads, P(XY, "scene")),
        check_vma=False,
    )
```

time: 205 us -> 211 us (1.029)
  the two profiles are of different devices: /device:TPU:12 before, /device:TPU:112 now
where the time goes in v3:
time: 211 us; the launch traced here: 210 us
  starting transfers between devices  118 us (56%)
  waiting for transfers between devices  68 us (32%)
  local copies, waits for them, and re-layouts  7.3 us (3%)
  other arithmetic  5.63 us (3%)
  matrix products  4.97 us (2%)
  Pallas kernels  4.43 us (2%)
    ppermute x12, starting transfers between devices, ring_gather(): lax.ppermute(block, axis, shift(-k))  58.3 us
    all_to_all x4, starting transfers between devices, exchange(): return lax.all_to_all(blocks, axis, 0, 0, axis_index_groups=groups)  31.9 us
    ppermute x6, waiting for transfers between devices, ring_exchange(): lax.ppermute(b, axis, shift(k))  26.4 us
    ppermute x1, waiting for transfers between devices, shards(): lax.ppermute(total, ('section', 'scene', 'mp'), swap_head_and_scene())  22 us
    ppermute x6, starting transfers between devices, ring_exchange(): lax.ppermute(b, axis, shift(k))  20 us
    ppermute x12, waiting for transfers between devices, ring_gather(): lax.ppermute(block, axis, shift(-k))  12.9 us
    all_to_all x4, waiting for transfers between devices, exchange(): return lax.all_to_all(blocks, axis, 0, 0, axis_index_groups=groups)  6.67 us
    unnamed x23, local copies, waits for them, and re-layouts  4.31 us
  transfers between devices with their start and end apart: 25, of which 10 were waited for; matrix products, arithmetic and copies ran while one was open for 3% of the time, Pallas kernels for 1%

profile of v3, /device:TPU:112, one launch (start us, length us, event | category | flops | bytes accessed | tf_op | source)
XLA Modules:
  0.0 209.8 jit_solution(10917515771710796477)
XLA Ops:
  1.8 1.3 fusion.24
  3.7 1.0 copy-done.3
  5.8 7.0 %all-to-all-start = ((bf16[8,128,256]{2,1,0:T(8,128)(2,1)}), bf16[8,128,256]{2,1,0:T(8,128)(2,1)S(1)}, u32[]{:S(2)}, u32[]{:S(2)}) async-start(bf16[8,128,256]{2,1,0:T(8,128)(2,1)} %broadcast_in_dim.51), calls=%async_computation | async-start | bytes 1048576 | tf_op jit(solution)/shard_map/gather_attended/all_to_all | solution.py:70
  13.0 3.4 %collective-permute-start = (bf16[256,1024]{1,0:T(8,128)(2,1)S(1)}, bf16[256,1024]{1,0:T(8,128)(2,1)S(1)}, u32[]{:S(2)}, u32[]{:S(2)}) collective-permute-start(bf16[256,1024]{1,0:T(8,128)(2,1)S(1)} %get-tuple-element.33), channel_id=1, source_target_pairs={{0,4},{1,5},{2,6},{3,7},{4,8},{5,9},{6,10},{7,11},{8,12},{9,13},{1... | collective-permute-start | bytes 1572872 | tf_op jit(solution)/shard_map/sum_over_x/ppermute | solution.py:82
  16.4 4.6 %collective-permute-start.1 = (bf16[256,1024]{1,0:T(8,128)(2,1)S(1)}, bf16[256,1024]{1,0:T(8,128)(2,1)S(1)}, u32[]{:S(2)}, u32[]{:S(2)}) collective-permute-start(bf16[256,1024]{1,0:T(8,128)(2,1)S(1)} %get-tuple-element.35), channel_id=1, source_target_pairs={{0,8},{1,9},{2,10},{3,11},{4,12},{5,13},{6,14},{7,15},{8,0},{9,1},... | collective-permute-start | bytes 1572872 | tf_op jit(solution)/shard_map/sum_over_x/ppermute | solution.py:82
  21.0 3.3 %collective-permute-start.2 = (bf16[256,1024]{1,0:T(8,128)(2,1)S(1)}, bf16[256,1024]{1,0:T(8,128)(2,1)S(1)}, u32[]{:S(2)}, u32[]{:S(2)}) collective-permute-start(bf16[256,1024]{1,0:T(8,128)(2,1)S(1)} %get-tuple-element.32), channel_id=1, source_target_pairs={{0,12},{1,13},{2,14},{3,15},{4,0},{5,1},{6,2},{7,3},{8,4},{9,5},{1... | collective-permute-start | bytes 1572872 | tf_op jit(solution)/shard_map/sum_over_x/ppermute | solution.py:82
  24.4 5.6 %collective-permute-done.refs_1_ = bf16[256,1024]{1,0:T(8,128)(2,1)S(1)} collective-permute-done((bf16[256,1024]{1,0:T(8,128)(2,1)S(1)}, bf16[256,1024]{1,0:T(8,128)(2,1)S(1)}, u32[]{:S(2)}, u32[]{:S(2)}) %collective-permute-start) | collective-permute-done | bytes 524320 | tf_op jit(solution)/shard_map/sum_over_x/ppermute | solution.py:82
  30.0 11.5 %collective-permute-done.1.refs_2_ = bf16[256,1024]{1,0:T(8,128)(2,1)S(1)} collective-permute-done((bf16[256,1024]{1,0:T(8,128)(2,1)S(1)}, bf16[256,1024]{1,0:T(8,128)(2,1)S(1)}, u32[]{:S(2)}, u32[]{:S(2)}) %collective-permute-start.1) | collective-permute-done | bytes 524320 | tf_op jit(solution)/shard_map/sum_over_x/ppermute | solution.py:82
  41.4 1.6 collective-permute-done.2.refs_3_
  43.0 1.1 split_sum.1
  44.1 7.2 %all-to-all-start.1 = ((bf16[8,256,128]{2,1,0:T(8,128)(2,1)}), bf16[8,256,128]{2,1,0:T(8,128)(2,1)S(1)}, u32[]{:S(2)}, u32[]{:S(2)}) async-start(bf16[8,256,128]{2,1,0:T(8,128)(2,1)} %split_sum.1), calls=%async_computation.1 | async-start | bytes 1048576 | tf_op jit(solution)/shard_map/sum_over_y/all_to_all | solution.py:70
  51.3 17.3 %collective-permute-start.6 = (bf16[128,128]{1,0:T(8,128)(2,1)S(1)}, bf16[128,128]{1,0:T(8,128)(2,1)S(1)}, u32[]{:S(2)}, u32[]{:S(2)}) collective-permute-start(bf16[128,128]{1,0:T(8,128)(2,1)S(1)} %copy-done.10), channel_id=1, source_target_pairs={{0,384},{16,400},{32,416},{48,432},{64,448},{80,464},{96,480},{112... | collective-permute-start | bytes 98312 | tf_op jit(solution)/shard_map/gather_projection/ppermute | solution.py:78
  68.6 3.1 %collective-permute-start.7 = (bf16[128,128]{1,0:T(8,128)(2,1)S(1)}, bf16[128,128]{1,0:T(8,128)(2,1)S(1)}, u32[]{:S(2)}, u32[]{:S(2)}) collective-permute-start(bf16[128,128]{1,0:T(8,128)(2,1)S(1)} %copy-done.10), channel_id=1, source_target_pairs={{0,256},{16,272},{32,288},{48,304},{64,320},{80,336},{96,352},{112... | collective-permute-start | bytes 98312 | tf_op jit(solution)/shard_map/gather_projection/ppermute | solution.py:78
  72.4 4.5 %collective-permute-start.3 = (bf16[8,128,256]{2,1,0:T(8,128)(2,1)S(1)}, bf16[8,128,256]{2,1,0:T(8,128)(2,1)S(1)}, u32[]{:S(2)}, u32[]{:S(2)}) collective-permute-start(bf16[8,128,256]{2,1,0:T(8,128)(2,1)S(1)} %all-to-all-done.refs_0_), channel_id=1, source_target_pairs={{0,12},{1,13},{2,14},{3,15},{4,0},{5,1},{6,2},{7,3},{8,4},{9,5},{1... | collective-permute-start | bytes 1572872 | tf_op jit(solution)/shard_map/gather_attended/ppermute | solution.py:78
  76.9 3.7 %collective-permute-start.4 = (bf16[8,128,256]{2,1,0:T(8,128)(2,1)S(1)}, bf16[8,128,256]{2,1,0:T(8,128)(2,1)S(1)}, u32[]{:S(2)}, u32[]{:S(2)}) collective-permute-start(bf16[8,128,256]{2,1,0:T(8,128)(2,1)S(1)} %all-to-all-done.refs_0_), channel_id=1, source_target_pairs={{0,8},{1,9},{2,10},{3,11},{4,12},{5,13},{6,14},{7,15},{8,0},{9,1},... | collective-permute-start | bytes 1572872 | tf_op jit(solution)/shard_map/gather_attended/ppermute | solution.py:78
  80.6 1.9 collective-permute-start.5
  82.6 7.8 %collective-permute-start.8 = (bf16[128,128]{1,0:T(8,128)(2,1)S(1)}, bf16[128,128]{1,0:T(8,128)(2,1)S(1)}, u32[]{:S(2)}, u32[]{:S(2)}) collective-permute-start(bf16[128,128]{1,0:T(8,128)(2,1)S(1)} %copy-done.10), channel_id=1, source_target_pairs={{0,128},{16,144},{32,160},{48,176},{64,192},{80,208},{96,224},{112... | collective-permute-start | bytes 98312 | tf_op jit(solution)/shard_map/gather_projection/ppermute | solution.py:78
  90.5 2.3 %collective-permute-done.8 = bf16[128,128]{1,0:T(8,128)(2,1)S(1)} collective-permute-done((bf16[128,128]{1,0:T(8,128)(2,1)S(1)}, bf16[128,128]{1,0:T(8,128)(2,1)S(1)}, u32[]{:S(2)}, u32[]{:S(2)}) %collective-permute-start.8) | collective-permute-done | bytes 32800 | tf_op jit(solution)/shard_map/gather_projection/ppermute | solution.py:78
  93.7 5.0 %collective-permute-done.3.refs_1_ = bf16[8,128,256]{2,1,0:T(8,128)(2,1)S(1)} collective-permute-done((bf16[8,128,256]{2,1,0:T(8,128)(2,1)S(1)}, bf16[8,128,256]{2,1,0:T(8,128)(2,1)S(1)}, u32[]{:S(2)}, u32[]{:S(2)}) %collective-permute-start.3) | collective-permute-done | bytes 524320 | tf_op jit(solution)/shard_map/gather_attended/ppermute | solution.py:78
  98.7 5.6 %collective-permute-done.5.refs_3_ = bf16[8,128,256]{2,1,0:T(8,128)(2,1)S(1)} collective-permute-done((bf16[8,128,256]{2,1,0:T(8,128)(2,1)S(1)}, bf16[8,128,256]{2,1,0:T(8,128)(2,1)S(1)}, u32[]{:S(2)}, u32[]{:S(2)}) %collective-permute-start.5) | collective-permute-done | bytes 524320 | tf_op jit(solution)/shard_map/gather_attended/ppermute | solution.py:78
  105.1 1.0 copy-done.2
  106.1 2.0 weight_terms.1
  108.1 1.9 collective-permute-start.9
  110.0 2.5 %collective-permute-start.10 = (bf16[4,128,128]{2,1,0:T(8,128)(2,1)}, bf16[4,128,128]{2,1,0:T(8,128)(2,1)S(1)}, u32[]{:S(2)}, u32[]{:S(2)}) collective-permute-start(bf16[4,128,128]{2,1,0:T(8,128)(2,1)} %get-tuple-element.40), channel_id=1, source_target_pairs={{0,96},{16,112},{32,0},{48,16},{64,32},{80,48},{96,64},{112,80},{1... | collective-permute-start | bytes 393224 | tf_op jit(solution)/shard_map/gather_projection/ppermute | solution.py:78
  112.5 4.3 %collective-permute-start.11 = (bf16[4,128,128]{2,1,0:T(8,128)(2,1)}, bf16[4,128,128]{2,1,0:T(8,128)(2,1)S(1)}, u32[]{:S(2)}, u32[]{:S(2)}) collective-permute-start(bf16[4,128,128]{2,1,0:T(8,128)(2,1)} %get-tuple-element.40), channel_id=1, source_target_pairs={{0,64},{16,80},{32,96},{48,112},{64,0},{80,16},{96,32},{112,48},{1... | collective-permute-start | bytes 393224 | tf_op jit(solution)/shard_map/gather_projection/ppermute | solution.py:78
  116.8 4.3 %collective-permute-start.12 = (bf16[4,128,128]{2,1,0:T(8,128)(2,1)}, bf16[4,128,128]{2,1,0:T(8,128)(2,1)S(1)}, u32[]{:S(2)}, u32[]{:S(2)}) collective-permute-start(bf16[4,128,128]{2,1,0:T(8,128)(2,1)} %get-tuple-element.40), channel_id=1, source_target_pairs={{0,32},{16,48},{32,64},{48,80},{64,96},{80,112},{96,0},{112,16},{1... | collective-permute-start | bytes 393224 | tf_op jit(solution)/shard_map/gather_projection/ppermute | solution.py:78
  121.1 0.9 broadcast_in_dim.53
  121.9 7.2 %all-to-all-start.2 = ((bf16[8,256,128]{2,1,0:T(8,128)(2,1)}), bf16[8,256,128]{2,1,0:T(8,128)(2,1)S(1)}, u32[]{:S(2)}, u32[]{:S(2)}) async-start(bf16[8,256,128]{2,1,0:T(8,128)(2,1)} %broadcast_in_dim.53), calls=%async_computation.2 | async-start | bytes 1048576 | tf_op jit(solution)/shard_map/gather_over_y/all_to_all | solution.py:70
  129.2 1.0 pad_maximum_fusion.w_own_ref
  130.3 1.9 collective-permute-start.16
  132.3 2.6 %collective-permute-start.13 = (bf16[4,128,128]{2,1,0:T(8,128)(2,1)S(1)}, bf16[4,128,128]{2,1,0:T(8,128)(2,1)S(1)}, u32[]{:S(2)}, u32[]{:S(2)}) collective-permute-start(bf16[4,128,128]{2,1,0:T(8,128)(2,1)S(1)} %get-tuple-element.36), channel_id=1, source_target_pairs={{0,32},{16,48},{32,64},{48,80},{64,96},{80,112},{96,0},{112,16},{1... | collective-permute-start | bytes 393224 | tf_op jit(solution)/shard_map/sum_over_z_lo/ppermute | solution.py:82
  134.8 3.3 %collective-permute-start.14 = (bf16[4,128,128]{2,1,0:T(8,128)(2,1)S(1)}, bf16[4,128,128]{2,1,0:T(8,128)(2,1)S(1)}, u32[]{:S(2)}, u32[]{:S(2)}) collective-permute-start(bf16[4,128,128]{2,1,0:T(8,128)(2,1)S(1)} %get-tuple-element.38), channel_id=1, source_target_pairs={{0,64},{16,80},{32,96},{48,112},{64,0},{80,16},{96,32},{112,48},{1... | collective-permute-start | bytes 393224 | tf_op jit(solution)/shard_map/sum_over_z_lo/ppermute | solution.py:82
  138.2 2.8 %collective-permute-start.15 = (bf16[4,128,128]{2,1,0:T(8,128)(2,1)S(1)}, bf16[4,128,128]{2,1,0:T(8,128)(2,1)S(1)}, u32[]{:S(2)}, u32[]{:S(2)}) collective-permute-start(bf16[4,128,128]{2,1,0:T(8,128)(2,1)S(1)} %get-tuple-element.37), channel_id=1, source_target_pairs={{0,96},{16,112},{32,0},{48,16},{64,32},{80,48},{96,64},{112,80},{1... | collective-permute-start | bytes 393224 | tf_op jit(solution)/shard_map/sum_over_z_lo/ppermute | solution.py:82
  141.0 5.9 %collective-permute-done.14 = bf16[4,128,128]{2,1,0:T(8,128)(2,1)S(1)} collective-permute-done((bf16[4,128,128]{2,1,0:T(8,128)(2,1)S(1)}, bf16[4,128,128]{2,1,0:T(8,128)(2,1)S(1)}, u32[]{:S(2)}, u32[]{:S(2)}) %collective-permute-start.14) | collective-permute-done | bytes 131104 | tf_op jit(solution)/shard_map/sum_over_z_lo/ppermute | solution.py:82
  146.9 2.0 collective-permute-done.15
  149.6 10.6 %all-to-all-start.3 = ((bf16[4,128,128]{2,1,0:T(8,128)(2,1)}), bf16[4,128,128]{2,1,0:T(8,128)(2,1)}, u32[]{:S(2)}, u32[]{:S(2)}) async-start(bf16[4,128,128]{2,1,0:T(8,128)(2,1)} %fusion.12), calls=%async_computation.3 | async-start | bytes 262144 | tf_op jit(solution)/shard_map/sum_over_z_hi/all_to_all | solution.py:70
  160.1 2.5 %collective-permute-start.17 = (bf16[8,256,128]{2,1,0:T(8,128)(2,1)S(1)}, bf16[8,256,128]{2,1,0:T(8,128)(2,1)S(1)}, u32[]{:S(2)}, u32[]{:S(2)}) collective-permute-start(bf16[8,256,128]{2,1,0:T(8,128)(2,1)S(1)} %all-to-all-done.2.refs_0_), channel_id=1, source_target_pairs={{0,12},{1,13},{2,14},{3,15},{4,0},{5,1},{6,2},{7,3},{8,4},{9,5},{1... | collective-permute-start | bytes 1572872 | tf_op jit(solution)/shard_map/gather_over_x/ppermute | solution.py:78
  162.6 3.7 %collective-permute-start.18 = (bf16[8,256,128]{2,1,0:T(8,128)(2,1)S(1)}, bf16[8,256,128]{2,1,0:T(8,128)(2,1)S(1)}, u32[]{:S(2)}, u32[]{:S(2)}) collective-permute-start(bf16[8,256,128]{2,1,0:T(8,128)(2,1)S(1)} %all-to-all-done.2.refs_0_), channel_id=1, source_target_pairs={{0,8},{1,9},{2,10},{3,11},{4,12},{5,13},{6,14},{7,15},{8,0},{9,1},... | collective-permute-start | bytes 1572872 | tf_op jit(solution)/shard_map/gather_over_x/ppermute | solution.py:78
  166.4 2.7 %collective-permute-start.19 = (bf16[8,256,128]{2,1,0:T(8,128)(2,1)S(1)}, bf16[8,256,128]{2,1,0:T(8,128)(2,1)S(1)}, u32[]{:S(2)}, u32[]{:S(2)}) collective-permute-start(bf16[8,256,128]{2,1,0:T(8,128)(2,1)S(1)} %all-to-all-done.2.refs_0_), channel_id=1, source_target_pairs={{0,4},{1,5},{2,6},{3,7},{4,8},{5,9},{6,10},{7,11},{8,12},{9,13},{1... | collective-permute-start | bytes 1572872 | tf_op jit(solution)/shard_map/gather_over_x/ppermute | solution.py:78
  169.1 6.7 %all-to-all-done.3 = bf16[4,128,128]{2,1,0:T(8,128)(2,1)} async-done(((bf16[4,128,128]{2,1,0:T(8,128)(2,1)}), bf16[4,128,128]{2,1,0:T(8,128)(2,1)}, u32[]{:S(2)}, u32[]{:S(2)}) %all-to-all-start.3) | async-done | bytes 131104 | tf_op jit(solution)/shard_map/sum_over_z_hi/all_to_all | solution.py:70
  175.8 1.5 add_bitcast_fusion
  177.2 3.6 %collective-permute-start.20 = (f32[128,128]{1,0:T(8,128)}, f32[128,128]{1,0:T(8,128)}, u32[]{:S(2)}, u32[]{:S(2)}) collective-permute-start(f32[128,128]{1,0:T(8,128)} %add_bitcast_fusion), channel_id=1, source_target_pairs={{0,0},{16,512},{32,1},{48,513},{64,2},{80,514},{96,3},{112,515},{1... | collective-permute-start | bytes 196616 | tf_op jit(solution)/shard_map/sum_over_z_hi/ppermute | solution.py:278
  181.6 22.0 %collective-permute-done.20 = f32[128,128]{1,0:T(8,128)} collective-permute-done((f32[128,128]{1,0:T(8,128)}, f32[128,128]{1,0:T(8,128)}, u32[]{:S(2)}, u32[]{:S(2)}) %collective-permute-start.20) | collective-permute-done | bytes 65568 | tf_op jit(solution)/shard_map/sum_over_z_hi/ppermute | solution.py:278
  203.6 1.3 head_grad.1
  204.9 1.1 fusion.5
  206.4 1.1 fusion.4
  207.4 0.9 fusion.7
  208.3 1.5 copy.16
  (54 shorter events, 6.8 us)
Async XLA Ops:
  0.6 1.1 copy-start
  1.7 2.9 %copy-start.6 = (bf16[1,1024,128]{2,1,0:T(8,128)(2,1)S(1)}, bf16[1,1024,128]{2,1,0:T(8,128)(2,1)}, u32[]{:S(2)}) copy-start(bf16[1,1024,128]{2,1,0:T(8,128)(2,1)} %param.10) | copy-start | bytes 786436
  3.7 1.0 copy-start.3
  4.6 8.2 %copy-start.5 = (bf16[1,1,256,4096]{3,2,1,0:T(8,128)(2,1)S(1)}, bf16[1,1,256,4096]{3,2,1,0:T(8,128)(2,1)}, u32[]{:S(2)}) copy-start(bf16[1,1,256,4096]{3,2,1,0:T(8,128)(2,1)} %param.7) | copy-start | bytes 6291460
  5.8 38.3 %all-to-all-start = ((bf16[8,128,256]{2,1,0:T(8,128)(2,1)}), bf16[8,128,256]{2,1,0:T(8,128)(2,1)S(1)}, u32[]{:S(2)}, u32[]{:S(2)}) async-start(bf16[8,128,256]{2,1,0:T(8,128)(2,1)} %broadcast_in_dim.51), calls=%async_computation | async-start | bytes 1048576 | tf_op jit(solution)/shard_map/gather_attended/all_to_all | solution.py:70
  13.0 38.4 %copy-start.10 = (bf16[128,128]{1,0:T(8,128)(2,1)S(1)}, bf16[128,128]{1,0:T(8,128)(2,1)}, u32[]{:S(2)}) copy-start(bf16[128,128]{1,0:T(8,128)(2,1)} %param.11) | copy-start | bytes 98308
  13.0 17.0 %collective-permute-start = (bf16[256,1024]{1,0:T(8,128)(2,1)S(1)}, bf16[256,1024]{1,0:T(8,128)(2,1)S(1)}, u32[]{:S(2)}, u32[]{:S(2)}) collective-permute-start(bf16[256,1024]{1,0:T(8,128)(2,1)S(1)} %get-tuple-element.33), channel_id=1, source_target_pairs={{0,4},{1,5},{2,6},{3,7},{4,8},{5,9},{6,10},{7,11},{8,12},{9,13},{1... | collective-permute-start | bytes 1572872 | tf_op jit(solution)/shard_map/sum_over_x/ppermute | solution.py:82
  16.4 25.0 %collective-permute-start.1 = (bf16[256,1024]{1,0:T(8,128)(2,1)S(1)}, bf16[256,1024]{1,0:T(8,128)(2,1)S(1)}, u32[]{:S(2)}, u32[]{:S(2)}) collective-permute-start(bf16[256,1024]{1,0:T(8,128)(2,1)S(1)} %get-tuple-element.35), channel_id=1, source_target_pairs={{0,8},{1,9},{2,10},{3,11},{4,12},{5,13},{6,14},{7,15},{8,0},{9,1},... | collective-permute-start | bytes 1572872 | tf_op jit(solution)/shard_map/sum_over_x/ppermute | solution.py:82
  21.0 21.9 %collective-permute-start.2 = (bf16[256,1024]{1,0:T(8,128)(2,1)S(1)}, bf16[256,1024]{1,0:T(8,128)(2,1)S(1)}, u32[]{:S(2)}, u32[]{:S(2)}) collective-permute-start(bf16[256,1024]{1,0:T(8,128)(2,1)S(1)} %get-tuple-element.32), channel_id=1, source_target_pairs={{0,12},{1,13},{2,14},{3,15},{4,0},{5,1},{6,2},{7,3},{8,4},{9,5},{1... | collective-permute-start | bytes 1572872 | tf_op jit(solution)/shard_map/sum_over_x/ppermute | solution.py:82
  44.1 49.4 %all-to-all-start.1 = ((bf16[8,256,128]{2,1,0:T(8,128)(2,1)}), bf16[8,256,128]{2,1,0:T(8,128)(2,1)S(1)}, u32[]{:S(2)}, u32[]{:S(2)}) async-start(bf16[8,256,128]{2,1,0:T(8,128)(2,1)} %split_sum.1), calls=%async_computation.1 | async-start | bytes 1048576 | tf_op jit(solution)/shard_map/sum_over_y/all_to_all | solution.py:70
  51.3 31.3 %collective-permute-start.6 = (bf16[128,128]{1,0:T(8,128)(2,1)S(1)}, bf16[128,128]{1,0:T(8,128)(2,1)S(1)}, u32[]{:S(2)}, u32[]{:S(2)}) collective-permute-start(bf16[128,128]{1,0:T(8,128)(2,1)S(1)} %copy-done.10), channel_id=1, source_target_pairs={{0,384},{16,400},{32,416},{48,432},{64,448},{80,464},{96,480},{112... | collective-permute-start | bytes 98312 | tf_op jit(solution)/shard_map/gather_projection/ppermute | solution.py:78
  68.6 21.9 %collective-permute-start.7 = (bf16[128,128]{1,0:T(8,128)(2,1)S(1)}, bf16[128,128]{1,0:T(8,128)(2,1)S(1)}, u32[]{:S(2)}, u32[]{:S(2)}) collective-permute-start(bf16[128,128]{1,0:T(8,128)(2,1)S(1)} %copy-done.10), channel_id=1, source_target_pairs={{0,256},{16,272},{32,288},{48,304},{64,320},{80,336},{96,352},{112... | collective-permute-start | bytes 98312 | tf_op jit(solution)/shard_map/gather_projection/ppermute | solution.py:78
  72.4 26.3 %collective-permute-start.3 = (bf16[8,128,256]{2,1,0:T(8,128)(2,1)S(1)}, bf16[8,128,256]{2,1,0:T(8,128)(2,1)S(1)}, u32[]{:S(2)}, u32[]{:S(2)}) collective-permute-start(bf16[8,128,256]{2,1,0:T(8,128)(2,1)S(1)} %all-to-all-done.refs_0_), channel_id=1, source_target_pairs={{0,12},{1,13},{2,14},{3,15},{4,0},{5,1},{6,2},{7,3},{8,4},{9,5},{1... | collective-permute-start | bytes 1572872 | tf_op jit(solution)/shard_map/gather_attended/ppermute | solution.py:78
  76.9 21.8 %collective-permute-start.4 = (bf16[8,128,256]{2,1,0:T(8,128)(2,1)S(1)}, bf16[8,128,256]{2,1,0:T(8,128)(2,1)S(1)}, u32[]{:S(2)}, u32[]{:S(2)}) collective-permute-start(bf16[8,128,256]{2,1,0:T(8,128)(2,1)S(1)} %all-to-all-done.refs_0_), channel_id=1, source_target_pairs={{0,8},{1,9},{2,10},{3,11},{4,12},{5,13},{6,14},{7,15},{8,0},{9,1},... | collective-permute-start | bytes 1572872 | tf_op jit(solution)/shard_map/gather_attended/ppermute | solution.py:78
  80.6 23.6 %collective-permute-start.5 = (bf16[8,128,256]{2,1,0:T(8,128)(2,1)S(1)}, bf16[8,128,256]{2,1,0:T(8,128)(2,1)S(1)}, u32[]{:S(2)}, u32[]{:S(2)}) collective-permute-start(bf16[8,128,256]{2,1,0:T(8,128)(2,1)S(1)} %all-to-all-done.refs_0_), channel_id=1, source_target_pairs={{0,4},{1,5},{2,6},{3,7},{4,8},{5,9},{6,10},{7,11},{8,12},{9,13},{1... | collective-permute-start | bytes 1572872 | tf_op jit(solution)/shard_map/gather_attended/ppermute | solution.py:78
  82.6 10.2 %collective-permute-start.8 = (bf16[128,128]{1,0:T(8,128)(2,1)S(1)}, bf16[128,128]{1,0:T(8,128)(2,1)S(1)}, u32[]{:S(2)}, u32[]{:S(2)}) collective-permute-start(bf16[128,128]{1,0:T(8,128)(2,1)S(1)} %copy-done.10), channel_id=1, source_target_pairs={{0,128},{16,144},{32,160},{48,176},{64,192},{80,208},{96,224},{112... | collective-permute-start | bytes 98312 | tf_op jit(solution)/shard_map/gather_projection/ppermute | solution.py:78
  104.3 0.8 copy-start.1
  105.0 1.0 copy-start.2
  108.1 22.0 %collective-permute-start.9 = (bf16[4,4,128,128]{3,2,1,0:T(8,128)(2,1)}, bf16[4,4,128,128]{3,2,1,0:T(8,128)(2,1)S(1)}, u32[]{:S(2)}, u32[]{:S(2)}) collective-permute-start(bf16[4,4,128,128]{3,2,1,0:T(8,128)(2,1)} %get-tuple-element.26), channel_id=1, source_target_pairs={{0,16},{16,0},{32,48},{48,32},{64,80},{80,64},{96,112},{112,96},{1... | collective-permute-start | bytes 1572872 | tf_op jit(solution)/shard_map/sum_over_core/ppermute | solution.py:262
  110.0 19.1 %collective-permute-start.10 = (bf16[4,128,128]{2,1,0:T(8,128)(2,1)}, bf16[4,128,128]{2,1,0:T(8,128)(2,1)S(1)}, u32[]{:S(2)}, u32[]{:S(2)}) collective-permute-start(bf16[4,128,128]{2,1,0:T(8,128)(2,1)} %get-tuple-element.40), channel_id=1, source_target_pairs={{0,96},{16,112},{32,0},{48,16},{64,32},{80,48},{96,64},{112,80},{1... | collective-permute-start | bytes 393224 | tf_op jit(solution)/shard_map/gather_projection/ppermute | solution.py:78
  112.5 16.7 %collective-permute-start.11 = (bf16[4,128,128]{2,1,0:T(8,128)(2,1)}, bf16[4,128,128]{2,1,0:T(8,128)(2,1)S(1)}, u32[]{:S(2)}, u32[]{:S(2)}) collective-permute-start(bf16[4,128,128]{2,1,0:T(8,128)(2,1)} %get-tuple-element.40), channel_id=1, source_target_pairs={{0,64},{16,80},{32,96},{48,112},{64,0},{80,16},{96,32},{112,48},{1... | collective-permute-start | bytes 393224 | tf_op jit(solution)/shard_map/gather_projection/ppermute | solution.py:78
  116.8 12.4 %collective-permute-start.12 = (bf16[4,128,128]{2,1,0:T(8,128)(2,1)}, bf16[4,128,128]{2,1,0:T(8,128)(2,1)S(1)}, u32[]{:S(2)}, u32[]{:S(2)}) collective-permute-start(bf16[4,128,128]{2,1,0:T(8,128)(2,1)} %get-tuple-element.40), channel_id=1, source_target_pairs={{0,32},{16,48},{32,64},{48,80},{64,96},{80,112},{96,0},{112,16},{1... | collective-permute-start | bytes 393224 | tf_op jit(solution)/shard_map/gather_projection/ppermute | solution.py:78
  121.9 27.6 %all-to-all-start.2 = ((bf16[8,256,128]{2,1,0:T(8,128)(2,1)}), bf16[8,256,128]{2,1,0:T(8,128)(2,1)S(1)}, u32[]{:S(2)}, u32[]{:S(2)}) async-start(bf16[8,256,128]{2,1,0:T(8,128)(2,1)} %broadcast_in_dim.53), calls=%async_computation.2 | async-start | bytes 1048576 | tf_op jit(solution)/shard_map/gather_over_y/all_to_all | solution.py:70
  130.3 19.3 %collective-permute-start.16 = (bf16[4,4,128,128]{3,2,1,0:T(8,128)(2,1)S(1)}, bf16[4,4,128,128]{3,2,1,0:T(8,128)(2,1)S(1)}, u32[]{:S(2)}, u32[]{:S(2)}) collective-permute-start(bf16[4,4,128,128]{3,2,1,0:T(8,128)(2,1)S(1)} %pad_maximum_fusion.w_own_ref), channel_id=1, source_target_pairs={{0,16},{16,0},{32,48},{48,32},{64,80},{80,64},{96,112},{112,96},{1... | collective-permute-start | bytes 1572872 | tf_op jit(solution)/shard_map/gather_projection/ppermute | solution.py:267
  132.3 8.7 %collective-permute-start.13 = (bf16[4,128,128]{2,1,0:T(8,128)(2,1)S(1)}, bf16[4,128,128]{2,1,0:T(8,128)(2,1)S(1)}, u32[]{:S(2)}, u32[]{:S(2)}) collective-permute-start(bf16[4,128,128]{2,1,0:T(8,128)(2,1)S(1)} %get-tuple-element.36), channel_id=1, source_target_pairs={{0,32},{16,48},{32,64},{48,80},{64,96},{80,112},{96,0},{112,16},{1... | collective-permute-start | bytes 393224 | tf_op jit(solution)/shard_map/sum_over_z_lo/ppermute | solution.py:82
  134.8 12.0 %collective-permute-start.14 = (bf16[4,128,128]{2,1,0:T(8,128)(2,1)S(1)}, bf16[4,128,128]{2,1,0:T(8,128)(2,1)S(1)}, u32[]{:S(2)}, u32[]{:S(2)}) collective-permute-start(bf16[4,128,128]{2,1,0:T(8,128)(2,1)S(1)} %get-tuple-element.38), channel_id=1, source_target_pairs={{0,64},{16,80},{32,96},{48,112},{64,0},{80,16},{96,32},{112,48},{1... | collective-permute-start | bytes 393224 | tf_op jit(solution)/shard_map/sum_over_z_lo/ppermute | solution.py:82
  138.2 10.7 %collective-permute-start.15 = (bf16[4,128,128]{2,1,0:T(8,128)(2,1)S(1)}, bf16[4,128,128]{2,1,0:T(8,128)(2,1)S(1)}, u32[]{:S(2)}, u32[]{:S(2)}) collective-permute-start(bf16[4,128,128]{2,1,0:T(8,128)(2,1)S(1)} %get-tuple-element.37), channel_id=1, source_target_pairs={{0,96},{16,112},{32,0},{48,16},{64,32},{80,48},{96,64},{112,80},{1... | collective-permute-start | bytes 393224 | tf_op jit(solution)/shard_map/sum_over_z_lo/ppermute | solution.py:82
  149.6 26.2 %all-to-all-start.3 = ((bf16[4,128,128]{2,1,0:T(8,128)(2,1)}), bf16[4,128,128]{2,1,0:T(8,128)(2,1)}, u32[]{:S(2)}, u32[]{:S(2)}) async-start(bf16[4,128,128]{2,1,0:T(8,128)(2,1)} %fusion.12), calls=%async_computation.3 | async-start | bytes 262144 | tf_op jit(solution)/shard_map/sum_over_z_hi/all_to_all | solution.py:70
  160.1 43.4 %collective-permute-start.17 = (bf16[8,256,128]{2,1,0:T(8,128)(2,1)S(1)}, bf16[8,256,128]{2,1,0:T(8,128)(2,1)S(1)}, u32[]{:S(2)}, u32[]{:S(2)}) collective-permute-start(bf16[8,256,128]{2,1,0:T(8,128)(2,1)S(1)} %all-to-all-done.2.refs_0_), channel_id=1, source_target_pairs={{0,12},{1,13},{2,14},{3,15},{4,0},{5,1},{6,2},{7,3},{8,4},{9,5},{1... | collective-permute-start | bytes 1572872 | tf_op jit(solution)/shard_map/gather_over_x/ppermute | solution.py:78
  162.6 40.9 %collective-permute-start.18 = (bf16[8,256,128]{2,1,0:T(8,128)(2,1)S(1)}, bf16[8,256,128]{2,1,0:T(8,128)(2,1)S(1)}, u32[]{:S(2)}, u32[]{:S(2)}) collective-permute-start(bf16[8,256,128]{2,1,0:T(8,128)(2,1)S(1)} %all-to-all-done.2.refs_0_), channel_id=1, source_target_pairs={{0,8},{1,9},{2,10},{3,11},{4,12},{5,13},{6,14},{7,15},{8,0},{9,1},... | collective-permute-start | bytes 1572872 | tf_op jit(solution)/shard_map/gather_over_x/ppermute | solution.py:78
  166.4 37.2 %collective-permute-start.19 = (bf16[8,256,128]{2,1,0:T(8,128)(2,1)S(1)}, bf16[8,256,128]{2,1,0:T(8,128)(2,1)S(1)}, u32[]{:S(2)}, u32[]{:S(2)}) collective-permute-start(bf16[8,256,128]{2,1,0:T(8,128)(2,1)S(1)} %all-to-all-done.2.refs_0_), channel_id=1, source_target_pairs={{0,4},{1,5},{2,6},{3,7},{4,8},{5,9},{6,10},{7,11},{8,12},{9,13},{1... | collective-permute-start | bytes 1572872 | tf_op jit(solution)/shard_map/gather_over_x/ppermute | solution.py:78
  177.2 26.4 %collective-permute-start.20 = (f32[128,128]{1,0:T(8,128)}, f32[128,128]{1,0:T(8,128)}, u32[]{:S(2)}, u32[]{:S(2)}) collective-permute-start(f32[128,128]{1,0:T(8,128)} %add_bitcast_fusion), channel_id=1, source_target_pairs={{0,0},{16,512},{32,1},{48,513},{64,2},{80,514},{96,3},{112,515},{1... | collective-permute-start | bytes 196616 | tf_op jit(solution)/shard_map/sum_over_z_hi/ppermute | solution.py:278
  181.6 23.3 %copy-start.4 = (f32[256,1024]{1,0:T(8,128)S(1)}, f32[256,1024]{1,0:T(8,128)}, u32[]{:S(2)}) copy-start(f32[256,1024]{1,0:T(8,128)} %copy-done.3) | copy-start | bytes 3145732
  181.6 24.4 %copy-start.8 = (f32[256,128]{1,0:T(8,128)S(1)}, f32[256,128]{1,0:T(8,128)}, u32[]{:S(2)}) copy-start(f32[256,128]{1,0:T(8,128)} %copy.11) | copy-start | bytes 393220
  181.6 24.5 %copy-start.7 = (bf16[1,1024,128]{2,1,0:T(8,128)(2,1)S(1)}, bf16[1,1024,128]{2,1,0:T(8,128)(2,1)}, u32[]{:S(2)}) copy-start(bf16[1,1024,128]{2,1,0:T(8,128)(2,1)} %param.10) | copy-start | bytes 786436
  204.8 1.5 copy-start.9

commit v4 on v2

--- a/solution.py
+++ b/solution.py
@@ -34,12 +34,15 @@
     ]
 
 
-def shift_zh(k):
+def z_lo_groups():
     return [
-        (scene_index(a, b, c), scene_index((a + k) % ZH, b, c))
-        for a in range(ZH)
-        for b in range(ZL)
-        for c in range(CORES)
+        [scene_index(a, b, c) for b in range(ZL)] for a in range(ZH) for c in range(CORES)
+    ]
+
+
+def z_hi_groups():
+    return [
+        [scene_index(a, b, c) for a in range(ZH)] for b in range(ZL) for c in range(CORES)
     ]
 
 
@@ -88,10 +91,11 @@
     return [g.astype(jnp.bfloat16) for g in (d_queries, d_keys, d_values)]
 
 
-def weight_terms_kernel(core_ref, block_ref, *refs):
+def weight_terms_kernel(place_ref, block_ref, *refs):
     attended, (send_ref, keep_ref) = refs[:X], refs[X:]
-    first = core_ref[0] == 0
+    first = place_ref[0] == 0
     for k in range(X):
+        head = (place_ref[1] + k) & (X - 1)
         term = lax.dot_general(
             attended[k][...],
             block_ref[...],
@@ -102,11 +106,11 @@
             left = b * CORES * HEAD_DIM
             low = term[:, left : left + HEAD_DIM]
             high = term[:, left + HEAD_DIM : left + 2 * HEAD_DIM]
-            send_ref[b, k] = jnp.where(first, high, low).astype(jnp.bfloat16)
-            keep_ref[b, k] = jnp.where(first, low, high)
-
-
-def weight_terms(core, block, attended):
+            send_ref[b, head] = jnp.where(first, high, low).astype(jnp.bfloat16)
+            keep_ref[b, head] = jnp.where(first, low, high)
+
+
+def weight_terms(place, block, attended):
     rows, width = block.shape
     shape = (ZL, X, HEAD_DIM, HEAD_DIM)
     vmem = pl.BlockSpec(memory_space=pltpu.VMEM)
@@ -125,34 +129,37 @@
             transcendentals=0,
         ),
         name="weight_terms",
-    )(core.reshape(1), block, *attended)
-
-
-def head_grad_kernel(place_ref, *refs):
-    blocks, weights, out_ref = refs[:X], refs[X : X + ZL], refs[X + ZL]
-    x, zh, zl = place_ref[0], place_ref[1], place_ref[2]
-    wide = CORES * HEAD_DIM
+    )(place, block, *attended)
+
+
+def head_grad_kernel(place_ref, w_own_ref, w_other_ref, *refs):
+    *blocks, out_ref = refs
+    core, x, zl = [place_ref[i] for i in range(3)]
     total = jnp.zeros(out_ref.shape, jnp.float32)
     for k in range(X):
-        far = (x + k - zh) & (ZH - 1)
-        for i in range(ZL):
-            left = pl.multiple_of(((zl + i) & (ZL - 1)) * wide, wide)
-            total += lax.dot_general(
-                blocks[k][:, pl.ds(left, wide)],
-                weights[i][far],
-                (((1,), (1,)), ((), ())),
-                preferred_element_type=jnp.float32,
-            )
+        far = (x + k) & (X - 1)
+        for b in range(ZL):
+            near = (b - zl) & (ZL - 1)
+            left = b * CORES * HEAD_DIM
+            own, other = w_own_ref[near, far], w_other_ref[near, far]
+            first, second = jnp.where(core == 0, own, other), jnp.where(core == 0, other, own)
+            for c, weight in enumerate((first, second)):
+                total += lax.dot_general(
+                    blocks[k][:, left + c * HEAD_DIM : left + (c + 1) * HEAD_DIM],
+                    weight,
+                    (((1,), (1,)), ((), ())),
+                    preferred_element_type=jnp.float32,
+                )
     out_ref[...] = total.astype(out_ref.dtype)
 
 
-def head_grad(place, blocks, weights):
+def head_grad(place, blocks, w_own, w_other):
     rows, width = blocks[0].shape
     vmem = pl.BlockSpec(memory_space=pltpu.VMEM)
     return pl.pallas_call(
         head_grad_kernel,
         out_shape=jax.ShapeDtypeStruct((rows, HEAD_DIM), jnp.bfloat16),
-        in_specs=[pl.BlockSpec(memory_space=pltpu.SMEM)] + [vmem] * (X + ZL),
+        in_specs=[pl.BlockSpec(memory_space=pltpu.SMEM)] + [vmem] * (2 + X),
         out_specs=vmem,
         compiler_params=pltpu.CompilerParams(vmem_limit_bytes=24 << 20),
         cost_estimate=pl.CostEstimate(
@@ -161,7 +168,7 @@
             transcendentals=0,
         ),
         name="head_grad",
-    )(place, *blocks, *weights)
+    )(place, w_own, w_other, *blocks)
 
 
 def shift_right(number, size):
@@ -170,8 +177,8 @@
 
 def sum_f32(parts):
     total = parts[0].astype(jnp.float32)
-    for part in parts[1:]:
-        total = total + part.astype(jnp.float32)
+    for k in range(1, len(parts)):
+        total = total + parts[k].astype(jnp.float32)
     return total
 
 
@@ -179,8 +186,9 @@
     scaling = 1.0 / math.sqrt(HEAD_DIM)
     section, mp, scene = (lax.axis_index(name) for name in ("section", "mp", "scene"))
     x, y = shift_right(mp, YH), (mp & (YH - 1)) * YL + section
-    zh, zl = shift_right(scene, ZL * CORES), shift_right(scene, CORES) & (ZL - 1)
+    zl = shift_right(scene, CORES) & (ZL - 1)
     core = scene & (CORES - 1)
+    place = jnp.stack([core, x, zl])
     sample = dec_grad[0, 0]
     tokens, model = sample.shape
     width = model // X
@@ -194,13 +202,8 @@
         partial = sum_f32([pieces[0]] + arrived).astype(jnp.bfloat16)
 
     with jax.named_scope("gather_projection"):
-        w_other = lax.ppermute(w_out, "scene", other_core())
-        w_chip = jnp.concatenate(
-            [jnp.where(core == 0, w_out, w_other), jnp.where(core == 0, w_other, w_out)], axis=1
-        )
-        w_far = jnp.stack(
-            [w_chip] + [lax.ppermute(w_chip, "scene", shift_zh(-k)) for k in range(1, ZH)]
-        )
+        w_spread = jnp.broadcast_to(w_out[None], (ZH, *w_out.shape))
+        w_far = lax.all_to_all(w_spread, "scene", 0, 0, axis_index_groups=z_hi_groups())
 
     queries, keys, values = agent_queries[0], map_keys[0], map_values[0]
     mask_rows = block_mask[0]
@@ -223,46 +226,43 @@
             lax.ppermute(attended_rounded, "mp", shift_x(-k)) for k in range(1, X)
         ]
 
-    own, attended_near, w_far = lax.optimization_barrier((own, attended_near, w_far))
+    own, attended_near = lax.optimization_barrier((own, attended_near))
     with jax.named_scope("gather_over_y"):
         spread = jnp.broadcast_to(own[None], (YH * YL, rows, width))
         block = lax.all_to_all(spread, XY, 0, 0, axis_index_groups=y_groups())
         block = block.reshape(tokens, width)
     with jax.named_scope("gather_projection"):
-        w_near = [w_far] + [lax.ppermute(w_far, "scene", shift_zl(-k)) for k in range(1, ZL)]
+        w_near = jnp.stack(
+            [w_far] + [lax.ppermute(w_far, "scene", shift_zl(-k)) for k in range(1, ZL)]
+        )
 
     block, w_near = lax.optimization_barrier((block, w_near))
     with jax.named_scope("weight_terms"):
-        send, keep = weight_terms(core, block, attended_near)
+        send, keep = weight_terms(place, block, attended_near)
 
     with jax.named_scope("sum_over_core"):
         pair = sum_f32([keep, lax.ppermute(send, "scene", other_core())]).astype(jnp.bfloat16)
 
+    with jax.named_scope("gather_projection"):
+        w_other = lax.ppermute(w_near, "scene", other_core())
+
     with jax.named_scope("gather_over_x"):
         upstream = [block] + [lax.ppermute(block, "mp", shift_x(-k)) for k in range(1, X)]
 
     with jax.named_scope("sum_over_z_lo"):
-        parts = [
-            lax.dynamic_index_in_dim(pair, (zl + k) & (ZL - 1), 0, keepdims=False)
-            for k in range(ZL)
-        ]
         near = sum_f32(
-            parts[:1] + [lax.ppermute(parts[k], "scene", shift_zl(k)) for k in range(1, ZL)]
+            lax.all_to_all(pair, "scene", 0, 0, axis_index_groups=z_lo_groups())
         ).astype(jnp.bfloat16)
 
-    near, upstream, w_near = lax.optimization_barrier((near, upstream, w_near))
+    near, upstream, w_other = lax.optimization_barrier((near, upstream, w_other))
     with jax.named_scope("sum_over_z_hi"):
-        parts = [
-            lax.dynamic_index_in_dim(near, (zh + k - x) & (X - 1), 0, keepdims=False)
-            for k in range(ZH)
-        ]
         summed_block = sum_f32(
-            parts[:1] + [lax.ppermute(parts[k], "scene", shift_zh(k)) for k in range(1, ZH)]
+            lax.all_to_all(near, "scene", 0, 0, axis_index_groups=z_hi_groups())
         )
         d_wout = lax.ppermute(summed_block, ("scene", "mp"), swap_x_zh())
 
     with jax.named_scope("head_gradients"):
-        d_attn = head_grad(jnp.stack([x, zh, zl]), upstream, w_near)
+        d_attn = head_grad(place, upstream, w_near, w_other)
         d_queries, d_keys, d_values = attend_backward(
             queries, keys, values, d_attn, probs, weights, attended, scaling
         )

time: 193 us -> 179 us (0.927)
  the two profiles are of different devices: /device:TPU:76 before, /device:TPU:4 now
where the time goes in v4:
time: 179 us; the launch traced here: 178 us
  starting transfers between devices  100 us (56%)
  waiting for transfers between devices  58.6 us (33%)
  other arithmetic  7.27 us (4%)
  local copies, waits for them, and re-layouts  4.14 us (2%)
  matrix products  4.06 us (2%)
  Pallas kernels  2.26 us (1%)
    ppermute x3, starting transfers between devices, shards(): arrived = [lax.ppermute(pieces[k], 'mp', shift_x(k)) for k in range(1, X)]  21.5 us
    ppermute x3, waiting for transfers between devices, shards(): lax.ppermute(block, 'mp', shift_x(-k))  14.5 us
    all_to_all x1, waiting for transfers between devices, shards(): lax.all_to_all(near, 'scene', 0, 0, axis_index_groups=z_hi_groups())  12.3 us
    ppermute x3, starting transfers between devices, shards(): lax.ppermute(block, 'mp', shift_x(-k))  11.9 us
    all_to_all x1, starting transfers between devices, shards(): lax.all_to_all(near, 'scene', 0, 0, axis_index_groups=z_hi_groups())  11.8 us
    ppermute x3, starting transfers between devices, shards(): lax.ppermute(attended_rounded, 'mp', shift_x(-k))  11.4 us
    ppermute x1, waiting for transfers between devices, shards(): d_wout = lax.ppermute(summed_block, ('scene', 'mp'), swap_x_zh())  10.8 us
    all_to_all x1, waiting for transfers between devices, shards(): lax.all_to_all(w_spread, 'scene', 0, 0, axis_index_groups=z_hi_groups())  10.5 us
  transfers between devices with their start and end apart: 20, of which 12 were waited for; matrix products, arithmetic and copies ran while one was open for 6% of the time, Pallas kernels for 1%

profile of v4, /device:TPU:4, one launch (start us, length us, event | category | flops | bytes accessed | tf_op | source)
XLA Modules:
  0.0 178.0 jit_solution(6755698543082853913)
XLA Ops:
  0.7 1.6 dynamic-slice_bitcast_fusion.2
  2.3 3.1 %collective-permute-start = (bf16[256,1024]{1,0:T(8,128)(2,1)S(1)}, bf16[256,1024]{1,0:T(8,128)(2,1)}, u32[]{:S(2)}, u32[]{:S(2)}) collective-permute-start(bf16[256,1024]{1,0:T(8,128)(2,1)S(1)} %get-tuple-element.40), channel_id=1, source_target_pairs={{0,4},{1,5},{2,6},{3,7},{4,8},{5,9},{6,10},{7,11},{8,12},{9,13},{1... | collective-permute-start | bytes 1572872 | tf_op jit(solution)/shard_map/sum_over_x/ppermute | solution.py:201
  5.4 13.9 %collective-permute-start.1 = (bf16[256,1024]{1,0:T(8,128)(2,1)S(1)}, bf16[256,1024]{1,0:T(8,128)(2,1)}, u32[]{:S(2)}, u32[]{:S(2)}) collective-permute-start(bf16[256,1024]{1,0:T(8,128)(2,1)S(1)} %get-tuple-element.42), channel_id=1, source_target_pairs={{0,8},{1,9},{2,10},{3,11},{4,12},{5,13},{6,14},{7,15},{8,0},{9,1},... | collective-permute-start | bytes 1572872 | tf_op jit(solution)/shard_map/sum_over_x/ppermute | solution.py:201
  19.3 4.5 %collective-permute-start.2 = (bf16[256,1024]{1,0:T(8,128)(2,1)S(1)}, bf16[256,1024]{1,0:T(8,128)(2,1)}, u32[]{:S(2)}, u32[]{:S(2)}) collective-permute-start(bf16[256,1024]{1,0:T(8,128)(2,1)S(1)} %get-tuple-element.41), channel_id=1, source_target_pairs={{0,12},{1,13},{2,14},{3,15},{4,0},{5,1},{6,2},{7,3},{8,4},{9,5},{1... | collective-permute-start | bytes 1572872 | tf_op jit(solution)/shard_map/sum_over_x/ppermute | solution.py:201
  23.8 0.7 broadcast_in_dim.51
  24.5 6.1 %all-to-all-start = ((bf16[4,128,128]{2,1,0:T(8,128)(2,1)}), bf16[4,128,128]{2,1,0:T(8,128)(2,1)S(1)}, u32[]{:S(2)}, u32[]{:S(2)}) async-start(bf16[4,128,128]{2,1,0:T(8,128)(2,1)} %broadcast_in_dim.51), calls=%async_computation | async-start | bytes 262144 | tf_op jit(solution)/shard_map/gather_projection/all_to_all | solution.py:206
  30.6 0.3 broadcast_in_dim.48
  30.9 0.4 fusion.23
  31.4 0.3 fusion.12
  32.3 1.0 collective-permute-done.2
  33.3 2.7 %fusion.10 = bf16[256,1024]{1,0:T(8,128)(2,1)} fusion(bf16[256,1024]{1,0:T(8,128)(2,1)} %collective-permute-done.2, bf16[256,1024]{1,0:T(8,128)(2,1)} %collective-permute-done.1, bf16[256,1024]{1,0:T(8,128)(2,1)} %collective-permute-done, bf16[1,1,256,4096]{3,2,1,0:T(8,128)(2,1)} %param.7, s32[]{:T(128)S(6)} %select_n.21), kind=kLoop, calls=%fused_computation.16 | loop fusion | flops 2097152 | bytes 2621444 | tf_op jit(solution)/shard_map/sum_over_x/convert_element_type | solution.py:202
  36.0 10.5 %all-to-all-done = bf16[4,128,128]{2,1,0:T(8,128)(2,1)S(1)} async-done(((bf16[4,128,128]{2,1,0:T(8,128)(2,1)}), bf16[4,128,128]{2,1,0:T(8,128)(2,1)S(1)}, u32[]{:S(2)}, u32[]{:S(2)}) %all-to-all-start) | async-done | bytes 131104 | tf_op jit(solution)/shard_map/gather_projection/all_to_all | solution.py:206
  46.5 7.1 %all-to-all-start.1 = ((bf16[8,32,1024]{2,1,0:T(8,128)(2,1)}), bf16[8,32,1024]{2,1,0:T(8,128)(2,1)S(1)}, u32[]{:S(2)}, u32[]{:S(2)}) async-start(bf16[8,32,1024]{2,1,0:T(8,128)(2,1)} %bitcast.13), calls=%async_computation.1 | async-start | bytes 1048576 | tf_op jit(solution)/shard_map/sum_over_y/all_to_all | solution.py:218
  54.3 4.1 %collective-permute-start.3 = (bf16[256,128]{1,0:T(8,128)(2,1)S(1)}, bf16[256,128]{1,0:T(8,128)(2,1)S(1)}, u32[]{:S(2)}, u32[]{:S(2)}) collective-permute-start(bf16[256,128]{1,0:T(8,128)(2,1)S(1)} %get-tuple-element.28.refs_0_), channel_id=1, source_target_pairs={{0,12},{1,13},{2,14},{3,15},{4,0},{5,1},{6,2},{7,3},{8,4},{9,5},{1... | collective-permute-start | bytes 196616 | tf_op jit(solution)/shard_map/gather_attended/ppermute | solution.py:226
  58.4 2.8 %collective-permute-start.4 = (bf16[256,128]{1,0:T(8,128)(2,1)S(1)}, bf16[256,128]{1,0:T(8,128)(2,1)S(1)}, u32[]{:S(2)}, u32[]{:S(2)}) collective-permute-start(bf16[256,128]{1,0:T(8,128)(2,1)S(1)} %get-tuple-element.28.refs_0_), channel_id=1, source_target_pairs={{0,8},{1,9},{2,10},{3,11},{4,12},{5,13},{6,14},{7,15},{8,0},{9,1},... | collective-permute-start | bytes 196616 | tf_op jit(solution)/shard_map/gather_attended/ppermute | solution.py:226
  61.2 4.5 %collective-permute-start.5 = (bf16[256,128]{1,0:T(8,128)(2,1)S(1)}, bf16[256,128]{1,0:T(8,128)(2,1)S(1)}, u32[]{:S(2)}, u32[]{:S(2)}) collective-permute-start(bf16[256,128]{1,0:T(8,128)(2,1)S(1)} %get-tuple-element.28.refs_0_), channel_id=1, source_target_pairs={{0,4},{1,5},{2,6},{3,7},{4,8},{5,9},{6,10},{7,11},{8,12},{9,13},{1... | collective-permute-start | bytes 196616 | tf_op jit(solution)/shard_map/gather_attended/ppermute | solution.py:226
  65.7 1.6 all-to-all-done.1
  67.6 0.9 broadcast_in_dim.53
  68.5 7.2 %all-to-all-start.2 = ((bf16[8,32,1024]{2,1,0:T(8,128)(2,1)}), bf16[8,32,1024]{2,1,0:T(8,128)(2,1)S(1)}, u32[]{:S(2)}, u32[]{:S(2)}) async-start(bf16[8,32,1024]{2,1,0:T(8,128)(2,1)} %broadcast_in_dim.53), calls=%async_computation.2 | async-start | bytes 1048576 | tf_op jit(solution)/shard_map/gather_over_y/all_to_all | solution.py:232
  75.7 3.3 %collective-permute-start.6 = (bf16[4,128,128]{2,1,0:T(8,128)(2,1)S(1)}, bf16[4,128,128]{2,1,0:T(8,128)(2,1)S(1)}, u32[]{:S(2)}, u32[]{:S(2)}) collective-permute-start(bf16[4,128,128]{2,1,0:T(8,128)(2,1)S(1)} %all-to-all-done), channel_id=1, source_target_pairs={{0,96},{16,112},{32,0},{48,16},{64,32},{80,48},{96,64},{112,80},{1... | collective-permute-start | bytes 393224 | tf_op jit(solution)/shard_map/gather_projection/ppermute | solution.py:236
  78.9 2.5 %collective-permute-start.7 = (bf16[4,128,128]{2,1,0:T(8,128)(2,1)S(1)}, bf16[4,128,128]{2,1,0:T(8,128)(2,1)S(1)}, u32[]{:S(2)}, u32[]{:S(2)}) collective-permute-start(bf16[4,128,128]{2,1,0:T(8,128)(2,1)S(1)} %all-to-all-done), channel_id=1, source_target_pairs={{0,64},{16,80},{32,96},{48,112},{64,0},{80,16},{96,32},{112,48},{1... | collective-permute-start | bytes 393224 | tf_op jit(solution)/shard_map/gather_projection/ppermute | solution.py:236
  81.4 3.9 %collective-permute-start.8 = (bf16[4,128,128]{2,1,0:T(8,128)(2,1)S(1)}, bf16[4,128,128]{2,1,0:T(8,128)(2,1)S(1)}, u32[]{:S(2)}, u32[]{:S(2)}) collective-permute-start(bf16[4,128,128]{2,1,0:T(8,128)(2,1)S(1)} %all-to-all-done), channel_id=1, source_target_pairs={{0,32},{16,48},{32,64},{48,80},{64,96},{80,112},{96,0},{112,16},{1... | collective-permute-start | bytes 393224 | tf_op jit(solution)/shard_map/gather_projection/ppermute | solution.py:236
  85.4 2.7 %collective-permute-done.7 = bf16[4,128,128]{2,1,0:T(8,128)(2,1)S(1)} collective-permute-done((bf16[4,128,128]{2,1,0:T(8,128)(2,1)S(1)}, bf16[4,128,128]{2,1,0:T(8,128)(2,1)S(1)}, u32[]{:S(2)}, u32[]{:S(2)}) %collective-permute-start.7) | collective-permute-done | bytes 131104 | tf_op jit(solution)/shard_map/gather_projection/ppermute | solution.py:236
  88.1 2.0 %collective-permute-done.8 = bf16[4,128,128]{2,1,0:T(8,128)(2,1)S(1)} collective-permute-done((bf16[4,128,128]{2,1,0:T(8,128)(2,1)S(1)}, bf16[4,128,128]{2,1,0:T(8,128)(2,1)S(1)}, u32[]{:S(2)}, u32[]{:S(2)}) %collective-permute-start.8) | collective-permute-done | bytes 131104 | tf_op jit(solution)/shard_map/gather_projection/ppermute | solution.py:236
  90.1 1.0 weight_terms.1
  91.2 1.9 %collective-permute-start.9 = (bf16[4,4,128,128]{3,2,1,0:T(8,128)(2,1)S(1)}, bf16[4,4,128,128]{3,2,1,0:T(8,128)(2,1)S(1)}, u32[]{:S(2)}, u32[]{:S(2)}) collective-permute-start(bf16[4,4,128,128]{3,2,1,0:T(8,128)(2,1)S(1)} %get-tuple-element.33), channel_id=1, source_target_pairs={{0,16},{16,0},{32,48},{48,32},{64,80},{80,64},{96,112},{112,96},{1... | collective-permute-start | bytes 1572872 | tf_op jit(solution)/shard_map/sum_over_core/ppermute | solution.py:244
  93.1 1.9 %collective-permute-done.9 = bf16[4,4,128,128]{3,2,1,0:T(8,128)(2,1)S(1)} collective-permute-done((bf16[4,4,128,128]{3,2,1,0:T(8,128)(2,1)S(1)}, bf16[4,4,128,128]{3,2,1,0:T(8,128)(2,1)S(1)}, u32[]{:S(2)}, u32[]{:S(2)}) %collective-permute-start.9) | collective-permute-done | bytes 524320 | tf_op jit(solution)/shard_map/sum_over_core/ppermute | solution.py:244
  95.0 0.9 add_convert_fusion
  95.9 4.1 %all-to-all-start.3 = ((bf16[4,4,128,128]{3,2,1,0:T(8,128)(2,1)}), bf16[4,4,128,128]{3,2,1,0:T(8,128)(2,1)}, u32[]{:S(2)}, u32[]{:S(2)}) async-start(bf16[4,4,128,128]{3,2,1,0:T(8,128)(2,1)} %add_convert_fusion), calls=%async_computation.3 | async-start | bytes 1048576 | tf_op jit(solution)/shard_map/sum_over_z_lo/all_to_all | solution.py:254
  100.0 2.8 %collective-permute-start.10 = (bf16[256,1024]{1,0:T(8,128)(2,1)S(1)}, bf16[256,1024]{1,0:T(8,128)(2,1)S(1)}, u32[]{:S(2)}, u32[]{:S(2)}) collective-permute-start(bf16[256,1024]{1,0:T(8,128)(2,1)S(1)} %bitcast.62), channel_id=1, source_target_pairs={{0,12},{1,13},{2,14},{3,15},{4,0},{5,1},{6,2},{7,3},{8,4},{9,5},{1... | collective-permute-start | bytes 1572872 | tf_op jit(solution)/shard_map/gather_over_x/ppermute | solution.py:250
  102.9 5.4 %collective-permute-start.11 = (bf16[256,1024]{1,0:T(8,128)(2,1)S(1)}, bf16[256,1024]{1,0:T(8,128)(2,1)S(1)}, u32[]{:S(2)}, u32[]{:S(2)}) collective-permute-start(bf16[256,1024]{1,0:T(8,128)(2,1)S(1)} %bitcast.63), channel_id=1, source_target_pairs={{0,8},{1,9},{2,10},{3,11},{4,12},{5,13},{6,14},{7,15},{8,0},{9,1},... | collective-permute-start | bytes 1572872 | tf_op jit(solution)/shard_map/gather_over_x/ppermute | solution.py:250
  108.3 3.7 %collective-permute-start.12 = (bf16[256,1024]{1,0:T(8,128)(2,1)S(1)}, bf16[256,1024]{1,0:T(8,128)(2,1)S(1)}, u32[]{:S(2)}, u32[]{:S(2)}) collective-permute-start(bf16[256,1024]{1,0:T(8,128)(2,1)S(1)} %bitcast.64), channel_id=1, source_target_pairs={{0,4},{1,5},{2,6},{3,7},{4,8},{5,9},{6,10},{7,11},{8,12},{9,13},{1... | collective-permute-start | bytes 1572872 | tf_op jit(solution)/shard_map/gather_over_x/ppermute | solution.py:250
  112.0 1.9 %collective-permute-start.13 = (bf16[4,4,128,128]{3,2,1,0:T(8,128)(2,1)S(1)}, bf16[4,4,128,128]{3,2,1,0:T(8,128)(2,1)S(1)}, u32[]{:S(2)}, u32[]{:S(2)}) collective-permute-start(bf16[4,4,128,128]{3,2,1,0:T(8,128)(2,1)S(1)} %pad_maximum_fusion.w_own_ref), channel_id=1, source_target_pairs={{0,16},{16,0},{32,48},{48,32},{64,80},{80,64},{96,112},{112,96},{1... | collective-permute-start | bytes 1572872 | tf_op jit(solution)/shard_map/gather_projection/ppermute | solution.py:247
  113.9 1.2 all-to-all-done.3
  115.2 1.8 %fusion.20 = bf16[4,128,128]{2,1,0:T(8,128)(2,1)} fusion(bf16[4,4,128,128]{3,2,1,0:T(8,128)(2,1)} %all-to-all-done.3), kind=kLoop, calls=%fused_computation.34 | loop fusion | flops 524288 | bytes 655360 | tf_op jit(solution)/shard_map/sum_over_z_lo/add | solution.py:181
  117.0 4.1 %collective-permute-done.11.refs_2_ = bf16[256,1024]{1,0:T(8,128)(2,1)S(1)} collective-permute-done((bf16[256,1024]{1,0:T(8,128)(2,1)S(1)}, bf16[256,1024]{1,0:T(8,128)(2,1)S(1)}, u32[]{:S(2)}, u32[]{:S(2)}) %collective-permute-start.11) | collective-permute-done | bytes 524320 | tf_op jit(solution)/shard_map/gather_over_x/ppermute | solution.py:250
  121.1 10.4 %collective-permute-done.12.refs_3_ = bf16[256,1024]{1,0:T(8,128)(2,1)S(1)} collective-permute-done((bf16[256,1024]{1,0:T(8,128)(2,1)S(1)}, bf16[256,1024]{1,0:T(8,128)(2,1)S(1)}, u32[]{:S(2)}, u32[]{:S(2)}) %collective-permute-start.12) | collective-permute-done | bytes 524320 | tf_op jit(solution)/shard_map/gather_over_x/ppermute | solution.py:250
  131.4 11.8 %all-to-all-start.4 = ((bf16[4,128,128]{2,1,0:T(8,128)(2,1)}), bf16[4,128,128]{2,1,0:T(8,128)(2,1)}, u32[]{:S(2)}, u32[]{:S(2)}) async-start(bf16[4,128,128]{2,1,0:T(8,128)(2,1)} %fusion.20), calls=%async_computation.4 | async-start | bytes 262144 | tf_op jit(solution)/shard_map/sum_over_z_hi/all_to_all | solution.py:260
  143.2 1.3 head_grad.1
  144.6 0.3 fusion.2
  144.9 0.9 fusion.7
  145.9 1.1 fusion.5
  146.9 12.3 %all-to-all-done.4 = bf16[4,128,128]{2,1,0:T(8,128)(2,1)} async-done(((bf16[4,128,128]{2,1,0:T(8,128)(2,1)}), bf16[4,128,128]{2,1,0:T(8,128)(2,1)}, u32[]{:S(2)}, u32[]{:S(2)}) %all-to-all-start.4) | async-done | bytes 131104 | tf_op jit(solution)/shard_map/sum_over_z_hi/all_to_all | solution.py:260
  159.2 0.8 add_bitcast_fusion
  160.1 5.4 %collective-permute-start.14 = (f32[128,128]{1,0:T(8,128)S(1)}, f32[128,128]{1,0:T(8,128)S(1)}, u32[]{:S(2)}, u32[]{:S(2)}) collective-permute-start(f32[128,128]{1,0:T(8,128)S(1)} %add_bitcast_fusion), channel_id=1, source_target_pairs={{0,0},{1,1},{2,2},{3,3},{4,128},{5,129},{6,130},{7,131},{8,256},{9... | collective-permute-start | bytes 196616 | tf_op jit(solution)/shard_map/sum_over_z_hi/ppermute | solution.py:262
  165.5 1.1 fusion.4
  166.6 10.8 %collective-permute-done.14 = f32[128,128]{1,0:T(8,128)S(1)} collective-permute-done((f32[128,128]{1,0:T(8,128)S(1)}, f32[128,128]{1,0:T(8,128)S(1)}, u32[]{:S(2)}, u32[]{:S(2)}) %collective-permute-start.14) | collective-permute-done | bytes 65568 | tf_op jit(solution)/shard_map/sum_over_z_hi/ppermute | solution.py:262
  177.3 0.6 copy.18
  (37 shorter events, 1.1 us)
Async XLA Ops:
  0.6 31.4 %copy-start = (bf16[1,1024,128]{2,1,0:T(8,128)(2,1)S(1)}, bf16[1,1024,128]{2,1,0:T(8,128)(2,1)}, u32[]{:S(2)}) copy-start(bf16[1,1024,128]{2,1,0:T(8,128)(2,1)} %param.10) | copy-start | bytes 786436
  0.6 23.2 %copy-start.7 = (bf16[128,128]{1,0:T(8,128)(2,1)S(1)}, bf16[128,128]{1,0:T(8,128)(2,1)}, u32[]{:S(2)}) copy-start(bf16[128,128]{1,0:T(8,128)(2,1)} %param.11) | copy-start | bytes 98308
  0.7 29.9 %copy-start.8 = (s32[1,2,8]{2,1,0:T(2,128)S(1)}, s32[1,2,8]{2,1,0:T(2,128)}, u32[]{:S(2)}) copy-start(s32[1,2,8]{2,1,0:T(2,128)} %param.12) | copy-start | bytes 196
  0.7 30.3 %copy-start.5 = (bf16[1,256,128]{2,1,0:T(8,128)(2,1)S(1)}, bf16[1,256,128]{2,1,0:T(8,128)(2,1)}, u32[]{:S(2)}) copy-start(bf16[1,256,128]{2,1,0:T(8,128)(2,1)} %param.8) | copy-start | bytes 196612
  0.7 30.3 %copy-start.3 = (bf16[1,1024,128]{2,1,0:T(8,128)(2,1)S(1)}, bf16[1,1024,128]{2,1,0:T(8,128)(2,1)}, u32[]{:S(2)}) copy-start(bf16[1,1024,128]{2,1,0:T(8,128)(2,1)} %param.9) | copy-start | bytes 786436
  2.3 30.0 %collective-permute-start = (bf16[256,1024]{1,0:T(8,128)(2,1)S(1)}, bf16[256,1024]{1,0:T(8,128)(2,1)}, u32[]{:S(2)}, u32[]{:S(2)}) collective-permute-start(bf16[256,1024]{1,0:T(8,128)(2,1)S(1)} %get-tuple-element.40), channel_id=1, source_target_pairs={{0,4},{1,5},{2,6},{3,7},{4,8},{5,9},{6,10},{7,11},{8,12},{9,13},{1... | collective-permute-start | bytes 1572872 | tf_op jit(solution)/shard_map/sum_over_x/ppermute | solution.py:201
  5.4 26.9 %collective-permute-start.1 = (bf16[256,1024]{1,0:T(8,128)(2,1)S(1)}, bf16[256,1024]{1,0:T(8,128)(2,1)}, u32[]{:S(2)}, u32[]{:S(2)}) collective-permute-start(bf16[256,1024]{1,0:T(8,128)(2,1)S(1)} %get-tuple-element.42), channel_id=1, source_target_pairs={{0,8},{1,9},{2,10},{3,11},{4,12},{5,13},{6,14},{7,15},{8,0},{9,1},... | collective-permute-start | bytes 1572872 | tf_op jit(solution)/shard_map/sum_over_x/ppermute | solution.py:201
  19.3 14.0 %collective-permute-start.2 = (bf16[256,1024]{1,0:T(8,128)(2,1)S(1)}, bf16[256,1024]{1,0:T(8,128)(2,1)}, u32[]{:S(2)}, u32[]{:S(2)}) collective-permute-start(bf16[256,1024]{1,0:T(8,128)(2,1)S(1)} %get-tuple-element.41), channel_id=1, source_target_pairs={{0,12},{1,13},{2,14},{3,15},{4,0},{5,1},{6,2},{7,3},{8,4},{9,5},{1... | collective-permute-start | bytes 1572872 | tf_op jit(solution)/shard_map/sum_over_x/ppermute | solution.py:201
  24.5 22.0 %all-to-all-start = ((bf16[4,128,128]{2,1,0:T(8,128)(2,1)}), bf16[4,128,128]{2,1,0:T(8,128)(2,1)S(1)}, u32[]{:S(2)}, u32[]{:S(2)}) async-start(bf16[4,128,128]{2,1,0:T(8,128)(2,1)} %broadcast_in_dim.51), calls=%async_computation | async-start | bytes 262144 | tf_op jit(solution)/shard_map/gather_projection/all_to_all | solution.py:206
  32.0 14.5 %copy-start.1 = (f32[256,1024]{1,0:T(8,128)}, f32[256,1024]{1,0:T(8,128)S(1)}, u32[]{:S(2)}) copy-start(f32[256,1024]{1,0:T(8,128)S(1)} %fusion.11) | copy-start | bytes 3145732
  46.5 20.8 %all-to-all-start.1 = ((bf16[8,32,1024]{2,1,0:T(8,128)(2,1)}), bf16[8,32,1024]{2,1,0:T(8,128)(2,1)S(1)}, u32[]{:S(2)}, u32[]{:S(2)}) async-start(bf16[8,32,1024]{2,1,0:T(8,128)(2,1)} %bitcast.13), calls=%async_computation.1 | async-start | bytes 1048576 | tf_op jit(solution)/shard_map/sum_over_y/all_to_all | solution.py:218
  54.3 13.2 %collective-permute-start.3 = (bf16[256,128]{1,0:T(8,128)(2,1)S(1)}, bf16[256,128]{1,0:T(8,128)(2,1)S(1)}, u32[]{:S(2)}, u32[]{:S(2)}) collective-permute-start(bf16[256,128]{1,0:T(8,128)(2,1)S(1)} %get-tuple-element.28.refs_0_), channel_id=1, source_target_pairs={{0,12},{1,13},{2,14},{3,15},{4,0},{5,1},{6,2},{7,3},{8,4},{9,5},{1... | collective-permute-start | bytes 196616 | tf_op jit(solution)/shard_map/gather_attended/ppermute | solution.py:226
  58.4 9.1 %collective-permute-start.4 = (bf16[256,128]{1,0:T(8,128)(2,1)S(1)}, bf16[256,128]{1,0:T(8,128)(2,1)S(1)}, u32[]{:S(2)}, u32[]{:S(2)}) collective-permute-start(bf16[256,128]{1,0:T(8,128)(2,1)S(1)} %get-tuple-element.28.refs_0_), channel_id=1, source_target_pairs={{0,8},{1,9},{2,10},{3,11},{4,12},{5,13},{6,14},{7,15},{8,0},{9,1},... | collective-permute-start | bytes 196616 | tf_op jit(solution)/shard_map/gather_attended/ppermute | solution.py:226
  61.2 6.4 %collective-permute-start.5 = (bf16[256,128]{1,0:T(8,128)(2,1)S(1)}, bf16[256,128]{1,0:T(8,128)(2,1)S(1)}, u32[]{:S(2)}, u32[]{:S(2)}) collective-permute-start(bf16[256,128]{1,0:T(8,128)(2,1)S(1)} %get-tuple-element.28.refs_0_), channel_id=1, source_target_pairs={{0,4},{1,5},{2,6},{3,7},{4,8},{5,9},{6,10},{7,11},{8,12},{9,13},{1... | collective-permute-start | bytes 196616 | tf_op jit(solution)/shard_map/gather_attended/ppermute | solution.py:226
  68.5 21.7 %all-to-all-start.2 = ((bf16[8,32,1024]{2,1,0:T(8,128)(2,1)}), bf16[8,32,1024]{2,1,0:T(8,128)(2,1)S(1)}, u32[]{:S(2)}, u32[]{:S(2)}) async-start(bf16[8,32,1024]{2,1,0:T(8,128)(2,1)} %broadcast_in_dim.53), calls=%async_computation.2 | async-start | bytes 1048576 | tf_op jit(solution)/shard_map/gather_over_y/all_to_all | solution.py:232
  75.7 9.8 %collective-permute-start.6 = (bf16[4,128,128]{2,1,0:T(8,128)(2,1)S(1)}, bf16[4,128,128]{2,1,0:T(8,128)(2,1)S(1)}, u32[]{:S(2)}, u32[]{:S(2)}) collective-permute-start(bf16[4,128,128]{2,1,0:T(8,128)(2,1)S(1)} %all-to-all-done), channel_id=1, source_target_pairs={{0,96},{16,112},{32,0},{48,16},{64,32},{80,48},{96,64},{112,80},{1... | collective-permute-start | bytes 393224 | tf_op jit(solution)/shard_map/gather_projection/ppermute | solution.py:236
  78.9 9.2 %collective-permute-start.7 = (bf16[4,128,128]{2,1,0:T(8,128)(2,1)S(1)}, bf16[4,128,128]{2,1,0:T(8,128)(2,1)S(1)}, u32[]{:S(2)}, u32[]{:S(2)}) collective-permute-start(bf16[4,128,128]{2,1,0:T(8,128)(2,1)S(1)} %all-to-all-done), channel_id=1, source_target_pairs={{0,64},{16,80},{32,96},{48,112},{64,0},{80,16},{96,32},{112,48},{1... | collective-permute-start | bytes 393224 | tf_op jit(solution)/shard_map/gather_projection/ppermute | solution.py:236
  81.4 8.7 %collective-permute-start.8 = (bf16[4,128,128]{2,1,0:T(8,128)(2,1)S(1)}, bf16[4,128,128]{2,1,0:T(8,128)(2,1)S(1)}, u32[]{:S(2)}, u32[]{:S(2)}) collective-permute-start(bf16[4,128,128]{2,1,0:T(8,128)(2,1)S(1)} %all-to-all-done), channel_id=1, source_target_pairs={{0,32},{16,48},{32,64},{48,80},{64,96},{80,112},{96,0},{112,16},{1... | collective-permute-start | bytes 393224 | tf_op jit(solution)/shard_map/gather_projection/ppermute | solution.py:236
  91.2 3.8 %collective-permute-start.9 = (bf16[4,4,128,128]{3,2,1,0:T(8,128)(2,1)S(1)}, bf16[4,4,128,128]{3,2,1,0:T(8,128)(2,1)S(1)}, u32[]{:S(2)}, u32[]{:S(2)}) collective-permute-start(bf16[4,4,128,128]{3,2,1,0:T(8,128)(2,1)S(1)} %get-tuple-element.33), channel_id=1, source_target_pairs={{0,16},{16,0},{32,48},{48,32},{64,80},{80,64},{96,112},{112,96},{1... | collective-permute-start | bytes 1572872 | tf_op jit(solution)/shard_map/sum_over_core/ppermute | solution.py:244
  95.9 19.3 %all-to-all-start.3 = ((bf16[4,4,128,128]{3,2,1,0:T(8,128)(2,1)}), bf16[4,4,128,128]{3,2,1,0:T(8,128)(2,1)}, u32[]{:S(2)}, u32[]{:S(2)}) async-start(bf16[4,4,128,128]{3,2,1,0:T(8,128)(2,1)} %add_convert_fusion), calls=%async_computation.3 | async-start | bytes 1048576 | tf_op jit(solution)/shard_map/sum_over_z_lo/all_to_all | solution.py:254
  100.0 17.0 %collective-permute-start.10 = (bf16[256,1024]{1,0:T(8,128)(2,1)S(1)}, bf16[256,1024]{1,0:T(8,128)(2,1)S(1)}, u32[]{:S(2)}, u32[]{:S(2)}) collective-permute-start(bf16[256,1024]{1,0:T(8,128)(2,1)S(1)} %bitcast.62), channel_id=1, source_target_pairs={{0,12},{1,13},{2,14},{3,15},{4,0},{5,1},{6,2},{7,3},{8,4},{9,5},{1... | collective-permute-start | bytes 1572872 | tf_op jit(solution)/shard_map/gather_over_x/ppermute | solution.py:250
  102.9 18.2 %collective-permute-start.11 = (bf16[256,1024]{1,0:T(8,128)(2,1)S(1)}, bf16[256,1024]{1,0:T(8,128)(2,1)S(1)}, u32[]{:S(2)}, u32[]{:S(2)}) collective-permute-start(bf16[256,1024]{1,0:T(8,128)(2,1)S(1)} %bitcast.63), channel_id=1, source_target_pairs={{0,8},{1,9},{2,10},{3,11},{4,12},{5,13},{6,14},{7,15},{8,0},{9,1},... | collective-permute-start | bytes 1572872 | tf_op jit(solution)/shard_map/gather_over_x/ppermute | solution.py:250
  108.3 23.2 %collective-permute-start.12 = (bf16[256,1024]{1,0:T(8,128)(2,1)S(1)}, bf16[256,1024]{1,0:T(8,128)(2,1)S(1)}, u32[]{:S(2)}, u32[]{:S(2)}) collective-permute-start(bf16[256,1024]{1,0:T(8,128)(2,1)S(1)} %bitcast.64), channel_id=1, source_target_pairs={{0,4},{1,5},{2,6},{3,7},{4,8},{5,9},{6,10},{7,11},{8,12},{9,13},{1... | collective-permute-start | bytes 1572872 | tf_op jit(solution)/shard_map/gather_over_x/ppermute | solution.py:250
  112.0 19.5 %collective-permute-start.13 = (bf16[4,4,128,128]{3,2,1,0:T(8,128)(2,1)S(1)}, bf16[4,4,128,128]{3,2,1,0:T(8,128)(2,1)S(1)}, u32[]{:S(2)}, u32[]{:S(2)}) collective-permute-start(bf16[4,4,128,128]{3,2,1,0:T(8,128)(2,1)S(1)} %pad_maximum_fusion.w_own_ref), channel_id=1, source_target_pairs={{0,16},{16,0},{32,48},{48,32},{64,80},{80,64},{96,112},{112,96},{1... | collective-permute-start | bytes 1572872 | tf_op jit(solution)/shard_map/gather_projection/ppermute | solution.py:247
  131.4 27.8 %all-to-all-start.4 = ((bf16[4,128,128]{2,1,0:T(8,128)(2,1)}), bf16[4,128,128]{2,1,0:T(8,128)(2,1)}, u32[]{:S(2)}, u32[]{:S(2)}) async-start(bf16[4,128,128]{2,1,0:T(8,128)(2,1)} %fusion.20), calls=%async_computation.4 | async-start | bytes 262144 | tf_op jit(solution)/shard_map/sum_over_z_hi/all_to_all | solution.py:260
  143.2 1.4 copy-start.2
  143.2 1.7 copy-start.4
  144.6 20.9 %copy-start.6 = (bf16[1,256,128]{2,1,0:T(8,128)(2,1)S(1)}, bf16[1,256,128]{2,1,0:T(8,128)(2,1)}, u32[]{:S(2)}) copy-start(bf16[1,256,128]{2,1,0:T(8,128)(2,1)} %param.8) | copy-start | bytes 196612
  160.1 17.3 %collective-permute-start.14 = (f32[128,128]{1,0:T(8,128)S(1)}, f32[128,128]{1,0:T(8,128)S(1)}, u32[]{:S(2)}, u32[]{:S(2)}) collective-permute-start(f32[128,128]{1,0:T(8,128)S(1)} %add_bitcast_fusion), channel_id=1, source_target_pairs={{0,0},{1,1},{2,2},{3,3},{4,128},{5,129},{6,130},{7,131},{8,256},{9... | collective-permute-start | bytes 196616 | tf_op jit(solution)/shard_map/sum_over_z_hi/ppermute | solution.py:262

commit v5 on v4

--- a/solution.py
+++ b/solution.py
@@ -28,6 +28,15 @@
 def shift_zl(k):
     return [
         (scene_index(a, b, c), scene_index(a, (b + k) % ZL, c))
+        for a in range(ZH)
+        for b in range(ZL)
+        for c in range(CORES)
+    ]
+
+
+def shift_zh(k):
+    return [
+        (scene_index(a, b, c), scene_index((a + k) % ZH, b, c))
         for a in range(ZH)
         for b in range(ZL)
         for c in range(CORES)
@@ -91,6 +100,34 @@
     return [g.astype(jnp.bfloat16) for g in (d_queries, d_keys, d_values)]
 
 
+def add_own_kernel(x_ref, own_ref, *refs):
+    *part_refs, out_ref = refs
+    total = own_ref[...].astype(jnp.float32)
+    for part_ref in part_refs:
+        total += part_ref[...].astype(jnp.float32)
+    out_ref[...] = total.astype(out_ref.dtype)
+
+
+def add_own(x, sample, arrived):
+    rows, width = arrived[0].shape
+    whole = pl.BlockSpec((rows, width), lambda i, x: (0, 0))
+    return pl.pallas_call(
+        add_own_kernel,
+        out_shape=jax.ShapeDtypeStruct((rows, width), jnp.bfloat16),
+        grid_spec=pltpu.PrefetchScalarGridSpec(
+            num_scalar_prefetch=1,
+            grid=(1,),
+            in_specs=[pl.BlockSpec((rows, width), lambda i, x: (0, x[0]))] + [whole] * (X - 1),
+            out_specs=whole,
+        ),
+        compiler_params=pltpu.CompilerParams(vmem_limit_bytes=16 << 20),
+        cost_estimate=pl.CostEstimate(
+            flops=rows * width * X, bytes_accessed=2 * rows * width * (X + 1), transcendentals=0
+        ),
+        name="add_own",
+    )(x.reshape(1), sample, *arrived)
+
+
 def weight_terms_kernel(place_ref, block_ref, *refs):
     attended, (send_ref, keep_ref) = refs[:X], refs[X:]
     first = place_ref[0] == 0
@@ -134,10 +171,10 @@
 
 def head_grad_kernel(place_ref, w_own_ref, w_other_ref, *refs):
     *blocks, out_ref = refs
-    core, x, zl = [place_ref[i] for i in range(3)]
+    core, x, zl, zh = [place_ref[i] for i in range(4)]
     total = jnp.zeros(out_ref.shape, jnp.float32)
     for k in range(X):
-        far = (x + k) & (X - 1)
+        far = (x + k - zh) & (ZH - 1)
         for b in range(ZL):
             near = (b - zl) & (ZL - 1)
             left = b * CORES * HEAD_DIM
@@ -186,9 +223,9 @@
     scaling = 1.0 / math.sqrt(HEAD_DIM)
     section, mp, scene = (lax.axis_index(name) for name in ("section", "mp", "scene"))
     x, y = shift_right(mp, YH), (mp & (YH - 1)) * YL + section
-    zl = shift_right(scene, CORES) & (ZL - 1)
+    zh, zl = shift_right(scene, ZL * CORES), shift_right(scene, CORES) & (ZL - 1)
     core = scene & (CORES - 1)
-    place = jnp.stack([core, x, zl])
+    place = jnp.stack([core, x, zl, zh])
     sample = dec_grad[0, 0]
     tokens, model = sample.shape
     width = model // X
@@ -196,14 +233,13 @@
     with jax.named_scope("sum_over_x"):
         pieces = [
             lax.dynamic_slice(sample, (0, ((x + k) & (X - 1)) * width), (tokens, width))
-            for k in range(X)
+            for k in range(1, X)
         ]
-        arrived = [lax.ppermute(pieces[k], "mp", shift_x(k)) for k in range(1, X)]
-        partial = sum_f32([pieces[0]] + arrived).astype(jnp.bfloat16)
+        arrived = [lax.ppermute(piece, "mp", shift_x(k + 1)) for k, piece in enumerate(pieces)]
+        partial = add_own(x, sample, arrived)
 
     with jax.named_scope("gather_projection"):
-        w_spread = jnp.broadcast_to(w_out[None], (ZH, *w_out.shape))
-        w_far = lax.all_to_all(w_spread, "scene", 0, 0, axis_index_groups=z_hi_groups())
+        w_rows = [w_out] + [lax.ppermute(w_out, "scene", shift_zh(-k)) for k in range(1, ZH)]
 
     queries, keys, values = agent_queries[0], map_keys[0], map_values[0]
     mask_rows = block_mask[0]
@@ -212,7 +248,9 @@
     probs, weights, attended = attend_forward(queries, keys, values, visible, scaling)
     attended_rounded = attended.astype(jnp.bfloat16)
 
-    partial, w_far, attended_rounded = lax.optimization_barrier((partial, w_far, attended_rounded))
+    partial, w_rows[1], attended_rounded = lax.optimization_barrier(
+        (partial, w_rows[1], attended_rounded)
+    )
     with jax.named_scope("sum_over_y"):
         rows = tokens // (YH * YL)
         lines = lax.all_to_all(
@@ -226,7 +264,8 @@
             lax.ppermute(attended_rounded, "mp", shift_x(-k)) for k in range(1, X)
         ]
 
-    own, attended_near = lax.optimization_barrier((own, attended_near))
+    own, attended_near, w_rows = lax.optimization_barrier((own, attended_near, w_rows))
+    w_far = jnp.stack(w_rows)
     with jax.named_scope("gather_over_y"):
         spread = jnp.broadcast_to(own[None], (YH * YL, rows, width))
         block = lax.all_to_all(spread, XY, 0, 0, axis_index_groups=y_groups())
@@ -254,7 +293,6 @@
             lax.all_to_all(pair, "scene", 0, 0, axis_index_groups=z_lo_groups())
         ).astype(jnp.bfloat16)
 
-    near, upstream, w_other = lax.optimization_barrier((near, upstream, w_other))
     with jax.named_scope("sum_over_z_hi"):
         summed_block = sum_f32(
             lax.all_to_all(near, "scene", 0, 0, axis_index_groups=z_hi_groups())
@@ -262,6 +300,7 @@
         d_wout = lax.ppermute(summed_block, ("scene", "mp"), swap_x_zh())
 
     with jax.named_scope("head_gradients"):
+        upstream, w_other, _ = lax.optimization_barrier((upstream, w_other, near))
         d_attn = head_grad(place, upstream, w_near, w_other)
         d_queries, d_keys, d_values = attend_backward(
             queries, keys, values, d_attn, probs, weights, attended, scaling

time: 179 us -> 172 us (0.961)
  the two profiles are of different devices: /device:TPU:4 before, /device:TPU:12 now
where the time goes in v5:
time: 172 us; the launch traced here: 171 us
  starting transfers between devices  113 us (66%)
  waiting for transfers between devices  40.1 us (23%)
  other arithmetic  4.62 us (3%)
  matrix products  4.08 us (2%)
  local copies, waits for them, and re-layouts  3.46 us (2%)
  Pallas kernels  3.34 us (2%)
  between operations  1.77 us (1%)
    ppermute x3, starting transfers between devices, shards(): lax.ppermute(w_out, 'scene', shift_zh(-k))  43.7 us
    ppermute x1, waiting for transfers between devices, shards(): d_wout = lax.ppermute(summed_block, ('scene', 'mp'), swap_x_zh())  12.8 us
    ppermute x3, starting transfers between devices, shards(): lax.ppermute(block, 'mp', shift_x(-k))  11.4 us
    ppermute x3, starting transfers between devices, shards(): lax.ppermute(w_far, 'scene', shift_zl(-k))  10.1 us
    ppermute x3, waiting for transfers between devices, shards(): lax.ppermute(block, 'mp', shift_x(-k))  9.67 us
    ppermute x3, starting transfers between devices, shards(): lax.ppermute(attended_rounded, 'mp', shift_x(-k))  9.22 us
    ppermute x3, starting transfers between devices, shards(): lax.ppermute(piece, 'mp', shift_x(k + 1))  8.86 us
    all_to_all x1, starting transfers between devices, shards(): lax.all_to_all(partial.reshape(YH * YL, rows, width), XY, 0, 0, axis_inde...  7.55 us
  transfers between devices with their start and end apart: 22, of which 10 were waited for; matrix products, arithmetic and copies ran while one was open for 4% of the time, Pallas kernels for 1%

profile of v5, /device:TPU:12, one launch (start us, length us, event | category | flops | bytes accessed | tf_op | source)
XLA Modules:
  0.0 170.6 jit_solution(13438017731088188502)
XLA Ops:
  0.7 1.6 dynamic-slice_bitcast_fusion
  2.3 3.1 %collective-permute-start = (bf16[256,1024]{1,0:T(8,128)(2,1)S(1)}, bf16[256,1024]{1,0:T(8,128)(2,1)S(1)}, u32[]{:S(2)}, u32[]{:S(2)}) collective-permute-start(bf16[256,1024]{1,0:T(8,128)(2,1)S(1)} %get-tuple-element.47), channel_id=1, source_target_pairs={{0,4},{1,5},{2,6},{3,7},{4,8},{5,9},{6,10},{7,11},{8,12},{9,13},{1... | collective-permute-start | bytes 1572872 | tf_op jit(solution)/shard_map/sum_over_x/ppermute | solution.py:238
  5.4 2.7 %collective-permute-start.1 = (bf16[256,1024]{1,0:T(8,128)(2,1)S(1)}, bf16[256,1024]{1,0:T(8,128)(2,1)S(1)}, u32[]{:S(2)}, u32[]{:S(2)}) collective-permute-start(bf16[256,1024]{1,0:T(8,128)(2,1)S(1)} %get-tuple-element.48), channel_id=1, source_target_pairs={{0,8},{1,9},{2,10},{3,11},{4,12},{5,13},{6,14},{7,15},{8,0},{9,1},... | collective-permute-start | bytes 1572872 | tf_op jit(solution)/shard_map/sum_over_x/ppermute | solution.py:238
  8.1 3.0 %collective-permute-start.2 = (bf16[256,1024]{1,0:T(8,128)(2,1)S(1)}, bf16[256,1024]{1,0:T(8,128)(2,1)S(1)}, u32[]{:S(2)}, u32[]{:S(2)}) collective-permute-start(bf16[256,1024]{1,0:T(8,128)(2,1)S(1)} %get-tuple-element.46), channel_id=1, source_target_pairs={{0,12},{1,13},{2,14},{3,15},{4,0},{5,1},{6,2},{7,3},{8,4},{9,5},{1... | collective-permute-start | bytes 1572872 | tf_op jit(solution)/shard_map/sum_over_x/ppermute | solution.py:238
  11.2 18.2 %collective-permute-start.3 = (bf16[128,128]{1,0:T(8,128)(2,1)S(1)}, bf16[128,128]{1,0:T(8,128)(2,1)S(1)}, u32[]{:S(2)}, u32[]{:S(2)}) collective-permute-start(bf16[128,128]{1,0:T(8,128)(2,1)S(1)} %copy-done.8), channel_id=1, source_target_pairs={{0,384},{16,400},{32,416},{48,432},{64,448},{80,464},{96,480},{112... | collective-permute-start | bytes 98312 | tf_op jit(solution)/shard_map/gather_projection/ppermute | solution.py:242
  29.4 0.3 broadcast_in_dim.42
  29.8 0.4 fusion.21
  30.2 0.3 fusion.9
  31.1 1.7 collective-permute-done.2.refs_2_
  32.8 1.1 add_own.1
  33.9 7.5 %all-to-all-start = ((bf16[8,32,1024]{2,1,0:T(8,128)(2,1)}), bf16[8,32,1024]{2,1,0:T(8,128)(2,1)S(1)}, u32[]{:S(2)}, u32[]{:S(2)}) async-start(bf16[8,32,1024]{2,1,0:T(8,128)(2,1)} %bitcast.14), calls=%async_computation | async-start | bytes 1048576 | tf_op jit(solution)/shard_map/sum_over_y/all_to_all | solution.py:256
  41.4 19.3 %collective-permute-start.7 = (bf16[128,128]{1,0:T(8,128)(2,1)S(1)}, bf16[128,128]{1,0:T(8,128)(2,1)S(1)}, u32[]{:S(2)}, u32[]{:S(2)}) collective-permute-start(bf16[128,128]{1,0:T(8,128)(2,1)S(1)} %copy-done.8), channel_id=1, source_target_pairs={{0,256},{16,272},{32,288},{48,304},{64,320},{80,336},{96,352},{112... | collective-permute-start | bytes 98312 | tf_op jit(solution)/shard_map/gather_projection/ppermute | solution.py:242
  60.8 6.1 %collective-permute-start.8 = (bf16[128,128]{1,0:T(8,128)(2,1)S(1)}, bf16[128,128]{1,0:T(8,128)(2,1)S(1)}, u32[]{:S(2)}, u32[]{:S(2)}) collective-permute-start(bf16[128,128]{1,0:T(8,128)(2,1)S(1)} %copy-done.8), channel_id=1, source_target_pairs={{0,128},{16,144},{32,160},{48,176},{64,192},{80,208},{96,224},{112... | collective-permute-start | bytes 98312 | tf_op jit(solution)/shard_map/gather_projection/ppermute | solution.py:242
  67.6 3.3 %collective-permute-start.4 = (bf16[256,128]{1,0:T(8,128)(2,1)S(1)}, bf16[256,128]{1,0:T(8,128)(2,1)S(1)}, u32[]{:S(2)}, u32[]{:S(2)}) collective-permute-start(bf16[256,128]{1,0:T(8,128)(2,1)S(1)} %get-tuple-element.35.refs_0_), channel_id=1, source_target_pairs={{0,12},{1,13},{2,14},{3,15},{4,0},{5,1},{6,2},{7,3},{8,4},{9,5},{1... | collective-permute-start | bytes 196616 | tf_op jit(solution)/shard_map/gather_attended/ppermute | solution.py:264
  70.9 3.6 %collective-permute-start.5 = (bf16[256,128]{1,0:T(8,128)(2,1)S(1)}, bf16[256,128]{1,0:T(8,128)(2,1)S(1)}, u32[]{:S(2)}, u32[]{:S(2)}) collective-permute-start(bf16[256,128]{1,0:T(8,128)(2,1)S(1)} %get-tuple-element.35.refs_0_), channel_id=1, source_target_pairs={{0,8},{1,9},{2,10},{3,11},{4,12},{5,13},{6,14},{7,15},{8,0},{9,1},... | collective-permute-start | bytes 196616 | tf_op jit(solution)/shard_map/gather_attended/ppermute | solution.py:264
  74.5 2.3 %collective-permute-start.6 = (bf16[256,128]{1,0:T(8,128)(2,1)S(1)}, bf16[256,128]{1,0:T(8,128)(2,1)S(1)}, u32[]{:S(2)}, u32[]{:S(2)}) collective-permute-start(bf16[256,128]{1,0:T(8,128)(2,1)S(1)} %get-tuple-element.35.refs_0_), channel_id=1, source_target_pairs={{0,4},{1,5},{2,6},{3,7},{4,8},{5,9},{6,10},{7,11},{8,12},{9,13},{1... | collective-permute-start | bytes 196616 | tf_op jit(solution)/shard_map/gather_attended/ppermute | solution.py:264
  77.0 1.8 %collective-permute-done.5.refs_2_ = bf16[256,128]{1,0:T(8,128)(2,1)S(1)} collective-permute-done((bf16[256,128]{1,0:T(8,128)(2,1)S(1)}, bf16[256,128]{1,0:T(8,128)(2,1)S(1)}, u32[]{:S(2)}, u32[]{:S(2)}) %collective-permute-start.5) | collective-permute-done | bytes 65568 | tf_op jit(solution)/shard_map/gather_attended/ppermute | solution.py:264
  78.8 1.9 %collective-permute-done.6.refs_3_ = bf16[256,128]{1,0:T(8,128)(2,1)S(1)} collective-permute-done((bf16[256,128]{1,0:T(8,128)(2,1)S(1)}, bf16[256,128]{1,0:T(8,128)(2,1)S(1)}, u32[]{:S(2)}, u32[]{:S(2)}) %collective-permute-start.6) | collective-permute-done | bytes 65568 | tf_op jit(solution)/shard_map/gather_attended/ppermute | solution.py:264
  80.7 0.9 broadcast_in_dim.46
  81.6 7.2 %all-to-all-start.1 = ((bf16[8,32,1024]{2,1,0:T(8,128)(2,1)}), bf16[8,32,1024]{2,1,0:T(8,128)(2,1)S(1)}, u32[]{:S(2)}, u32[]{:S(2)}) async-start(bf16[8,32,1024]{2,1,0:T(8,128)(2,1)} %broadcast_in_dim.46), calls=%async_computation.1 | async-start | bytes 1048576 | tf_op jit(solution)/shard_map/gather_over_y/all_to_all | solution.py:271
  88.8 5.2 %collective-permute-start.9 = (bf16[4,128,128]{2,1,0:T(8,128)(2,1)S(1)}, bf16[4,128,128]{2,1,0:T(8,128)(2,1)S(1)}, u32[]{:S(2)}, u32[]{:S(2)}) collective-permute-start(bf16[4,128,128]{2,1,0:T(8,128)(2,1)S(1)} %get-tuple-element.50), channel_id=1, source_target_pairs={{0,96},{16,112},{32,0},{48,16},{64,32},{80,48},{96,64},{112,80},{1... | collective-permute-start | bytes 393224 | tf_op jit(solution)/shard_map/gather_projection/ppermute | solution.py:275
  94.0 1.9 %collective-permute-start.10 = (bf16[4,128,128]{2,1,0:T(8,128)(2,1)S(1)}, bf16[4,128,128]{2,1,0:T(8,128)(2,1)S(1)}, u32[]{:S(2)}, u32[]{:S(2)}) collective-permute-start(bf16[4,128,128]{2,1,0:T(8,128)(2,1)S(1)} %get-tuple-element.50), channel_id=1, source_target_pairs={{0,64},{16,80},{32,96},{48,112},{64,0},{80,16},{96,32},{112,48},{1... | collective-permute-start | bytes 393224 | tf_op jit(solution)/shard_map/gather_projection/ppermute | solution.py:275
  95.9 3.0 %collective-permute-start.11 = (bf16[4,128,128]{2,1,0:T(8,128)(2,1)S(1)}, bf16[4,128,128]{2,1,0:T(8,128)(2,1)S(1)}, u32[]{:S(2)}, u32[]{:S(2)}) collective-permute-start(bf16[4,128,128]{2,1,0:T(8,128)(2,1)S(1)} %get-tuple-element.50), channel_id=1, source_target_pairs={{0,32},{16,48},{32,64},{48,80},{64,96},{80,112},{96,0},{112,16},{1... | collective-permute-start | bytes 393224 | tf_op jit(solution)/shard_map/gather_projection/ppermute | solution.py:275
  99.0 3.9 %collective-permute-done.10 = bf16[4,128,128]{2,1,0:T(8,128)(2,1)S(1)} collective-permute-done((bf16[4,128,128]{2,1,0:T(8,128)(2,1)S(1)}, bf16[4,128,128]{2,1,0:T(8,128)(2,1)S(1)}, u32[]{:S(2)}, u32[]{:S(2)}) %collective-permute-start.10) | collective-permute-done | bytes 131104 | tf_op jit(solution)/shard_map/gather_projection/ppermute | solution.py:275
  102.9 1.7 collective-permute-done.11
  104.7 1.0 weight_terms.1
  105.7 1.9 %collective-permute-start.16 = (bf16[4,4,128,128]{3,2,1,0:T(8,128)(2,1)S(1)}, bf16[4,4,128,128]{3,2,1,0:T(8,128)(2,1)S(1)}, u32[]{:S(2)}, u32[]{:S(2)}) collective-permute-start(bf16[4,4,128,128]{3,2,1,0:T(8,128)(2,1)S(1)} %get-tuple-element.40), channel_id=1, source_target_pairs={{0,16},{16,0},{32,48},{48,32},{64,80},{80,64},{96,112},{112,96},{1... | collective-permute-start | bytes 1572872 | tf_op jit(solution)/shard_map/sum_over_core/ppermute | solution.py:283
  107.6 1.9 %collective-permute-done.16 = bf16[4,4,128,128]{3,2,1,0:T(8,128)(2,1)S(1)} collective-permute-done((bf16[4,4,128,128]{3,2,1,0:T(8,128)(2,1)S(1)}, bf16[4,4,128,128]{3,2,1,0:T(8,128)(2,1)S(1)}, u32[]{:S(2)}, u32[]{:S(2)}) %collective-permute-start.16) | collective-permute-done | bytes 524320 | tf_op jit(solution)/shard_map/sum_over_core/ppermute | solution.py:283
  109.5 0.9 add_convert_fusion
  110.4 4.1 %all-to-all-start.2 = ((bf16[4,4,128,128]{3,2,1,0:T(8,128)(2,1)}), bf16[4,4,128,128]{3,2,1,0:T(8,128)(2,1)}, u32[]{:S(2)}, u32[]{:S(2)}) async-start(bf16[4,4,128,128]{3,2,1,0:T(8,128)(2,1)} %add_convert_fusion), calls=%async_computation.2 | async-start | bytes 1048576 | tf_op jit(solution)/shard_map/sum_over_z_lo/all_to_all | solution.py:293
  114.6 2.3 %collective-permute-start.12 = (bf16[256,1024]{1,0:T(8,128)(2,1)S(1)}, bf16[256,1024]{1,0:T(8,128)(2,1)S(1)}, u32[]{:S(2)}, u32[]{:S(2)}) collective-permute-start(bf16[256,1024]{1,0:T(8,128)(2,1)S(1)} %bitcast.67), channel_id=1, source_target_pairs={{0,12},{1,13},{2,14},{3,15},{4,0},{5,1},{6,2},{7,3},{8,4},{9,5},{1... | collective-permute-start | bytes 1572872 | tf_op jit(solution)/shard_map/gather_over_x/ppermute | solution.py:289
  116.9 4.6 %collective-permute-start.13 = (bf16[256,1024]{1,0:T(8,128)(2,1)S(1)}, bf16[256,1024]{1,0:T(8,128)(2,1)S(1)}, u32[]{:S(2)}, u32[]{:S(2)}) collective-permute-start(bf16[256,1024]{1,0:T(8,128)(2,1)S(1)} %bitcast.68), channel_id=1, source_target_pairs={{0,8},{1,9},{2,10},{3,11},{4,12},{5,13},{6,14},{7,15},{8,0},{9,1},... | collective-permute-start | bytes 1572872 | tf_op jit(solution)/shard_map/gather_over_x/ppermute | solution.py:289
  121.4 4.5 %collective-permute-start.14 = (bf16[256,1024]{1,0:T(8,128)(2,1)S(1)}, bf16[256,1024]{1,0:T(8,128)(2,1)S(1)}, u32[]{:S(2)}, u32[]{:S(2)}) collective-permute-start(bf16[256,1024]{1,0:T(8,128)(2,1)S(1)} %bitcast.69), channel_id=1, source_target_pairs={{0,4},{1,5},{2,6},{3,7},{4,8},{5,9},{6,10},{7,11},{8,12},{9,13},{1... | collective-permute-start | bytes 1572872 | tf_op jit(solution)/shard_map/gather_over_x/ppermute | solution.py:289
  126.0 1.9 %collective-permute-start.15 = (bf16[4,4,128,128]{3,2,1,0:T(8,128)(2,1)S(1)}, bf16[4,4,128,128]{3,2,1,0:T(8,128)(2,1)S(1)}, u32[]{:S(2)}, u32[]{:S(2)}) collective-permute-start(bf16[4,4,128,128]{3,2,1,0:T(8,128)(2,1)S(1)} %pad_maximum_fusion.w_own_ref), channel_id=1, source_target_pairs={{0,16},{16,0},{32,48},{48,32},{64,80},{80,64},{96,112},{112,96},{1... | collective-permute-start | bytes 1572872 | tf_op jit(solution)/shard_map/gather_projection/ppermute | solution.py:286
  127.9 1.8 %all-to-all-done.2 = bf16[4,4,128,128]{3,2,1,0:T(8,128)(2,1)} async-done(((bf16[4,4,128,128]{3,2,1,0:T(8,128)(2,1)}), bf16[4,4,128,128]{3,2,1,0:T(8,128)(2,1)}, u32[]{:S(2)}, u32[]{:S(2)}) %all-to-all-start.2) | async-done | bytes 524320 | tf_op jit(solution)/shard_map/sum_over_z_lo/all_to_all | solution.py:293
  129.7 1.8 %fusion.17 = bf16[4,128,128]{2,1,0:T(8,128)(2,1)} fusion(bf16[4,4,128,128]{3,2,1,0:T(8,128)(2,1)} %all-to-all-done.2), kind=kLoop, calls=%fused_computation.30 | loop fusion | flops 524288 | bytes 655360 | tf_op jit(solution)/shard_map/sum_over_z_lo/add | solution.py:218
  131.5 3.9 %all-to-all-start.3 = ((bf16[4,128,128]{2,1,0:T(8,128)(2,1)}), bf16[4,128,128]{2,1,0:T(8,128)(2,1)}, u32[]{:S(2)}, u32[]{:S(2)}) async-start(bf16[4,128,128]{2,1,0:T(8,128)(2,1)} %fusion.17), calls=%async_computation.3 | async-start | bytes 262144 | tf_op jit(solution)/shard_map/sum_over_z_hi/all_to_all | solution.py:298
  135.5 9.7 %collective-permute-done.14.refs_3_ = bf16[256,1024]{1,0:T(8,128)(2,1)S(1)} collective-permute-done((bf16[256,1024]{1,0:T(8,128)(2,1)S(1)}, bf16[256,1024]{1,0:T(8,128)(2,1)S(1)}, u32[]{:S(2)}, u32[]{:S(2)}) %collective-permute-start.14) | collective-permute-done | bytes 524320 | tf_op jit(solution)/shard_map/gather_over_x/ppermute | solution.py:289
  145.2 1.3 head_grad.1
  146.6 0.3 fusion.2
  146.9 0.9 fusion.7
  147.8 1.1 fusion.5
  148.9 3.0 %all-to-all-done.3 = bf16[4,128,128]{2,1,0:T(8,128)(2,1)} async-done(((bf16[4,128,128]{2,1,0:T(8,128)(2,1)}), bf16[4,128,128]{2,1,0:T(8,128)(2,1)}, u32[]{:S(2)}, u32[]{:S(2)}) %all-to-all-start.3) | async-done | bytes 131104 | tf_op jit(solution)/shard_map/sum_over_z_hi/all_to_all | solution.py:298
  151.9 0.8 add_bitcast_fusion
  152.7 3.4 %collective-permute-start.17 = (f32[128,128]{1,0:T(8,128)S(1)}, f32[128,128]{1,0:T(8,128)S(1)}, u32[]{:S(2)}, u32[]{:S(2)}) collective-permute-start(f32[128,128]{1,0:T(8,128)S(1)} %add_bitcast_fusion), channel_id=1, source_target_pairs={{0,0},{1,1},{2,2},{3,3},{4,128},{5,129},{6,130},{7,131},{8,256},{9... | collective-permute-start | bytes 196616 | tf_op jit(solution)/shard_map/sum_over_z_hi/ppermute | solution.py:300
  156.1 1.1 fusion.4
  157.2 12.8 %collective-permute-done.17 = f32[128,128]{1,0:T(8,128)S(1)} collective-permute-done((f32[128,128]{1,0:T(8,128)S(1)}, f32[128,128]{1,0:T(8,128)S(1)}, u32[]{:S(2)}, u32[]{:S(2)}) %collective-permute-start.17) | collective-permute-done | bytes 65568 | tf_op jit(solution)/shard_map/sum_over_z_hi/ppermute | solution.py:300
  170.0 0.6 copy.18
  (43 shorter events, 1.1 us)
Async XLA Ops:
  0.6 30.2 %copy-start = (bf16[1,1024,128]{2,1,0:T(8,128)(2,1)S(1)}, bf16[1,1024,128]{2,1,0:T(8,128)(2,1)}, u32[]{:S(2)}) copy-start(bf16[1,1024,128]{2,1,0:T(8,128)(2,1)} %param.10) | copy-start | bytes 786436
  0.6 10.5 %copy-start.8 = (bf16[128,128]{1,0:T(8,128)(2,1)S(1)}, bf16[128,128]{1,0:T(8,128)(2,1)}, u32[]{:S(2)}) copy-start(bf16[128,128]{1,0:T(8,128)(2,1)} %param.11) | copy-start | bytes 98308
  0.7 28.7 %copy-start.9 = (s32[1,2,8]{2,1,0:T(2,128)S(1)}, s32[1,2,8]{2,1,0:T(2,128)}, u32[]{:S(2)}) copy-start(s32[1,2,8]{2,1,0:T(2,128)} %param.12) | copy-start | bytes 196
  0.7 29.1 %copy-start.6 = (bf16[1,256,128]{2,1,0:T(8,128)(2,1)S(1)}, bf16[1,256,128]{2,1,0:T(8,128)(2,1)}, u32[]{:S(2)}) copy-start(bf16[1,256,128]{2,1,0:T(8,128)(2,1)} %param.8) | copy-start | bytes 196612
  0.7 29.1 %copy-start.4 = (bf16[1,1024,128]{2,1,0:T(8,128)(2,1)S(1)}, bf16[1,1024,128]{2,1,0:T(8,128)(2,1)}, u32[]{:S(2)}) copy-start(bf16[1,1024,128]{2,1,0:T(8,128)(2,1)} %param.9) | copy-start | bytes 786436
  2.3 28.9 %collective-permute-start = (bf16[256,1024]{1,0:T(8,128)(2,1)S(1)}, bf16[256,1024]{1,0:T(8,128)(2,1)S(1)}, u32[]{:S(2)}, u32[]{:S(2)}) collective-permute-start(bf16[256,1024]{1,0:T(8,128)(2,1)S(1)} %get-tuple-element.47), channel_id=1, source_target_pairs={{0,4},{1,5},{2,6},{3,7},{4,8},{5,9},{6,10},{7,11},{8,12},{9,13},{1... | collective-permute-start | bytes 1572872 | tf_op jit(solution)/shard_map/sum_over_x/ppermute | solution.py:238
  5.4 25.8 %collective-permute-start.1 = (bf16[256,1024]{1,0:T(8,128)(2,1)S(1)}, bf16[256,1024]{1,0:T(8,128)(2,1)S(1)}, u32[]{:S(2)}, u32[]{:S(2)}) collective-permute-start(bf16[256,1024]{1,0:T(8,128)(2,1)S(1)} %get-tuple-element.48), channel_id=1, source_target_pairs={{0,8},{1,9},{2,10},{3,11},{4,12},{5,13},{6,14},{7,15},{8,0},{9,1},... | collective-permute-start | bytes 1572872 | tf_op jit(solution)/shard_map/sum_over_x/ppermute | solution.py:238
  8.1 24.7 %collective-permute-start.2 = (bf16[256,1024]{1,0:T(8,128)(2,1)S(1)}, bf16[256,1024]{1,0:T(8,128)(2,1)S(1)}, u32[]{:S(2)}, u32[]{:S(2)}) collective-permute-start(bf16[256,1024]{1,0:T(8,128)(2,1)S(1)} %get-tuple-element.46), channel_id=1, source_target_pairs={{0,12},{1,13},{2,14},{3,15},{4,0},{5,1},{6,2},{7,3},{8,4},{9,5},{1... | collective-permute-start | bytes 1572872 | tf_op jit(solution)/shard_map/sum_over_x/ppermute | solution.py:238
  11.2 22.7 %collective-permute-start.3 = (bf16[128,128]{1,0:T(8,128)(2,1)S(1)}, bf16[128,128]{1,0:T(8,128)(2,1)S(1)}, u32[]{:S(2)}, u32[]{:S(2)}) collective-permute-start(bf16[128,128]{1,0:T(8,128)(2,1)S(1)} %copy-done.8), channel_id=1, source_target_pairs={{0,384},{16,400},{32,416},{48,432},{64,448},{80,464},{96,480},{112... | collective-permute-start | bytes 98312 | tf_op jit(solution)/shard_map/gather_projection/ppermute | solution.py:242
  30.2 2.6 %copy-start.1 = (bf16[1,1,256,4096]{3,2,1,0:T(8,128)(2,1)S(1)}, bf16[1,1,256,4096]{3,2,1,0:T(8,128)(2,1)}, u32[]{:S(2)}) copy-start(bf16[1,1,256,4096]{3,2,1,0:T(8,128)(2,1)} %param.7) | copy-start | bytes 6291460
  30.8 2.0 %copy-start.2 = (f32[256,1024]{1,0:T(8,128)}, f32[256,1024]{1,0:T(8,128)S(1)}, u32[]{:S(2)}) copy-start(f32[256,1024]{1,0:T(8,128)S(1)} %fusion.8) | copy-start | bytes 3145732
  33.9 42.9 %all-to-all-start = ((bf16[8,32,1024]{2,1,0:T(8,128)(2,1)}), bf16[8,32,1024]{2,1,0:T(8,128)(2,1)S(1)}, u32[]{:S(2)}, u32[]{:S(2)}) async-start(bf16[8,32,1024]{2,1,0:T(8,128)(2,1)} %bitcast.14), calls=%async_computation | async-start | bytes 1048576 | tf_op jit(solution)/shard_map/sum_over_y/all_to_all | solution.py:256
  41.4 35.6 %collective-permute-start.7 = (bf16[128,128]{1,0:T(8,128)(2,1)S(1)}, bf16[128,128]{1,0:T(8,128)(2,1)S(1)}, u32[]{:S(2)}, u32[]{:S(2)}) collective-permute-start(bf16[128,128]{1,0:T(8,128)(2,1)S(1)} %copy-done.8), channel_id=1, source_target_pairs={{0,256},{16,272},{32,288},{48,304},{64,320},{80,336},{96,352},{112... | collective-permute-start | bytes 98312 | tf_op jit(solution)/shard_map/gather_projection/ppermute | solution.py:242
  60.8 16.2 %collective-permute-start.8 = (bf16[128,128]{1,0:T(8,128)(2,1)S(1)}, bf16[128,128]{1,0:T(8,128)(2,1)S(1)}, u32[]{:S(2)}, u32[]{:S(2)}) collective-permute-start(bf16[128,128]{1,0:T(8,128)(2,1)S(1)} %copy-done.8), channel_id=1, source_target_pairs={{0,128},{16,144},{32,160},{48,176},{64,192},{80,208},{96,224},{112... | collective-permute-start | bytes 98312 | tf_op jit(solution)/shard_map/gather_projection/ppermute | solution.py:242
  67.6 9.4 %collective-permute-start.4 = (bf16[256,128]{1,0:T(8,128)(2,1)S(1)}, bf16[256,128]{1,0:T(8,128)(2,1)S(1)}, u32[]{:S(2)}, u32[]{:S(2)}) collective-permute-start(bf16[256,128]{1,0:T(8,128)(2,1)S(1)} %get-tuple-element.35.refs_0_), channel_id=1, source_target_pairs={{0,12},{1,13},{2,14},{3,15},{4,0},{5,1},{6,2},{7,3},{8,4},{9,5},{1... | collective-permute-start | bytes 196616 | tf_op jit(solution)/shard_map/gather_attended/ppermute | solution.py:264
  70.9 7.9 %collective-permute-start.5 = (bf16[256,128]{1,0:T(8,128)(2,1)S(1)}, bf16[256,128]{1,0:T(8,128)(2,1)S(1)}, u32[]{:S(2)}, u32[]{:S(2)}) collective-permute-start(bf16[256,128]{1,0:T(8,128)(2,1)S(1)} %get-tuple-element.35.refs_0_), channel_id=1, source_target_pairs={{0,8},{1,9},{2,10},{3,11},{4,12},{5,13},{6,14},{7,15},{8,0},{9,1},... | collective-permute-start | bytes 196616 | tf_op jit(solution)/shard_map/gather_attended/ppermute | solution.py:264
  74.5 6.2 %collective-permute-start.6 = (bf16[256,128]{1,0:T(8,128)(2,1)S(1)}, bf16[256,128]{1,0:T(8,128)(2,1)S(1)}, u32[]{:S(2)}, u32[]{:S(2)}) collective-permute-start(bf16[256,128]{1,0:T(8,128)(2,1)S(1)} %get-tuple-element.35.refs_0_), channel_id=1, source_target_pairs={{0,4},{1,5},{2,6},{3,7},{4,8},{5,9},{6,10},{7,11},{8,12},{9,13},{1... | collective-permute-start | bytes 196616 | tf_op jit(solution)/shard_map/gather_attended/ppermute | solution.py:264
  81.6 23.1 %all-to-all-start.1 = ((bf16[8,32,1024]{2,1,0:T(8,128)(2,1)}), bf16[8,32,1024]{2,1,0:T(8,128)(2,1)S(1)}, u32[]{:S(2)}, u32[]{:S(2)}) async-start(bf16[8,32,1024]{2,1,0:T(8,128)(2,1)} %broadcast_in_dim.46), calls=%async_computation.1 | async-start | bytes 1048576 | tf_op jit(solution)/shard_map/gather_over_y/all_to_all | solution.py:271
  88.8 10.2 %collective-permute-start.9 = (bf16[4,128,128]{2,1,0:T(8,128)(2,1)S(1)}, bf16[4,128,128]{2,1,0:T(8,128)(2,1)S(1)}, u32[]{:S(2)}, u32[]{:S(2)}) collective-permute-start(bf16[4,128,128]{2,1,0:T(8,128)(2,1)S(1)} %get-tuple-element.50), channel_id=1, source_target_pairs={{0,96},{16,112},{32,0},{48,16},{64,32},{80,48},{96,64},{112,80},{1... | collective-permute-start | bytes 393224 | tf_op jit(solution)/shard_map/gather_projection/ppermute | solution.py:275
  94.0 8.9 %collective-permute-start.10 = (bf16[4,128,128]{2,1,0:T(8,128)(2,1)S(1)}, bf16[4,128,128]{2,1,0:T(8,128)(2,1)S(1)}, u32[]{:S(2)}, u32[]{:S(2)}) collective-permute-start(bf16[4,128,128]{2,1,0:T(8,128)(2,1)S(1)} %get-tuple-element.50), channel_id=1, source_target_pairs={{0,64},{16,80},{32,96},{48,112},{64,0},{80,16},{96,32},{112,48},{1... | collective-permute-start | bytes 393224 | tf_op jit(solution)/shard_map/gather_projection/ppermute | solution.py:275
  95.9 8.7 %collective-permute-start.11 = (bf16[4,128,128]{2,1,0:T(8,128)(2,1)S(1)}, bf16[4,128,128]{2,1,0:T(8,128)(2,1)S(1)}, u32[]{:S(2)}, u32[]{:S(2)}) collective-permute-start(bf16[4,128,128]{2,1,0:T(8,128)(2,1)S(1)} %get-tuple-element.50), channel_id=1, source_target_pairs={{0,32},{16,48},{32,64},{48,80},{64,96},{80,112},{96,0},{112,16},{1... | collective-permute-start | bytes 393224 | tf_op jit(solution)/shard_map/gather_projection/ppermute | solution.py:275
  105.7 3.8 %collective-permute-start.16 = (bf16[4,4,128,128]{3,2,1,0:T(8,128)(2,1)S(1)}, bf16[4,4,128,128]{3,2,1,0:T(8,128)(2,1)S(1)}, u32[]{:S(2)}, u32[]{:S(2)}) collective-permute-start(bf16[4,4,128,128]{3,2,1,0:T(8,128)(2,1)S(1)} %get-tuple-element.40), channel_id=1, source_target_pairs={{0,16},{16,0},{32,48},{48,32},{64,80},{80,64},{96,112},{112,96},{1... | collective-permute-start | bytes 1572872 | tf_op jit(solution)/shard_map/sum_over_core/ppermute | solution.py:283
  110.4 19.3 %all-to-all-start.2 = ((bf16[4,4,128,128]{3,2,1,0:T(8,128)(2,1)}), bf16[4,4,128,128]{3,2,1,0:T(8,128)(2,1)}, u32[]{:S(2)}, u32[]{:S(2)}) async-start(bf16[4,4,128,128]{3,2,1,0:T(8,128)(2,1)} %add_convert_fusion), calls=%async_computation.2 | async-start | bytes 1048576 | tf_op jit(solution)/shard_map/sum_over_z_lo/all_to_all | solution.py:293
  114.6 20.9 %collective-permute-start.12 = (bf16[256,1024]{1,0:T(8,128)(2,1)S(1)}, bf16[256,1024]{1,0:T(8,128)(2,1)S(1)}, u32[]{:S(2)}, u32[]{:S(2)}) collective-permute-start(bf16[256,1024]{1,0:T(8,128)(2,1)S(1)} %bitcast.67), channel_id=1, source_target_pairs={{0,12},{1,13},{2,14},{3,15},{4,0},{5,1},{6,2},{7,3},{8,4},{9,5},{1... | collective-permute-start | bytes 1572872 | tf_op jit(solution)/shard_map/gather_over_x/ppermute | solution.py:289
  116.9 18.7 %collective-permute-start.13 = (bf16[256,1024]{1,0:T(8,128)(2,1)S(1)}, bf16[256,1024]{1,0:T(8,128)(2,1)S(1)}, u32[]{:S(2)}, u32[]{:S(2)}) collective-permute-start(bf16[256,1024]{1,0:T(8,128)(2,1)S(1)} %bitcast.68), channel_id=1, source_target_pairs={{0,8},{1,9},{2,10},{3,11},{4,12},{5,13},{6,14},{7,15},{8,0},{9,1},... | collective-permute-start | bytes 1572872 | tf_op jit(solution)/shard_map/gather_over_x/ppermute | solution.py:289
  121.4 23.7 %collective-permute-start.14 = (bf16[256,1024]{1,0:T(8,128)(2,1)S(1)}, bf16[256,1024]{1,0:T(8,128)(2,1)S(1)}, u32[]{:S(2)}, u32[]{:S(2)}) collective-permute-start(bf16[256,1024]{1,0:T(8,128)(2,1)S(1)} %bitcast.69), channel_id=1, source_target_pairs={{0,4},{1,5},{2,6},{3,7},{4,8},{5,9},{6,10},{7,11},{8,12},{9,13},{1... | collective-permute-start | bytes 1572872 | tf_op jit(solution)/shard_map/gather_over_x/ppermute | solution.py:289
  126.0 19.2 %collective-permute-start.15 = (bf16[4,4,128,128]{3,2,1,0:T(8,128)(2,1)S(1)}, bf16[4,4,128,128]{3,2,1,0:T(8,128)(2,1)S(1)}, u32[]{:S(2)}, u32[]{:S(2)}) collective-permute-start(bf16[4,4,128,128]{3,2,1,0:T(8,128)(2,1)S(1)} %pad_maximum_fusion.w_own_ref), channel_id=1, source_target_pairs={{0,16},{16,0},{32,48},{48,32},{64,80},{80,64},{96,112},{112,96},{1... | collective-permute-start | bytes 1572872 | tf_op jit(solution)/shard_map/gather_projection/ppermute | solution.py:286
  131.5 20.4 %all-to-all-start.3 = ((bf16[4,128,128]{2,1,0:T(8,128)(2,1)}), bf16[4,128,128]{2,1,0:T(8,128)(2,1)}, u32[]{:S(2)}, u32[]{:S(2)}) async-start(bf16[4,128,128]{2,1,0:T(8,128)(2,1)} %fusion.17), calls=%async_computation.3 | async-start | bytes 262144 | tf_op jit(solution)/shard_map/sum_over_z_hi/all_to_all | solution.py:298
  135.5 11.1 %copy-start.3 = (f32[256,1024]{1,0:T(8,128)S(1)}, f32[256,1024]{1,0:T(8,128)}, u32[]{:S(2)}) copy-start(f32[256,1024]{1,0:T(8,128)} %copy-done.2) | copy-start | bytes 3145732
  135.5 11.4 %copy-start.5 = (bf16[1,1024,128]{2,1,0:T(8,128)(2,1)S(1)}, bf16[1,1024,128]{2,1,0:T(8,128)(2,1)}, u32[]{:S(2)}) copy-start(bf16[1,1024,128]{2,1,0:T(8,128)(2,1)} %param.9) | copy-start | bytes 786436
  146.6 9.5 %copy-start.7 = (bf16[1,256,128]{2,1,0:T(8,128)(2,1)S(1)}, bf16[1,256,128]{2,1,0:T(8,128)(2,1)}, u32[]{:S(2)}) copy-start(bf16[1,256,128]{2,1,0:T(8,128)(2,1)} %param.8) | copy-start | bytes 196612
  152.7 17.3 %collective-permute-start.17 = (f32[128,128]{1,0:T(8,128)S(1)}, f32[128,128]{1,0:T(8,128)S(1)}, u32[]{:S(2)}, u32[]{:S(2)}) collective-permute-start(f32[128,128]{1,0:T(8,128)S(1)} %add_bitcast_fusion), channel_id=1, source_target_pairs={{0,0},{1,1},{2,2},{3,3},{4,128},{5,129},{6,130},{7,131},{8,256},{9... | collective-permute-start | bytes 196616 | tf_op jit(solution)/shard_map/sum_over_z_hi/ppermute | solution.py:300

commit v6 on v5

--- a/solution.py
+++ b/solution.py
@@ -28,15 +28,6 @@
 def shift_zl(k):
     return [
         (scene_index(a, b, c), scene_index(a, (b + k) % ZL, c))
-        for a in range(ZH)
-        for b in range(ZL)
-        for c in range(CORES)
-    ]
-
-
-def shift_zh(k):
-    return [
-        (scene_index(a, b, c), scene_index((a + k) % ZH, b, c))
         for a in range(ZH)
         for b in range(ZL)
         for c in range(CORES)
@@ -171,10 +162,10 @@
 
 def head_grad_kernel(place_ref, w_own_ref, w_other_ref, *refs):
     *blocks, out_ref = refs
-    core, x, zl, zh = [place_ref[i] for i in range(4)]
+    core, x, zl = [place_ref[i] for i in range(3)]
     total = jnp.zeros(out_ref.shape, jnp.float32)
     for k in range(X):
-        far = (x + k - zh) & (ZH - 1)
+        far = (x + k) & (X - 1)
         for b in range(ZL):
             near = (b - zl) & (ZL - 1)
             left = b * CORES * HEAD_DIM
@@ -223,9 +214,9 @@
     scaling = 1.0 / math.sqrt(HEAD_DIM)
     section, mp, scene = (lax.axis_index(name) for name in ("section", "mp", "scene"))
     x, y = shift_right(mp, YH), (mp & (YH - 1)) * YL + section
-    zh, zl = shift_right(scene, ZL * CORES), shift_right(scene, CORES) & (ZL - 1)
+    zl = shift_right(scene, CORES) & (ZL - 1)
     core = scene & (CORES - 1)
-    place = jnp.stack([core, x, zl, zh])
+    place = jnp.stack([core, x, zl])
     sample = dec_grad[0, 0]
     tokens, model = sample.shape
     width = model // X
@@ -239,7 +230,8 @@
         partial = add_own(x, sample, arrived)
 
     with jax.named_scope("gather_projection"):
-        w_rows = [w_out] + [lax.ppermute(w_out, "scene", shift_zh(-k)) for k in range(1, ZH)]
+        w_spread = jnp.broadcast_to(w_out[None], (ZH, *w_out.shape))
+        w_far = lax.all_to_all(w_spread, "scene", 0, 0, axis_index_groups=z_hi_groups())
 
     queries, keys, values = agent_queries[0], map_keys[0], map_values[0]
     mask_rows = block_mask[0]
@@ -248,9 +240,7 @@
     probs, weights, attended = attend_forward(queries, keys, values, visible, scaling)
     attended_rounded = attended.astype(jnp.bfloat16)
 
-    partial, w_rows[1], attended_rounded = lax.optimization_barrier(
-        (partial, w_rows[1], attended_rounded)
-    )
+    partial, w_far, attended_rounded = lax.optimization_barrier((partial, w_far, attended_rounded))
     with jax.named_scope("sum_over_y"):
         rows = tokens // (YH * YL)
         lines = lax.all_to_all(
@@ -264,8 +254,7 @@
             lax.ppermute(attended_rounded, "mp", shift_x(-k)) for k in range(1, X)
         ]
 
-    own, attended_near, w_rows = lax.optimization_barrier((own, attended_near, w_rows))
-    w_far = jnp.stack(w_rows)
+    own, attended_near = lax.optimization_barrier((own, attended_near))
     with jax.named_scope("gather_over_y"):
         spread = jnp.broadcast_to(own[None], (YH * YL, rows, width))
         block = lax.all_to_all(spread, XY, 0, 0, axis_index_groups=y_groups())

time: 172 us -> 160 us (0.930)
  starting transfers between devices: 113 us -> 96.2 us
  waiting for transfers between devices: 40.1 us -> 42.7 us
    ppermute x3 -> x0, starting transfers between devices: 43.7 us -> none  [shards(): lax.ppermute(w_out, 'scene', shift_zh(-k))]
    all_to_all x0 -> x1, starting transfers between devices: none -> 18.7 us  [shards(): lax.all_to_all(w_spread, 'scene', 0, 0, axis_index_groups=z_hi_groups())]
    all_to_all x0 -> x1, waiting for transfers between devices: none -> 11.5 us  [shards(): lax.all_to_all(w_spread, 'scene', 0, 0, axis_index_groups=z_hi_groups())]
    ppermute x3, waiting for transfers between devices: 9.67 us -> 4.52 us  [shards(): lax.ppermute(block, 'mp', shift_x(-k))]
    all_to_all x1, starting transfers between devices: 3.94 us -> 7.61 us  [shards(): lax.all_to_all(near, 'scene', 0, 0, axis_index_groups=z_hi_groups())]
    all_to_all x1, waiting for transfers between devices: 3 us -> 6.15 us  [shards(): lax.all_to_all(near, 'scene', 0, 0, axis_index_groups=z_hi_groups())]
    ppermute x1, waiting for transfers between devices: 12.8 us -> 10.4 us  [shards(): d_wout = lax.ppermute(summed_block, ('scene', 'mp'), swap_x_zh())]
    ppermute x1, starting transfers between devices: 3.36 us -> 5.83 us  [shards(): d_wout = lax.ppermute(summed_block, ('scene', 'mp'), swap_x_zh())]
  transfers between devices with their start and end apart: 22 -> 20, of which waited for: 10 -> 10; matrix products, arithmetic and copies ran while one was open for 4% -> 7% of each run, Pallas kernels for 1% -> 1%
where the time goes in v6:
time: 160 us; the launch traced here: 159 us
  starting transfers between devices  96.2 us (60%)
  waiting for transfers between devices  42.7 us (27%)
  matrix products  5.8 us (4%)
  other arithmetic  5.49 us (3%)
  local copies, waits for them, and re-layouts  4.11 us (3%)
  Pallas kernels  3.33 us (2%)
  between operations  1.67 us (1%)
    all_to_all x1, starting transfers between devices, shards(): lax.all_to_all(w_spread, 'scene', 0, 0, axis_index_groups=z_hi_groups())  18.7 us
    all_to_all x1, waiting for transfers between devices, shards(): lax.all_to_all(w_spread, 'scene', 0, 0, axis_index_groups=z_hi_groups())  11.5 us
    ppermute x3, starting transfers between devices, shards(): lax.ppermute(block, 'mp', shift_x(-k))  11.5 us
    ppermute x3, starting transfers between devices, shards(): lax.ppermute(attended_rounded, 'mp', shift_x(-k))  11.4 us
    ppermute x1, waiting for transfers between devices, shards(): d_wout = lax.ppermute(summed_block, ('scene', 'mp'), swap_x_zh())  10.4 us
    ppermute x3, starting transfers between devices, shards(): lax.ppermute(w_far, 'scene', shift_zl(-k))  9.64 us
    ppermute x3, starting transfers between devices, shards(): lax.ppermute(piece, 'mp', shift_x(k + 1))  8.86 us
    all_to_all x1, starting transfers between devices, shards(): lax.all_to_all(near, 'scene', 0, 0, axis_index_groups=z_hi_groups())  7.61 us
  transfers between devices with their start and end apart: 20, of which 10 were waited for; matrix products, arithmetic and copies ran while one was open for 7% of the time, Pallas kernels for 1%

profile of v6, /device:TPU:12, one launch (start us, length us, event | category | flops | bytes accessed | tf_op | source)
XLA Modules:
  0.0 159.3 jit_solution(12314794787843694533)
XLA Ops:
  0.7 1.5 dynamic-slice_bitcast_fusion
  2.2 3.1 %collective-permute-start = (bf16[256,1024]{1,0:T(8,128)(2,1)S(1)}, bf16[256,1024]{1,0:T(8,128)(2,1)S(1)}, u32[]{:S(2)}, u32[]{:S(2)}) collective-permute-start(bf16[256,1024]{1,0:T(8,128)(2,1)S(1)} %get-tuple-element.39), channel_id=1, source_target_pairs={{0,4},{1,5},{2,6},{3,7},{4,8},{5,9},{6,10},{7,11},{8,12},{9,13},{1... | collective-permute-start | bytes 1572872 | tf_op jit(solution)/shard_map/sum_over_x/ppermute | solution.py:229
  5.3 2.7 %collective-permute-start.1 = (bf16[256,1024]{1,0:T(8,128)(2,1)S(1)}, bf16[256,1024]{1,0:T(8,128)(2,1)S(1)}, u32[]{:S(2)}, u32[]{:S(2)}) collective-permute-start(bf16[256,1024]{1,0:T(8,128)(2,1)S(1)} %get-tuple-element.40), channel_id=1, source_target_pairs={{0,8},{1,9},{2,10},{3,11},{4,12},{5,13},{6,14},{7,15},{8,0},{9,1},... | collective-permute-start | bytes 1572872 | tf_op jit(solution)/shard_map/sum_over_x/ppermute | solution.py:229
  8.1 3.0 %collective-permute-start.2 = (bf16[256,1024]{1,0:T(8,128)(2,1)S(1)}, bf16[256,1024]{1,0:T(8,128)(2,1)S(1)}, u32[]{:S(2)}, u32[]{:S(2)}) collective-permute-start(bf16[256,1024]{1,0:T(8,128)(2,1)S(1)} %get-tuple-element.38), channel_id=1, source_target_pairs={{0,12},{1,13},{2,14},{3,15},{4,0},{5,1},{6,2},{7,3},{8,4},{9,5},{1... | collective-permute-start | bytes 1572872 | tf_op jit(solution)/shard_map/sum_over_x/ppermute | solution.py:229
  11.1 0.7 broadcast_in_dim.51
  11.8 18.7 %all-to-all-start = ((bf16[4,128,128]{2,1,0:T(8,128)(2,1)}), bf16[4,128,128]{2,1,0:T(8,128)(2,1)}, u32[]{:S(2)}, u32[]{:S(2)}) async-start(bf16[4,128,128]{2,1,0:T(8,128)(2,1)} %broadcast_in_dim.51), calls=%async_computation | async-start | bytes 262144 | tf_op jit(solution)/shard_map/gather_projection/all_to_all | solution.py:234
  30.6 0.3 broadcast_in_dim.48
  30.9 1.4 fusion.20
  32.3 0.3 fusion.9
  32.9 1.1 fusion.21
  34.0 1.1 add_own.1
  35.1 11.5 %all-to-all-done = bf16[4,128,128]{2,1,0:T(8,128)(2,1)} async-done(((bf16[4,128,128]{2,1,0:T(8,128)(2,1)}), bf16[4,128,128]{2,1,0:T(8,128)(2,1)}, u32[]{:S(2)}, u32[]{:S(2)}) %all-to-all-start) | async-done | bytes 131104 | tf_op jit(solution)/shard_map/gather_projection/all_to_all | solution.py:234
  46.6 7.5 %all-to-all-start.1 = ((bf16[8,32,1024]{2,1,0:T(8,128)(2,1)}), bf16[8,32,1024]{2,1,0:T(8,128)(2,1)S(1)}, u32[]{:S(2)}, u32[]{:S(2)}) async-start(bf16[8,32,1024]{2,1,0:T(8,128)(2,1)} %bitcast.13), calls=%async_computation.1 | async-start | bytes 1048576 | tf_op jit(solution)/shard_map/sum_over_y/all_to_all | solution.py:246
  54.8 4.1 %collective-permute-start.3 = (bf16[256,128]{1,0:T(8,128)(2,1)S(1)}, bf16[256,128]{1,0:T(8,128)(2,1)S(1)}, u32[]{:S(2)}, u32[]{:S(2)}) collective-permute-start(bf16[256,128]{1,0:T(8,128)(2,1)S(1)} %get-tuple-element.27.refs_0_), channel_id=1, source_target_pairs={{0,12},{1,13},{2,14},{3,15},{4,0},{5,1},{6,2},{7,3},{8,4},{9,5},{1... | collective-permute-start | bytes 196616 | tf_op jit(solution)/shard_map/gather_attended/ppermute | solution.py:254
  58.9 2.8 %collective-permute-start.4 = (bf16[256,128]{1,0:T(8,128)(2,1)S(1)}, bf16[256,128]{1,0:T(8,128)(2,1)S(1)}, u32[]{:S(2)}, u32[]{:S(2)}) collective-permute-start(bf16[256,128]{1,0:T(8,128)(2,1)S(1)} %get-tuple-element.27.refs_0_), channel_id=1, source_target_pairs={{0,8},{1,9},{2,10},{3,11},{4,12},{5,13},{6,14},{7,15},{8,0},{9,1},... | collective-permute-start | bytes 196616 | tf_op jit(solution)/shard_map/gather_attended/ppermute | solution.py:254
  61.7 4.5 %collective-permute-start.5 = (bf16[256,128]{1,0:T(8,128)(2,1)S(1)}, bf16[256,128]{1,0:T(8,128)(2,1)S(1)}, u32[]{:S(2)}, u32[]{:S(2)}) collective-permute-start(bf16[256,128]{1,0:T(8,128)(2,1)S(1)} %get-tuple-element.27.refs_0_), channel_id=1, source_target_pairs={{0,4},{1,5},{2,6},{3,7},{4,8},{5,9},{6,10},{7,11},{8,12},{9,13},{1... | collective-permute-start | bytes 196616 | tf_op jit(solution)/shard_map/gather_attended/ppermute | solution.py:254
  66.5 1.6 collective-permute-done.5.refs_3_
  68.1 0.9 broadcast_in_dim.53
  68.9 7.2 %all-to-all-start.2 = ((bf16[8,32,1024]{2,1,0:T(8,128)(2,1)}), bf16[8,32,1024]{2,1,0:T(8,128)(2,1)S(1)}, u32[]{:S(2)}, u32[]{:S(2)}) async-start(bf16[8,32,1024]{2,1,0:T(8,128)(2,1)} %broadcast_in_dim.53), calls=%async_computation.2 | async-start | bytes 1048576 | tf_op jit(solution)/shard_map/gather_over_y/all_to_all | solution.py:260
  76.2 3.3 %collective-permute-start.6 = (bf16[4,128,128]{2,1,0:T(8,128)(2,1)}, bf16[4,128,128]{2,1,0:T(8,128)(2,1)S(1)}, u32[]{:S(2)}, u32[]{:S(2)}) collective-permute-start(bf16[4,128,128]{2,1,0:T(8,128)(2,1)} %all-to-all-done), channel_id=1, source_target_pairs={{0,96},{16,112},{32,0},{48,16},{64,32},{80,48},{96,64},{112,80},{1... | collective-permute-start | bytes 393224 | tf_op jit(solution)/shard_map/gather_projection/ppermute | solution.py:264
  79.4 2.5 %collective-permute-start.7 = (bf16[4,128,128]{2,1,0:T(8,128)(2,1)}, bf16[4,128,128]{2,1,0:T(8,128)(2,1)S(1)}, u32[]{:S(2)}, u32[]{:S(2)}) collective-permute-start(bf16[4,128,128]{2,1,0:T(8,128)(2,1)} %all-to-all-done), channel_id=1, source_target_pairs={{0,64},{16,80},{32,96},{48,112},{64,0},{80,16},{96,32},{112,48},{1... | collective-permute-start | bytes 393224 | tf_op jit(solution)/shard_map/gather_projection/ppermute | solution.py:264
  81.9 3.9 %collective-permute-start.8 = (bf16[4,128,128]{2,1,0:T(8,128)(2,1)}, bf16[4,128,128]{2,1,0:T(8,128)(2,1)S(1)}, u32[]{:S(2)}, u32[]{:S(2)}) collective-permute-start(bf16[4,128,128]{2,1,0:T(8,128)(2,1)} %all-to-all-done), channel_id=1, source_target_pairs={{0,32},{16,48},{32,64},{48,80},{64,96},{80,112},{96,0},{112,16},{1... | collective-permute-start | bytes 393224 | tf_op jit(solution)/shard_map/gather_projection/ppermute | solution.py:264
  85.9 2.9 %collective-permute-done.7 = bf16[4,128,128]{2,1,0:T(8,128)(2,1)S(1)} collective-permute-done((bf16[4,128,128]{2,1,0:T(8,128)(2,1)}, bf16[4,128,128]{2,1,0:T(8,128)(2,1)S(1)}, u32[]{:S(2)}, u32[]{:S(2)}) %collective-permute-start.7) | collective-permute-done | bytes 131104 | tf_op jit(solution)/shard_map/gather_projection/ppermute | solution.py:264
  88.8 2.0 %collective-permute-done.8 = bf16[4,128,128]{2,1,0:T(8,128)(2,1)S(1)} collective-permute-done((bf16[4,128,128]{2,1,0:T(8,128)(2,1)}, bf16[4,128,128]{2,1,0:T(8,128)(2,1)S(1)}, u32[]{:S(2)}, u32[]{:S(2)}) %collective-permute-start.8) | collective-permute-done | bytes 131104 | tf_op jit(solution)/shard_map/gather_projection/ppermute | solution.py:264
  90.8 1.0 pad_maximum_fusion.w_own_ref
  91.7 1.0 weight_terms.1
  92.8 1.9 %collective-permute-start.13 = (bf16[4,4,128,128]{3,2,1,0:T(8,128)(2,1)S(1)}, bf16[4,4,128,128]{3,2,1,0:T(8,128)(2,1)S(1)}, u32[]{:S(2)}, u32[]{:S(2)}) collective-permute-start(bf16[4,4,128,128]{3,2,1,0:T(8,128)(2,1)S(1)} %get-tuple-element.32), channel_id=1, source_target_pairs={{0,16},{16,0},{32,48},{48,32},{64,80},{80,64},{96,112},{112,96},{1... | collective-permute-start | bytes 1572872 | tf_op jit(solution)/shard_map/sum_over_core/ppermute | solution.py:272
  94.7 1.9 %collective-permute-done.13 = bf16[4,4,128,128]{3,2,1,0:T(8,128)(2,1)S(1)} collective-permute-done((bf16[4,4,128,128]{3,2,1,0:T(8,128)(2,1)S(1)}, bf16[4,4,128,128]{3,2,1,0:T(8,128)(2,1)S(1)}, u32[]{:S(2)}, u32[]{:S(2)}) %collective-permute-start.13) | collective-permute-done | bytes 524320 | tf_op jit(solution)/shard_map/sum_over_core/ppermute | solution.py:272
  96.6 0.9 add_convert_fusion
  97.5 4.1 %all-to-all-start.3 = ((bf16[4,4,128,128]{3,2,1,0:T(8,128)(2,1)}), bf16[4,4,128,128]{3,2,1,0:T(8,128)(2,1)}, u32[]{:S(2)}, u32[]{:S(2)}) async-start(bf16[4,4,128,128]{3,2,1,0:T(8,128)(2,1)} %add_convert_fusion), calls=%async_computation.3 | async-start | bytes 1048576 | tf_op jit(solution)/shard_map/sum_over_z_lo/all_to_all | solution.py:282
  101.7 5.6 %collective-permute-start.10 = (bf16[256,1024]{1,0:T(8,128)(2,1)S(1)}, bf16[256,1024]{1,0:T(8,128)(2,1)S(1)}, u32[]{:S(2)}, u32[]{:S(2)}) collective-permute-start(bf16[256,1024]{1,0:T(8,128)(2,1)S(1)} %bitcast.61), channel_id=1, source_target_pairs={{0,8},{1,9},{2,10},{3,11},{4,12},{5,13},{6,14},{7,15},{8,0},{9,1},... | collective-permute-start | bytes 1572872 | tf_op jit(solution)/shard_map/gather_over_x/ppermute | solution.py:278
  107.3 1.9 %collective-permute-start.11 = (bf16[256,1024]{1,0:T(8,128)(2,1)S(1)}, bf16[256,1024]{1,0:T(8,128)(2,1)S(1)}, u32[]{:S(2)}, u32[]{:S(2)}) collective-permute-start(bf16[256,1024]{1,0:T(8,128)(2,1)S(1)} %bitcast.62), channel_id=1, source_target_pairs={{0,4},{1,5},{2,6},{3,7},{4,8},{5,9},{6,10},{7,11},{8,12},{9,13},{1... | collective-permute-start | bytes 1572872 | tf_op jit(solution)/shard_map/gather_over_x/ppermute | solution.py:278
  109.2 1.9 %collective-permute-start.12 = (bf16[4,4,128,128]{3,2,1,0:T(8,128)(2,1)S(1)}, bf16[4,4,128,128]{3,2,1,0:T(8,128)(2,1)S(1)}, u32[]{:S(2)}, u32[]{:S(2)}) collective-permute-start(bf16[4,4,128,128]{3,2,1,0:T(8,128)(2,1)S(1)} %pad_maximum_fusion.w_own_ref), channel_id=1, source_target_pairs={{0,16},{16,0},{32,48},{48,32},{64,80},{80,64},{96,112},{112,96},{1... | collective-permute-start | bytes 1572872 | tf_op jit(solution)/shard_map/gather_projection/ppermute | solution.py:275
  111.1 3.9 %collective-permute-start.9 = (bf16[256,1024]{1,0:T(8,128)(2,1)S(1)}, bf16[256,1024]{1,0:T(8,128)(2,1)S(1)}, u32[]{:S(2)}, u32[]{:S(2)}) collective-permute-start(bf16[256,1024]{1,0:T(8,128)(2,1)S(1)} %bitcast.63), channel_id=1, source_target_pairs={{0,12},{1,13},{2,14},{3,15},{4,0},{5,1},{6,2},{7,3},{8,4},{9,5},{1... | collective-permute-start | bytes 1572872 | tf_op jit(solution)/shard_map/gather_over_x/ppermute | solution.py:278
  115.1 1.7 %all-to-all-done.3 = bf16[4,4,128,128]{3,2,1,0:T(8,128)(2,1)} async-done(((bf16[4,4,128,128]{3,2,1,0:T(8,128)(2,1)}), bf16[4,4,128,128]{3,2,1,0:T(8,128)(2,1)}, u32[]{:S(2)}, u32[]{:S(2)}) %all-to-all-start.3) | async-done | bytes 524320 | tf_op jit(solution)/shard_map/sum_over_z_lo/all_to_all | solution.py:282
  116.8 1.8 %fusion.17 = bf16[4,128,128]{2,1,0:T(8,128)(2,1)} fusion(bf16[4,4,128,128]{3,2,1,0:T(8,128)(2,1)} %all-to-all-done.3), kind=kLoop, calls=%fused_computation.30 | loop fusion | flops 524288 | bytes 655360 | tf_op jit(solution)/shard_map/sum_over_z_lo/add | solution.py:209
  118.6 7.6 %all-to-all-start.4 = ((bf16[4,128,128]{2,1,0:T(8,128)(2,1)}), bf16[4,128,128]{2,1,0:T(8,128)(2,1)}, u32[]{:S(2)}, u32[]{:S(2)}) async-start(bf16[4,128,128]{2,1,0:T(8,128)(2,1)} %fusion.17), calls=%async_computation.4 | async-start | bytes 262144 | tf_op jit(solution)/shard_map/sum_over_z_hi/all_to_all | solution.py:287
  126.2 4.5 %collective-permute-done.11.refs_3_ = bf16[256,1024]{1,0:T(8,128)(2,1)S(1)} collective-permute-done((bf16[256,1024]{1,0:T(8,128)(2,1)S(1)}, bf16[256,1024]{1,0:T(8,128)(2,1)S(1)}, u32[]{:S(2)}, u32[]{:S(2)}) %collective-permute-start.11) | collective-permute-done | bytes 524320 | tf_op jit(solution)/shard_map/gather_over_x/ppermute | solution.py:278
  130.7 1.3 head_grad.1
  132.2 0.3 fusion.2
  132.5 0.9 fusion.7
  133.4 1.1 fusion.5
  134.5 6.1 %all-to-all-done.4 = bf16[4,128,128]{2,1,0:T(8,128)(2,1)} async-done(((bf16[4,128,128]{2,1,0:T(8,128)(2,1)}), bf16[4,128,128]{2,1,0:T(8,128)(2,1)}, u32[]{:S(2)}, u32[]{:S(2)}) %all-to-all-start.4) | async-done | bytes 131104 | tf_op jit(solution)/shard_map/sum_over_z_hi/all_to_all | solution.py:287
  140.6 0.8 add_bitcast_fusion
  141.4 5.8 %collective-permute-start.14 = (f32[128,128]{1,0:T(8,128)S(1)}, f32[128,128]{1,0:T(8,128)S(1)}, u32[]{:S(2)}, u32[]{:S(2)}) collective-permute-start(f32[128,128]{1,0:T(8,128)S(1)} %add_bitcast_fusion), channel_id=1, source_target_pairs={{0,0},{1,1},{2,2},{3,3},{4,128},{5,129},{6,130},{7,131},{8,256},{9... | collective-permute-start | bytes 196616 | tf_op jit(solution)/shard_map/sum_over_z_hi/ppermute | solution.py:289
  147.3 1.1 fusion.4
  148.3 10.4 %collective-permute-done.14 = f32[128,128]{1,0:T(8,128)S(1)} collective-permute-done((f32[128,128]{1,0:T(8,128)S(1)}, f32[128,128]{1,0:T(8,128)S(1)}, u32[]{:S(2)}, u32[]{:S(2)}) %collective-permute-start.14) | collective-permute-done | bytes 65568 | tf_op jit(solution)/shard_map/sum_over_z_hi/ppermute | solution.py:289
  158.7 0.6 copy.18
  (39 shorter events, 0.9 us)
Async XLA Ops:
  0.6 32.3 %copy-start = (bf16[1,1024,128]{2,1,0:T(8,128)(2,1)S(1)}, bf16[1,1024,128]{2,1,0:T(8,128)(2,1)}, u32[]{:S(2)}) copy-start(bf16[1,1024,128]{2,1,0:T(8,128)(2,1)} %param.10) | copy-start | bytes 786436
  0.6 10.5 %copy-start.8 = (bf16[128,128]{1,0:T(8,128)(2,1)S(1)}, bf16[128,128]{1,0:T(8,128)(2,1)}, u32[]{:S(2)}) copy-start(bf16[128,128]{1,0:T(8,128)(2,1)} %param.11) | copy-start | bytes 98308
  0.7 29.9 %copy-start.9 = (s32[1,2,8]{2,1,0:T(2,128)S(1)}, s32[1,2,8]{2,1,0:T(2,128)}, u32[]{:S(2)}) copy-start(s32[1,2,8]{2,1,0:T(2,128)} %param.12) | copy-start | bytes 196
  0.7 30.2 %copy-start.6 = (bf16[1,256,128]{2,1,0:T(8,128)(2,1)S(1)}, bf16[1,256,128]{2,1,0:T(8,128)(2,1)}, u32[]{:S(2)}) copy-start(bf16[1,256,128]{2,1,0:T(8,128)(2,1)} %param.8) | copy-start | bytes 196612
  2.2 31.8 %collective-permute-start = (bf16[256,1024]{1,0:T(8,128)(2,1)S(1)}, bf16[256,1024]{1,0:T(8,128)(2,1)S(1)}, u32[]{:S(2)}, u32[]{:S(2)}) collective-permute-start(bf16[256,1024]{1,0:T(8,128)(2,1)S(1)} %get-tuple-element.39), channel_id=1, source_target_pairs={{0,4},{1,5},{2,6},{3,7},{4,8},{5,9},{6,10},{7,11},{8,12},{9,13},{1... | collective-permute-start | bytes 1572872 | tf_op jit(solution)/shard_map/sum_over_x/ppermute | solution.py:229
  5.3 28.6 %collective-permute-start.1 = (bf16[256,1024]{1,0:T(8,128)(2,1)S(1)}, bf16[256,1024]{1,0:T(8,128)(2,1)S(1)}, u32[]{:S(2)}, u32[]{:S(2)}) collective-permute-start(bf16[256,1024]{1,0:T(8,128)(2,1)S(1)} %get-tuple-element.40), channel_id=1, source_target_pairs={{0,8},{1,9},{2,10},{3,11},{4,12},{5,13},{6,14},{7,15},{8,0},{9,1},... | collective-permute-start | bytes 1572872 | tf_op jit(solution)/shard_map/sum_over_x/ppermute | solution.py:229
  8.1 25.9 %collective-permute-start.2 = (bf16[256,1024]{1,0:T(8,128)(2,1)S(1)}, bf16[256,1024]{1,0:T(8,128)(2,1)S(1)}, u32[]{:S(2)}, u32[]{:S(2)}) collective-permute-start(bf16[256,1024]{1,0:T(8,128)(2,1)S(1)} %get-tuple-element.38), channel_id=1, source_target_pairs={{0,12},{1,13},{2,14},{3,15},{4,0},{5,1},{6,2},{7,3},{8,4},{9,5},{1... | collective-permute-start | bytes 1572872 | tf_op jit(solution)/shard_map/sum_over_x/ppermute | solution.py:229
  11.8 34.8 %all-to-all-start = ((bf16[4,128,128]{2,1,0:T(8,128)(2,1)}), bf16[4,128,128]{2,1,0:T(8,128)(2,1)}, u32[]{:S(2)}, u32[]{:S(2)}) async-start(bf16[4,128,128]{2,1,0:T(8,128)(2,1)} %broadcast_in_dim.51), calls=%async_computation | async-start | bytes 262144 | tf_op jit(solution)/shard_map/gather_projection/all_to_all | solution.py:234
  32.3 1.7 %copy-start.1 = (bf16[1,1,256,4096]{3,2,1,0:T(8,128)(2,1)S(1)}, bf16[1,1,256,4096]{3,2,1,0:T(8,128)(2,1)}, u32[]{:S(2)}) copy-start(bf16[1,1,256,4096]{3,2,1,0:T(8,128)(2,1)} %param.7) | copy-start | bytes 6291460
  32.9 1.1 copy-start.2
  46.6 19.6 %all-to-all-start.1 = ((bf16[8,32,1024]{2,1,0:T(8,128)(2,1)}), bf16[8,32,1024]{2,1,0:T(8,128)(2,1)S(1)}, u32[]{:S(2)}, u32[]{:S(2)}) async-start(bf16[8,32,1024]{2,1,0:T(8,128)(2,1)} %bitcast.13), calls=%async_computation.1 | async-start | bytes 1048576 | tf_op jit(solution)/shard_map/sum_over_y/all_to_all | solution.py:246
  54.8 11.6 %collective-permute-start.3 = (bf16[256,128]{1,0:T(8,128)(2,1)S(1)}, bf16[256,128]{1,0:T(8,128)(2,1)S(1)}, u32[]{:S(2)}, u32[]{:S(2)}) collective-permute-start(bf16[256,128]{1,0:T(8,128)(2,1)S(1)} %get-tuple-element.27.refs_0_), channel_id=1, source_target_pairs={{0,12},{1,13},{2,14},{3,15},{4,0},{5,1},{6,2},{7,3},{8,4},{9,5},{1... | collective-permute-start | bytes 196616 | tf_op jit(solution)/shard_map/gather_attended/ppermute | solution.py:254
  58.9 7.7 %collective-permute-start.4 = (bf16[256,128]{1,0:T(8,128)(2,1)S(1)}, bf16[256,128]{1,0:T(8,128)(2,1)S(1)}, u32[]{:S(2)}, u32[]{:S(2)}) collective-permute-start(bf16[256,128]{1,0:T(8,128)(2,1)S(1)} %get-tuple-element.27.refs_0_), channel_id=1, source_target_pairs={{0,8},{1,9},{2,10},{3,11},{4,12},{5,13},{6,14},{7,15},{8,0},{9,1},... | collective-permute-start | bytes 196616 | tf_op jit(solution)/shard_map/gather_attended/ppermute | solution.py:254
  61.7 6.4 %collective-permute-start.5 = (bf16[256,128]{1,0:T(8,128)(2,1)S(1)}, bf16[256,128]{1,0:T(8,128)(2,1)S(1)}, u32[]{:S(2)}, u32[]{:S(2)}) collective-permute-start(bf16[256,128]{1,0:T(8,128)(2,1)S(1)} %get-tuple-element.27.refs_0_), channel_id=1, source_target_pairs={{0,4},{1,5},{2,6},{3,7},{4,8},{5,9},{6,10},{7,11},{8,12},{9,13},{1... | collective-permute-start | bytes 196616 | tf_op jit(solution)/shard_map/gather_attended/ppermute | solution.py:254
  68.9 22.8 %all-to-all-start.2 = ((bf16[8,32,1024]{2,1,0:T(8,128)(2,1)}), bf16[8,32,1024]{2,1,0:T(8,128)(2,1)S(1)}, u32[]{:S(2)}, u32[]{:S(2)}) async-start(bf16[8,32,1024]{2,1,0:T(8,128)(2,1)} %broadcast_in_dim.53), calls=%async_computation.2 | async-start | bytes 1048576 | tf_op jit(solution)/shard_map/gather_over_y/all_to_all | solution.py:260
  76.2 9.8 %collective-permute-start.6 = (bf16[4,128,128]{2,1,0:T(8,128)(2,1)}, bf16[4,128,128]{2,1,0:T(8,128)(2,1)S(1)}, u32[]{:S(2)}, u32[]{:S(2)}) collective-permute-start(bf16[4,128,128]{2,1,0:T(8,128)(2,1)} %all-to-all-done), channel_id=1, source_target_pairs={{0,96},{16,112},{32,0},{48,16},{64,32},{80,48},{96,64},{112,80},{1... | collective-permute-start | bytes 393224 | tf_op jit(solution)/shard_map/gather_projection/ppermute | solution.py:264
  79.4 9.4 %collective-permute-start.7 = (bf16[4,128,128]{2,1,0:T(8,128)(2,1)}, bf16[4,128,128]{2,1,0:T(8,128)(2,1)S(1)}, u32[]{:S(2)}, u32[]{:S(2)}) collective-permute-start(bf16[4,128,128]{2,1,0:T(8,128)(2,1)} %all-to-all-done), channel_id=1, source_target_pairs={{0,64},{16,80},{32,96},{48,112},{64,0},{80,16},{96,32},{112,48},{1... | collective-permute-start | bytes 393224 | tf_op jit(solution)/shard_map/gather_projection/ppermute | solution.py:264
  81.9 8.9 %collective-permute-start.8 = (bf16[4,128,128]{2,1,0:T(8,128)(2,1)}, bf16[4,128,128]{2,1,0:T(8,128)(2,1)S(1)}, u32[]{:S(2)}, u32[]{:S(2)}) collective-permute-start(bf16[4,128,128]{2,1,0:T(8,128)(2,1)} %all-to-all-done), channel_id=1, source_target_pairs={{0,32},{16,48},{32,64},{48,80},{64,96},{80,112},{96,0},{112,16},{1... | collective-permute-start | bytes 393224 | tf_op jit(solution)/shard_map/gather_projection/ppermute | solution.py:264
  92.8 3.8 %collective-permute-start.13 = (bf16[4,4,128,128]{3,2,1,0:T(8,128)(2,1)S(1)}, bf16[4,4,128,128]{3,2,1,0:T(8,128)(2,1)S(1)}, u32[]{:S(2)}, u32[]{:S(2)}) collective-permute-start(bf16[4,4,128,128]{3,2,1,0:T(8,128)(2,1)S(1)} %get-tuple-element.32), channel_id=1, source_target_pairs={{0,16},{16,0},{32,48},{48,32},{64,80},{80,64},{96,112},{112,96},{1... | collective-permute-start | bytes 1572872 | tf_op jit(solution)/shard_map/sum_over_core/ppermute | solution.py:272
  97.5 19.3 %all-to-all-start.3 = ((bf16[4,4,128,128]{3,2,1,0:T(8,128)(2,1)}), bf16[4,4,128,128]{3,2,1,0:T(8,128)(2,1)}, u32[]{:S(2)}, u32[]{:S(2)}) async-start(bf16[4,4,128,128]{3,2,1,0:T(8,128)(2,1)} %add_convert_fusion), calls=%async_computation.3 | async-start | bytes 1048576 | tf_op jit(solution)/shard_map/sum_over_z_lo/all_to_all | solution.py:282
  101.7 30.4 %copy-start.4 = (f32[256,128]{1,0:T(8,128)S(1)}, f32[256,128]{1,0:T(8,128)}, u32[]{:S(2)}) copy-start(f32[256,128]{1,0:T(8,128)} %get-tuple-element.44) | copy-start | bytes 393220
  101.7 24.6 %collective-permute-start.10 = (bf16[256,1024]{1,0:T(8,128)(2,1)S(1)}, bf16[256,1024]{1,0:T(8,128)(2,1)S(1)}, u32[]{:S(2)}, u32[]{:S(2)}) collective-permute-start(bf16[256,1024]{1,0:T(8,128)(2,1)S(1)} %bitcast.61), channel_id=1, source_target_pairs={{0,8},{1,9},{2,10},{3,11},{4,12},{5,13},{6,14},{7,15},{8,0},{9,1},... | collective-permute-start | bytes 1572872 | tf_op jit(solution)/shard_map/gather_over_x/ppermute | solution.py:278
  107.3 23.4 %collective-permute-start.11 = (bf16[256,1024]{1,0:T(8,128)(2,1)S(1)}, bf16[256,1024]{1,0:T(8,128)(2,1)S(1)}, u32[]{:S(2)}, u32[]{:S(2)}) collective-permute-start(bf16[256,1024]{1,0:T(8,128)(2,1)S(1)} %bitcast.62), channel_id=1, source_target_pairs={{0,4},{1,5},{2,6},{3,7},{4,8},{5,9},{6,10},{7,11},{8,12},{9,13},{1... | collective-permute-start | bytes 1572872 | tf_op jit(solution)/shard_map/gather_over_x/ppermute | solution.py:278
  109.2 21.5 %collective-permute-start.12 = (bf16[4,4,128,128]{3,2,1,0:T(8,128)(2,1)S(1)}, bf16[4,4,128,128]{3,2,1,0:T(8,128)(2,1)S(1)}, u32[]{:S(2)}, u32[]{:S(2)}) collective-permute-start(bf16[4,4,128,128]{3,2,1,0:T(8,128)(2,1)S(1)} %pad_maximum_fusion.w_own_ref), channel_id=1, source_target_pairs={{0,16},{16,0},{32,48},{48,32},{64,80},{80,64},{96,112},{112,96},{1... | collective-permute-start | bytes 1572872 | tf_op jit(solution)/shard_map/gather_projection/ppermute | solution.py:275
  111.1 19.6 %collective-permute-start.9 = (bf16[256,1024]{1,0:T(8,128)(2,1)S(1)}, bf16[256,1024]{1,0:T(8,128)(2,1)S(1)}, u32[]{:S(2)}, u32[]{:S(2)}) collective-permute-start(bf16[256,1024]{1,0:T(8,128)(2,1)S(1)} %bitcast.63), channel_id=1, source_target_pairs={{0,12},{1,13},{2,14},{3,15},{4,0},{5,1},{6,2},{7,3},{8,4},{9,5},{1... | collective-permute-start | bytes 1572872 | tf_op jit(solution)/shard_map/gather_over_x/ppermute | solution.py:278
  118.6 22.0 %all-to-all-start.4 = ((bf16[4,128,128]{2,1,0:T(8,128)(2,1)}), bf16[4,128,128]{2,1,0:T(8,128)(2,1)}, u32[]{:S(2)}, u32[]{:S(2)}) async-start(bf16[4,128,128]{2,1,0:T(8,128)(2,1)} %fusion.17), calls=%async_computation.4 | async-start | bytes 262144 | tf_op jit(solution)/shard_map/sum_over_z_hi/all_to_all | solution.py:287
  126.2 5.9 %copy-start.3 = (f32[256,1024]{1,0:T(8,128)S(1)}, f32[256,1024]{1,0:T(8,128)}, u32[]{:S(2)}) copy-start(f32[256,1024]{1,0:T(8,128)} %copy-done.2) | copy-start | bytes 3145732
  126.2 6.3 %copy-start.5 = (bf16[1,1024,128]{2,1,0:T(8,128)(2,1)S(1)}, bf16[1,1024,128]{2,1,0:T(8,128)(2,1)}, u32[]{:S(2)}) copy-start(bf16[1,1024,128]{2,1,0:T(8,128)(2,1)} %param.9) | copy-start | bytes 786436
  132.1 15.1 %copy-start.7 = (bf16[1,256,128]{2,1,0:T(8,128)(2,1)S(1)}, bf16[1,256,128]{2,1,0:T(8,128)(2,1)}, u32[]{:S(2)}) copy-start(bf16[1,256,128]{2,1,0:T(8,128)(2,1)} %param.8) | copy-start | bytes 196612
  141.4 17.3 %collective-permute-start.14 = (f32[128,128]{1,0:T(8,128)S(1)}, f32[128,128]{1,0:T(8,128)S(1)}, u32[]{:S(2)}, u32[]{:S(2)}) collective-permute-start(f32[128,128]{1,0:T(8,128)S(1)} %add_bitcast_fusion), channel_id=1, source_target_pairs={{0,0},{1,1},{2,2},{3,3},{4,128},{5,129},{6,130},{7,131},{8,256},{9... | collective-permute-start | bytes 196616 | tf_op jit(solution)/shard_map/sum_over_z_hi/ppermute | solution.py:289

commit v7 on v6

--- a/solution.py
+++ b/solution.py
@@ -34,10 +34,8 @@
     ]
 
 
-def z_lo_groups():
-    return [
-        [scene_index(a, b, c) for b in range(ZL)] for a in range(ZH) for c in range(CORES)
-    ]
+def x_groups():
+    return [[x * YH + y for x in range(X)] for y in range(YH)]
 
 
 def z_hi_groups():
@@ -46,14 +44,14 @@
     ]
 
 
-def swap_x_zh():
+def to_owner(k):
     pairs = []
     for a in range(ZH):
         for rest in range(ZL * CORES):
             for x in range(X):
                 for yh in range(YH):
                     here = ((a * ZL * CORES + rest) * X + x) * YH + yh
-                    there = ((x * ZL * CORES + rest) * X + a) * YH + yh
+                    there = ((x * ZL * CORES + rest) * X + (a + k) % X) * YH + yh
                     pairs.append((here, there))
     return pairs
 
@@ -160,20 +158,18 @@
     )(place, block, *attended)
 
 
-def head_grad_kernel(place_ref, w_own_ref, w_other_ref, *refs):
-    *blocks, out_ref = refs
-    core, x, zl = [place_ref[i] for i in range(3)]
+def head_grad_kernel(place_ref, w_own_ref, w_other_ref, upstream_ref, out_ref):
+    core, zl = place_ref[0], place_ref[2]
     total = jnp.zeros(out_ref.shape, jnp.float32)
-    for k in range(X):
-        far = (x + k) & (X - 1)
+    for a in range(X):
         for b in range(ZL):
             near = (b - zl) & (ZL - 1)
             left = b * CORES * HEAD_DIM
-            own, other = w_own_ref[near, far], w_other_ref[near, far]
+            own, other = w_own_ref[near, a], w_other_ref[near, a]
             first, second = jnp.where(core == 0, own, other), jnp.where(core == 0, other, own)
             for c, weight in enumerate((first, second)):
                 total += lax.dot_general(
-                    blocks[k][:, left + c * HEAD_DIM : left + (c + 1) * HEAD_DIM],
+                    upstream_ref[a, :, left + c * HEAD_DIM : left + (c + 1) * HEAD_DIM],
                     weight,
                     (((1,), (1,)), ((), ())),
                     preferred_element_type=jnp.float32,
@@ -181,13 +177,13 @@
     out_ref[...] = total.astype(out_ref.dtype)
 
 
-def head_grad(place, blocks, w_own, w_other):
-    rows, width = blocks[0].shape
+def head_grad(place, upstream, w_own, w_other):
+    _, rows, width = upstream.shape
     vmem = pl.BlockSpec(memory_space=pltpu.VMEM)
     return pl.pallas_call(
         head_grad_kernel,
         out_shape=jax.ShapeDtypeStruct((rows, HEAD_DIM), jnp.bfloat16),
-        in_specs=[pl.BlockSpec(memory_space=pltpu.SMEM)] + [vmem] * (2 + X),
+        in_specs=[pl.BlockSpec(memory_space=pltpu.SMEM)] + [vmem] * 3,
         out_specs=vmem,
         compiler_params=pltpu.CompilerParams(vmem_limit_bytes=24 << 20),
         cost_estimate=pl.CostEstimate(
@@ -196,7 +192,7 @@
             transcendentals=0,
         ),
         name="head_grad",
-    )(place, w_own, w_other, *blocks)
+    )(place, w_own, w_other, upstream)
 
 
 def shift_right(number, size):
@@ -214,7 +210,7 @@
     scaling = 1.0 / math.sqrt(HEAD_DIM)
     section, mp, scene = (lax.axis_index(name) for name in ("section", "mp", "scene"))
     x, y = shift_right(mp, YH), (mp & (YH - 1)) * YL + section
-    zl = shift_right(scene, CORES) & (ZL - 1)
+    zh, zl = shift_right(scene, ZL * CORES), shift_right(scene, CORES) & (ZL - 1)
     core = scene & (CORES - 1)
     place = jnp.stack([core, x, zl])
     sample = dec_grad[0, 0]
@@ -274,19 +270,29 @@
     with jax.named_scope("gather_projection"):
         w_other = lax.ppermute(w_near, "scene", other_core())
 
+    pair, block = lax.optimization_barrier((pair, block))
     with jax.named_scope("gather_over_x"):
-        upstream = [block] + [lax.ppermute(block, "mp", shift_x(-k)) for k in range(1, X)]
+        spread = jnp.broadcast_to(block[None], (X, *block.shape))
+        upstream = lax.all_to_all(spread, "mp", 0, 0, axis_index_groups=x_groups())
 
     with jax.named_scope("sum_over_z_lo"):
+        parts = [
+            lax.dynamic_index_in_dim(pair, (zl + k) & (ZL - 1), 0, keepdims=False)
+            for k in range(ZL)
+        ]
         near = sum_f32(
-            lax.all_to_all(pair, "scene", 0, 0, axis_index_groups=z_lo_groups())
+            parts[:1] + [lax.ppermute(parts[k], "scene", shift_zl(k)) for k in range(1, ZL)]
         ).astype(jnp.bfloat16)
 
     with jax.named_scope("sum_over_z_hi"):
-        summed_block = sum_f32(
-            lax.all_to_all(near, "scene", 0, 0, axis_index_groups=z_hi_groups())
-        )
-        d_wout = lax.ppermute(summed_block, ("scene", "mp"), swap_x_zh())
+        terms = [
+            lax.ppermute(
+                lax.dynamic_index_in_dim(near, (zh + k) & (X - 1), 0, keepdims=False),
+                ("scene", "mp"),
+                to_owner(k),
+            )
+            for k in range(ZH)
+        ]
 
     with jax.named_scope("head_gradients"):
         upstream, w_other, _ = lax.optimization_barrier((upstream, w_other, near))
@@ -294,6 +300,8 @@
         d_queries, d_keys, d_values = attend_backward(
             queries, keys, values, d_attn, probs, weights, attended, scaling
         )
+        terms, d_queries = lax.optimization_barrier((terms, d_queries))
+        d_wout = sum_f32(terms)
     return d_queries[None], d_keys[None], d_values[None], d_wout
 
 

time: 160 us -> 164 us (1.025)
  the two profiles are of different devices: /device:TPU:12 before, /device:TPU:1 now
where the time goes in v7:
time: 164 us; the launch traced here: 163 us
  starting transfers between devices  109 us (66%)
  waiting for transfers between devices  29.8 us (18%)
  local copies, waits for them, and re-layouts  7.56 us (5%)
  matrix products  5.76 us (4%)
  other arithmetic  5.48 us (3%)
  Pallas kernels  3.41 us (2%)
  between operations  1.73 us (1%)
    ppermute x4, starting transfers between devices, shards(): lax.ppermute(lax.dynamic_index_in_dim(near, zh + k & X - 1, 0, keepdims=F...  23.8 us
    all_to_all x1, starting transfers between devices, shards(): lax.all_to_all(w_spread, 'scene', 0, 0, axis_index_groups=z_hi_groups())  18.4 us
    ppermute x3, starting transfers between devices, shards(): lax.ppermute(piece, 'mp', shift_x(k + 1))  11.4 us
    ppermute x3, starting transfers between devices, shards(): lax.ppermute(w_far, 'scene', shift_zl(-k))  9.96 us
    ppermute x3, starting transfers between devices, shards(): lax.ppermute(parts[k], 'scene', shift_zl(k))  9.87 us
    all_to_all x1, waiting for transfers between devices, shards(): lax.all_to_all(w_spread, 'scene', 0, 0, axis_index_groups=z_hi_groups())  8.84 us
    ppermute x3, waiting for transfers between devices, shards(): lax.ppermute(parts[k], 'scene', shift_zl(k))  8.55 us
    ppermute x1, starting transfers between devices, shards(): lax.ppermute(send, 'scene', other_core())  8.4 us
  transfers between devices with their start and end apart: 22, of which 8 were waited for; matrix products, arithmetic and copies ran while one was open for 8% of the time, Pallas kernels for 1%

profile of v7, /device:TPU:1, one launch (start us, length us, event | category | flops | bytes accessed | tf_op | source)
XLA Modules:
  0.0 162.6 jit_solution(13975685335175557407)
XLA Ops:
  0.7 1.5 dynamic-slice_bitcast_fusion
  2.2 3.9 %collective-permute-start = (bf16[256,1024]{1,0:T(8,128)(2,1)S(1)}, bf16[256,1024]{1,0:T(8,128)(2,1)S(1)}, u32[]{:S(2)}, u32[]{:S(2)}) collective-permute-start(bf16[256,1024]{1,0:T(8,128)(2,1)S(1)} %get-tuple-element.47), channel_id=1, source_target_pairs={{0,4},{1,5},{2,6},{3,7},{4,8},{5,9},{6,10},{7,11},{8,12},{9,13},{1... | collective-permute-start | bytes 1572872 | tf_op jit(solution)/shard_map/sum_over_x/ppermute | solution.py:225
  6.2 4.4 %collective-permute-start.1 = (bf16[256,1024]{1,0:T(8,128)(2,1)S(1)}, bf16[256,1024]{1,0:T(8,128)(2,1)S(1)}, u32[]{:S(2)}, u32[]{:S(2)}) collective-permute-start(bf16[256,1024]{1,0:T(8,128)(2,1)S(1)} %get-tuple-element.48), channel_id=1, source_target_pairs={{0,8},{1,9},{2,10},{3,11},{4,12},{5,13},{6,14},{7,15},{8,0},{9,1},... | collective-permute-start | bytes 1572872 | tf_op jit(solution)/shard_map/sum_over_x/ppermute | solution.py:225
  10.6 3.1 %collective-permute-start.2 = (bf16[256,1024]{1,0:T(8,128)(2,1)S(1)}, bf16[256,1024]{1,0:T(8,128)(2,1)S(1)}, u32[]{:S(2)}, u32[]{:S(2)}) collective-permute-start(bf16[256,1024]{1,0:T(8,128)(2,1)S(1)} %get-tuple-element.46), channel_id=1, source_target_pairs={{0,12},{1,13},{2,14},{3,15},{4,0},{5,1},{6,2},{7,3},{8,4},{9,5},{1... | collective-permute-start | bytes 1572872 | tf_op jit(solution)/shard_map/sum_over_x/ppermute | solution.py:225
  13.6 0.7 broadcast_in_dim.54
  14.3 18.4 %all-to-all-start = ((bf16[4,128,128]{2,1,0:T(8,128)(2,1)}), bf16[4,128,128]{2,1,0:T(8,128)(2,1)}, u32[]{:S(2)}, u32[]{:S(2)}) async-start(bf16[4,128,128]{2,1,0:T(8,128)(2,1)} %broadcast_in_dim.54), calls=%async_computation | async-start | bytes 262144 | tf_op jit(solution)/shard_map/gather_projection/all_to_all | solution.py:230
  33.1 1.4 fusion.21
  35.1 1.0 fusion.22
  36.2 1.1 add_own.1
  37.3 8.8 %all-to-all-done = bf16[4,128,128]{2,1,0:T(8,128)(2,1)} async-done(((bf16[4,128,128]{2,1,0:T(8,128)(2,1)}), bf16[4,128,128]{2,1,0:T(8,128)(2,1)}, u32[]{:S(2)}, u32[]{:S(2)}) %all-to-all-start) | async-done | bytes 131104 | tf_op jit(solution)/shard_map/gather_projection/all_to_all | solution.py:230
  46.1 6.8 %all-to-all-start.1 = ((bf16[8,32,1024]{2,1,0:T(8,128)(2,1)}), bf16[8,32,1024]{2,1,0:T(8,128)(2,1)S(1)}, u32[]{:S(2)}, u32[]{:S(2)}) async-start(bf16[8,32,1024]{2,1,0:T(8,128)(2,1)} %bitcast.13), calls=%async_computation.1 | async-start | bytes 1048576 | tf_op jit(solution)/shard_map/sum_over_y/all_to_all | solution.py:242
  53.6 1.9 %collective-permute-start.3 = (bf16[256,128]{1,0:T(8,128)(2,1)S(1)}, bf16[256,128]{1,0:T(8,128)(2,1)S(1)}, u32[]{:S(2)}, u32[]{:S(2)}) collective-permute-start(bf16[256,128]{1,0:T(8,128)(2,1)S(1)} %get-tuple-element.30.refs_0_), channel_id=1, source_target_pairs={{0,12},{1,13},{2,14},{3,15},{4,0},{5,1},{6,2},{7,3},{8,4},{9,5},{1... | collective-permute-start | bytes 196616 | tf_op jit(solution)/shard_map/gather_attended/ppermute | solution.py:250
  55.6 4.0 %collective-permute-start.4 = (bf16[256,128]{1,0:T(8,128)(2,1)S(1)}, bf16[256,128]{1,0:T(8,128)(2,1)S(1)}, u32[]{:S(2)}, u32[]{:S(2)}) collective-permute-start(bf16[256,128]{1,0:T(8,128)(2,1)S(1)} %get-tuple-element.30.refs_0_), channel_id=1, source_target_pairs={{0,8},{1,9},{2,10},{3,11},{4,12},{5,13},{6,14},{7,15},{8,0},{9,1},... | collective-permute-start | bytes 196616 | tf_op jit(solution)/shard_map/gather_attended/ppermute | solution.py:250
  59.6 1.9 %collective-permute-start.5 = (bf16[256,128]{1,0:T(8,128)(2,1)S(1)}, bf16[256,128]{1,0:T(8,128)(2,1)S(1)}, u32[]{:S(2)}, u32[]{:S(2)}) collective-permute-start(bf16[256,128]{1,0:T(8,128)(2,1)S(1)} %get-tuple-element.30.refs_0_), channel_id=1, source_target_pairs={{0,4},{1,5},{2,6},{3,7},{4,8},{5,9},{6,10},{7,11},{8,12},{9,13},{1... | collective-permute-start | bytes 196616 | tf_op jit(solution)/shard_map/gather_attended/ppermute | solution.py:250
  61.5 3.1 %all-to-all-done.1 = bf16[8,32,1024]{2,1,0:T(8,128)(2,1)S(1)} async-done(((bf16[8,32,1024]{2,1,0:T(8,128)(2,1)}), bf16[8,32,1024]{2,1,0:T(8,128)(2,1)S(1)}, u32[]{:S(2)}, u32[]{:S(2)}) %all-to-all-start.1) | async-done | bytes 524320 | tf_op jit(solution)/shard_map/sum_over_y/all_to_all | solution.py:242
  64.8 1.3 collective-permute-done.5.refs_3_
  66.1 0.9 broadcast_in_dim.59
  67.0 6.5 %all-to-all-start.2 = ((bf16[8,32,1024]{2,1,0:T(8,128)(2,1)}), bf16[8,32,1024]{2,1,0:T(8,128)(2,1)S(1)}, u32[]{:S(2)}, u32[]{:S(2)}) async-start(bf16[8,32,1024]{2,1,0:T(8,128)(2,1)} %broadcast_in_dim.59), calls=%async_computation.2 | async-start | bytes 1048576 | tf_op jit(solution)/shard_map/gather_over_y/all_to_all | solution.py:256
  73.5 1.9 %collective-permute-start.8 = (bf16[4,128,128]{2,1,0:T(8,128)(2,1)}, bf16[4,128,128]{2,1,0:T(8,128)(2,1)S(1)}, u32[]{:S(2)}, u32[]{:S(2)}) collective-permute-start(bf16[4,128,128]{2,1,0:T(8,128)(2,1)} %all-to-all-done), channel_id=1, source_target_pairs={{0,32},{16,48},{32,64},{48,80},{64,96},{80,112},{96,0},{112,16},{1... | collective-permute-start | bytes 393224 | tf_op jit(solution)/shard_map/gather_projection/ppermute | solution.py:260
  75.4 5.6 %collective-permute-start.7 = (bf16[4,128,128]{2,1,0:T(8,128)(2,1)}, bf16[4,128,128]{2,1,0:T(8,128)(2,1)S(1)}, u32[]{:S(2)}, u32[]{:S(2)}) collective-permute-start(bf16[4,128,128]{2,1,0:T(8,128)(2,1)} %all-to-all-done), channel_id=1, source_target_pairs={{0,64},{16,80},{32,96},{48,112},{64,0},{80,16},{96,32},{112,48},{1... | collective-permute-start | bytes 393224 | tf_op jit(solution)/shard_map/gather_projection/ppermute | solution.py:260
  81.0 2.5 %collective-permute-start.6 = (bf16[4,128,128]{2,1,0:T(8,128)(2,1)}, bf16[4,128,128]{2,1,0:T(8,128)(2,1)S(1)}, u32[]{:S(2)}, u32[]{:S(2)}) collective-permute-start(bf16[4,128,128]{2,1,0:T(8,128)(2,1)} %all-to-all-done), channel_id=1, source_target_pairs={{0,96},{16,112},{32,0},{48,16},{64,32},{80,48},{96,64},{112,80},{1... | collective-permute-start | bytes 393224 | tf_op jit(solution)/shard_map/gather_projection/ppermute | solution.py:260
  83.5 1.4 collective-permute-done.7
  84.9 2.3 %collective-permute-done.6 = bf16[4,128,128]{2,1,0:T(8,128)(2,1)S(1)} collective-permute-done((bf16[4,128,128]{2,1,0:T(8,128)(2,1)}, bf16[4,128,128]{2,1,0:T(8,128)(2,1)S(1)}, u32[]{:S(2)}, u32[]{:S(2)}) %collective-permute-start.6) | collective-permute-done | bytes 131104 | tf_op jit(solution)/shard_map/gather_projection/ppermute | solution.py:260
  87.2 1.0 pad_maximum_fusion.w_own_ref
  88.2 1.0 weight_terms.1
  89.2 8.4 %collective-permute-start.9 = (bf16[4,4,128,128]{3,2,1,0:T(8,128)(2,1)S(1)}, bf16[4,4,128,128]{3,2,1,0:T(8,128)(2,1)S(1)}, u32[]{:S(2)}, u32[]{:S(2)}) collective-permute-start(bf16[4,4,128,128]{3,2,1,0:T(8,128)(2,1)S(1)} %get-tuple-element.35), channel_id=1, source_target_pairs={{0,16},{16,0},{32,48},{48,32},{64,80},{80,64},{96,112},{112,96},{1... | collective-permute-start | bytes 1572872 | tf_op jit(solution)/shard_map/sum_over_core/ppermute | solution.py:268
  97.6 1.5 collective-permute-done.9
  99.1 0.9 add_convert_fusion
  100.1 1.6 broadcast_in_dim.60
  101.7 3.6 %all-to-all-start.3 = ((bf16[4,256,1024]{2,1,0:T(8,128)(2,1)}), bf16[4,256,1024]{2,1,0:T(8,128)(2,1)S(1)}, u32[]{:S(2)}, u32[]{:S(2)}) async-start(bf16[4,256,1024]{2,1,0:T(8,128)(2,1)} %broadcast_in_dim.60), calls=%async_computation.3 | async-start | bytes 4194304 | tf_op jit(solution)/shard_map/gather_over_x/all_to_all | solution.py:276
  105.3 2.3 %collective-permute-start.17 = (bf16[4,4,128,128]{3,2,1,0:T(8,128)(2,1)S(1)}, bf16[4,4,128,128]{3,2,1,0:T(8,128)(2,1)S(1)}, u32[]{:S(2)}, u32[]{:S(2)}) collective-permute-start(bf16[4,4,128,128]{3,2,1,0:T(8,128)(2,1)S(1)} %pad_maximum_fusion.w_own_ref), channel_id=1, source_target_pairs={{0,16},{16,0},{32,48},{48,32},{64,80},{80,64},{96,112},{112,96},{1... | collective-permute-start | bytes 1572872 | tf_op jit(solution)/shard_map/gather_projection/ppermute | solution.py:271
  107.6 1.8 %dynamic-slice_bitcast_fusion.5 = (bf16[4,128,128]{2,1,0:T(8,128)(2,1)S(1)}, bf16[4,128,128]{2,1,0:T(8,128)(2,1)}, bf16[4,128,128]{2,1,0:T(8,128)(2,1)}) fusion(bf16[4,4,128,128]{3,2,1,0:T(8,128)(2,1)} %add_convert_fusion, s32[]{:T(128)S(6)} %select_n.49, s32[]{:T(128)S(6)} %select_n.51, s32[]{:T(128)S(6)} %select_n.50), kind=kLoop, calls=%fused_computation.35 | loop fusion | bytes 786444 | tf_op jit(solution)/shard_map/sum_over_z_lo/jit(dynamic_index_in_dim)/squeeze | solution.py:280
  109.4 5.8 %collective-permute-start.12 = (bf16[4,128,128]{2,1,0:T(8,128)(2,1)}, bf16[4,128,128]{2,1,0:T(8,128)(2,1)}, u32[]{:S(2)}, u32[]{:S(2)}) collective-permute-start(bf16[4,128,128]{2,1,0:T(8,128)(2,1)} %get-tuple-element.50), channel_id=1, source_target_pairs={{0,96},{16,112},{32,0},{48,16},{64,32},{80,48},{96,64},{112,80},{1... | collective-permute-start | bytes 393224 | tf_op jit(solution)/shard_map/sum_over_z_lo/ppermute | solution.py:284
  115.1 1.9 %collective-permute-start.11 = (bf16[4,128,128]{2,1,0:T(8,128)(2,1)}, bf16[4,128,128]{2,1,0:T(8,128)(2,1)}, u32[]{:S(2)}, u32[]{:S(2)}) collective-permute-start(bf16[4,128,128]{2,1,0:T(8,128)(2,1)} %get-tuple-element.51), channel_id=1, source_target_pairs={{0,64},{16,80},{32,96},{48,112},{64,0},{80,16},{96,32},{112,48},{1... | collective-permute-start | bytes 393224 | tf_op jit(solution)/shard_map/sum_over_z_lo/ppermute | solution.py:284
  117.1 2.2 %collective-permute-start.10 = (bf16[4,128,128]{2,1,0:T(8,128)(2,1)S(1)}, bf16[4,128,128]{2,1,0:T(8,128)(2,1)}, u32[]{:S(2)}, u32[]{:S(2)}) collective-permute-start(bf16[4,128,128]{2,1,0:T(8,128)(2,1)S(1)} %get-tuple-element.49), channel_id=1, source_target_pairs={{0,32},{16,48},{32,64},{48,80},{64,96},{80,112},{96,0},{112,16},{1... | collective-permute-start | bytes 393224 | tf_op jit(solution)/shard_map/sum_over_z_lo/ppermute | solution.py:284
  119.3 8.5 %collective-permute-done.11 = bf16[4,128,128]{2,1,0:T(8,128)(2,1)} collective-permute-done((bf16[4,128,128]{2,1,0:T(8,128)(2,1)}, bf16[4,128,128]{2,1,0:T(8,128)(2,1)}, u32[]{:S(2)}, u32[]{:S(2)}) %collective-permute-start.11) | collective-permute-done | bytes 131104 | tf_op jit(solution)/shard_map/sum_over_z_lo/ppermute | solution.py:284
  127.8 1.2 fusion.11
  129.0 0.7 dynamic-slice_bitcast_fusion.6
  129.7 2.0 %collective-permute-start.13 = (bf16[128,128]{1,0:T(8,128)(2,1)}, bf16[128,128]{1,0:T(8,128)(2,1)}, u32[]{:S(2)}, u32[]{:S(2)}) collective-permute-start(bf16[128,128]{1,0:T(8,128)(2,1)} %get-tuple-element.55), channel_id=1, source_target_pairs={{0,0},{1,1},{2,2},{3,3},{4,128},{5,129},{6,130},{7,131},{8,256},{9... | collective-permute-start | bytes 98312 | tf_op jit(solution)/shard_map/sum_over_z_hi/ppermute | solution.py:289
  131.7 3.5 %collective-permute-start.14 = (bf16[128,128]{1,0:T(8,128)(2,1)}, bf16[128,128]{1,0:T(8,128)(2,1)}, u32[]{:S(2)}, u32[]{:S(2)}) collective-permute-start(bf16[128,128]{1,0:T(8,128)(2,1)} %get-tuple-element.54), channel_id=1, source_target_pairs={{0,4},{1,5},{2,6},{3,7},{4,132},{5,133},{6,134},{7,135},{8,260},{9... | collective-permute-start | bytes 98312 | tf_op jit(solution)/shard_map/sum_over_z_hi/ppermute | solution.py:289
  135.2 9.1 %collective-permute-start.15 = (bf16[128,128]{1,0:T(8,128)(2,1)}, bf16[128,128]{1,0:T(8,128)(2,1)}, u32[]{:S(2)}, u32[]{:S(2)}) collective-permute-start(bf16[128,128]{1,0:T(8,128)(2,1)} %get-tuple-element.53), channel_id=1, source_target_pairs={{0,8},{1,9},{2,10},{3,11},{4,136},{5,137},{6,138},{7,139},{8,264},... | collective-permute-start | bytes 98312 | tf_op jit(solution)/shard_map/sum_over_z_hi/ppermute | solution.py:289
  144.3 9.2 %collective-permute-start.16 = (bf16[128,128]{1,0:T(8,128)(2,1)}, bf16[128,128]{1,0:T(8,128)(2,1)}, u32[]{:S(2)}, u32[]{:S(2)}) collective-permute-start(bf16[128,128]{1,0:T(8,128)(2,1)} %get-tuple-element.52), channel_id=1, source_target_pairs={{0,12},{1,13},{2,14},{3,15},{4,140},{5,141},{6,142},{7,143},{8,268... | collective-permute-start | bytes 98312 | tf_op jit(solution)/shard_map/sum_over_z_hi/ppermute | solution.py:289
  153.6 1.3 head_grad.1
  154.9 1.1 fusion.5
  156.4 0.9 fusion.6
  157.4 1.1 fusion.4
  158.4 2.8 %collective-permute-done.16 = bf16[128,128]{1,0:T(8,128)(2,1)} collective-permute-done((bf16[128,128]{1,0:T(8,128)(2,1)}, bf16[128,128]{1,0:T(8,128)(2,1)}, u32[]{:S(2)}, u32[]{:S(2)}) %collective-permute-start.16) | collective-permute-done | bytes 32800 | tf_op jit(solution)/shard_map/sum_over_z_hi/ppermute | solution.py:289
  161.2 1.5 convert_add_fusion.1
  (45 shorter events, 1.7 us)
Async XLA Ops:
  0.6 34.5 %copy-start = (bf16[1,1024,128]{2,1,0:T(8,128)(2,1)S(1)}, bf16[1,1024,128]{2,1,0:T(8,128)(2,1)}, u32[]{:S(2)}) copy-start(bf16[1,1024,128]{2,1,0:T(8,128)(2,1)} %param.10) | copy-start | bytes 786436
  0.6 13.0 %copy-start.8 = (bf16[128,128]{1,0:T(8,128)(2,1)S(1)}, bf16[128,128]{1,0:T(8,128)(2,1)}, u32[]{:S(2)}) copy-start(bf16[128,128]{1,0:T(8,128)(2,1)} %param.11) | copy-start | bytes 98308
  0.7 32.1 %copy-start.9 = (s32[1,2,8]{2,1,0:T(2,128)S(1)}, s32[1,2,8]{2,1,0:T(2,128)}, u32[]{:S(2)}) copy-start(s32[1,2,8]{2,1,0:T(2,128)} %param.12) | copy-start | bytes 196
  0.7 32.5 %copy-start.6 = (bf16[1,256,128]{2,1,0:T(8,128)(2,1)S(1)}, bf16[1,256,128]{2,1,0:T(8,128)(2,1)}, u32[]{:S(2)}) copy-start(bf16[1,256,128]{2,1,0:T(8,128)(2,1)} %param.8) | copy-start | bytes 196612
  2.2 33.9 %collective-permute-start = (bf16[256,1024]{1,0:T(8,128)(2,1)S(1)}, bf16[256,1024]{1,0:T(8,128)(2,1)S(1)}, u32[]{:S(2)}, u32[]{:S(2)}) collective-permute-start(bf16[256,1024]{1,0:T(8,128)(2,1)S(1)} %get-tuple-element.47), channel_id=1, source_target_pairs={{0,4},{1,5},{2,6},{3,7},{4,8},{5,9},{6,10},{7,11},{8,12},{9,13},{1... | collective-permute-start | bytes 1572872 | tf_op jit(solution)/shard_map/sum_over_x/ppermute | solution.py:225
  6.2 30.0 %collective-permute-start.1 = (bf16[256,1024]{1,0:T(8,128)(2,1)S(1)}, bf16[256,1024]{1,0:T(8,128)(2,1)S(1)}, u32[]{:S(2)}, u32[]{:S(2)}) collective-permute-start(bf16[256,1024]{1,0:T(8,128)(2,1)S(1)} %get-tuple-element.48), channel_id=1, source_target_pairs={{0,8},{1,9},{2,10},{3,11},{4,12},{5,13},{6,14},{7,15},{8,0},{9,1},... | collective-permute-start | bytes 1572872 | tf_op jit(solution)/shard_map/sum_over_x/ppermute | solution.py:225
  10.6 25.6 %collective-permute-start.2 = (bf16[256,1024]{1,0:T(8,128)(2,1)S(1)}, bf16[256,1024]{1,0:T(8,128)(2,1)S(1)}, u32[]{:S(2)}, u32[]{:S(2)}) collective-permute-start(bf16[256,1024]{1,0:T(8,128)(2,1)S(1)} %get-tuple-element.46), channel_id=1, source_target_pairs={{0,12},{1,13},{2,14},{3,15},{4,0},{5,1},{6,2},{7,3},{8,4},{9,5},{1... | collective-permute-start | bytes 1572872 | tf_op jit(solution)/shard_map/sum_over_x/ppermute | solution.py:225
  14.3 31.8 %all-to-all-start = ((bf16[4,128,128]{2,1,0:T(8,128)(2,1)}), bf16[4,128,128]{2,1,0:T(8,128)(2,1)}, u32[]{:S(2)}, u32[]{:S(2)}) async-start(bf16[4,128,128]{2,1,0:T(8,128)(2,1)} %broadcast_in_dim.54), calls=%async_computation | async-start | bytes 262144 | tf_op jit(solution)/shard_map/gather_projection/all_to_all | solution.py:230
  34.5 1.7 %copy-start.1 = (bf16[1,1,256,4096]{3,2,1,0:T(8,128)(2,1)S(1)}, bf16[1,1,256,4096]{3,2,1,0:T(8,128)(2,1)}, u32[]{:S(2)}) copy-start(bf16[1,1,256,4096]{3,2,1,0:T(8,128)(2,1)} %param.7) | copy-start | bytes 6291460
  35.1 1.1 copy-start.2
  46.1 18.4 %all-to-all-start.1 = ((bf16[8,32,1024]{2,1,0:T(8,128)(2,1)}), bf16[8,32,1024]{2,1,0:T(8,128)(2,1)S(1)}, u32[]{:S(2)}, u32[]{:S(2)}) async-start(bf16[8,32,1024]{2,1,0:T(8,128)(2,1)} %bitcast.13), calls=%async_computation.1 | async-start | bytes 1048576 | tf_op jit(solution)/shard_map/sum_over_y/all_to_all | solution.py:242
  53.6 11.1 %collective-permute-start.3 = (bf16[256,128]{1,0:T(8,128)(2,1)S(1)}, bf16[256,128]{1,0:T(8,128)(2,1)S(1)}, u32[]{:S(2)}, u32[]{:S(2)}) collective-permute-start(bf16[256,128]{1,0:T(8,128)(2,1)S(1)} %get-tuple-element.30.refs_0_), channel_id=1, source_target_pairs={{0,12},{1,13},{2,14},{3,15},{4,0},{5,1},{6,2},{7,3},{8,4},{9,5},{1... | collective-permute-start | bytes 196616 | tf_op jit(solution)/shard_map/gather_attended/ppermute | solution.py:250
  55.6 9.2 %collective-permute-start.4 = (bf16[256,128]{1,0:T(8,128)(2,1)S(1)}, bf16[256,128]{1,0:T(8,128)(2,1)S(1)}, u32[]{:S(2)}, u32[]{:S(2)}) collective-permute-start(bf16[256,128]{1,0:T(8,128)(2,1)S(1)} %get-tuple-element.30.refs_0_), channel_id=1, source_target_pairs={{0,8},{1,9},{2,10},{3,11},{4,12},{5,13},{6,14},{7,15},{8,0},{9,1},... | collective-permute-start | bytes 196616 | tf_op jit(solution)/shard_map/gather_attended/ppermute | solution.py:250
  59.6 6.5 %collective-permute-start.5 = (bf16[256,128]{1,0:T(8,128)(2,1)S(1)}, bf16[256,128]{1,0:T(8,128)(2,1)S(1)}, u32[]{:S(2)}, u32[]{:S(2)}) collective-permute-start(bf16[256,128]{1,0:T(8,128)(2,1)S(1)} %get-tuple-element.30.refs_0_), channel_id=1, source_target_pairs={{0,4},{1,5},{2,6},{3,7},{4,8},{5,9},{6,10},{7,11},{8,12},{9,13},{1... | collective-permute-start | bytes 196616 | tf_op jit(solution)/shard_map/gather_attended/ppermute | solution.py:250
  67.0 21.2 %all-to-all-start.2 = ((bf16[8,32,1024]{2,1,0:T(8,128)(2,1)}), bf16[8,32,1024]{2,1,0:T(8,128)(2,1)S(1)}, u32[]{:S(2)}, u32[]{:S(2)}) async-start(bf16[8,32,1024]{2,1,0:T(8,128)(2,1)} %broadcast_in_dim.59), calls=%async_computation.2 | async-start | bytes 1048576 | tf_op jit(solution)/shard_map/gather_over_y/all_to_all | solution.py:256
  73.5 10.1 %collective-permute-start.8 = (bf16[4,128,128]{2,1,0:T(8,128)(2,1)}, bf16[4,128,128]{2,1,0:T(8,128)(2,1)S(1)}, u32[]{:S(2)}, u32[]{:S(2)}) collective-permute-start(bf16[4,128,128]{2,1,0:T(8,128)(2,1)} %all-to-all-done), channel_id=1, source_target_pairs={{0,32},{16,48},{32,64},{48,80},{64,96},{80,112},{96,0},{112,16},{1... | collective-permute-start | bytes 393224 | tf_op jit(solution)/shard_map/gather_projection/ppermute | solution.py:260
  75.4 9.5 %collective-permute-start.7 = (bf16[4,128,128]{2,1,0:T(8,128)(2,1)}, bf16[4,128,128]{2,1,0:T(8,128)(2,1)S(1)}, u32[]{:S(2)}, u32[]{:S(2)}) collective-permute-start(bf16[4,128,128]{2,1,0:T(8,128)(2,1)} %all-to-all-done), channel_id=1, source_target_pairs={{0,64},{16,80},{32,96},{48,112},{64,0},{80,16},{96,32},{112,48},{1... | collective-permute-start | bytes 393224 | tf_op jit(solution)/shard_map/gather_projection/ppermute | solution.py:260
  81.0 6.2 %collective-permute-start.6 = (bf16[4,128,128]{2,1,0:T(8,128)(2,1)}, bf16[4,128,128]{2,1,0:T(8,128)(2,1)S(1)}, u32[]{:S(2)}, u32[]{:S(2)}) collective-permute-start(bf16[4,128,128]{2,1,0:T(8,128)(2,1)} %all-to-all-done), channel_id=1, source_target_pairs={{0,96},{16,112},{32,0},{48,16},{64,32},{80,48},{96,64},{112,80},{1... | collective-permute-start | bytes 393224 | tf_op jit(solution)/shard_map/gather_projection/ppermute | solution.py:260
  89.2 9.9 %collective-permute-start.9 = (bf16[4,4,128,128]{3,2,1,0:T(8,128)(2,1)S(1)}, bf16[4,4,128,128]{3,2,1,0:T(8,128)(2,1)S(1)}, u32[]{:S(2)}, u32[]{:S(2)}) collective-permute-start(bf16[4,4,128,128]{3,2,1,0:T(8,128)(2,1)S(1)} %get-tuple-element.35), channel_id=1, source_target_pairs={{0,16},{16,0},{32,48},{48,32},{64,80},{80,64},{96,112},{112,96},{1... | collective-permute-start | bytes 1572872 | tf_op jit(solution)/shard_map/sum_over_core/ppermute | solution.py:268
  101.7 51.9 %all-to-all-start.3 = ((bf16[4,256,1024]{2,1,0:T(8,128)(2,1)}), bf16[4,256,1024]{2,1,0:T(8,128)(2,1)S(1)}, u32[]{:S(2)}, u32[]{:S(2)}) async-start(bf16[4,256,1024]{2,1,0:T(8,128)(2,1)} %broadcast_in_dim.60), calls=%async_computation.3 | async-start | bytes 4194304 | tf_op jit(solution)/shard_map/gather_over_x/all_to_all | solution.py:276
  105.3 48.2 %collective-permute-start.17 = (bf16[4,4,128,128]{3,2,1,0:T(8,128)(2,1)S(1)}, bf16[4,4,128,128]{3,2,1,0:T(8,128)(2,1)S(1)}, u32[]{:S(2)}, u32[]{:S(2)}) collective-permute-start(bf16[4,4,128,128]{3,2,1,0:T(8,128)(2,1)S(1)} %pad_maximum_fusion.w_own_ref), channel_id=1, source_target_pairs={{0,16},{16,0},{32,48},{48,32},{64,80},{80,64},{96,112},{112,96},{1... | collective-permute-start | bytes 1572872 | tf_op jit(solution)/shard_map/gather_projection/ppermute | solution.py:271
  109.4 9.9 %collective-permute-start.12 = (bf16[4,128,128]{2,1,0:T(8,128)(2,1)}, bf16[4,128,128]{2,1,0:T(8,128)(2,1)}, u32[]{:S(2)}, u32[]{:S(2)}) collective-permute-start(bf16[4,128,128]{2,1,0:T(8,128)(2,1)} %get-tuple-element.50), channel_id=1, source_target_pairs={{0,96},{16,112},{32,0},{48,16},{64,32},{80,48},{96,64},{112,80},{1... | collective-permute-start | bytes 393224 | tf_op jit(solution)/shard_map/sum_over_z_lo/ppermute | solution.py:284
  115.1 12.7 %collective-permute-start.11 = (bf16[4,128,128]{2,1,0:T(8,128)(2,1)}, bf16[4,128,128]{2,1,0:T(8,128)(2,1)}, u32[]{:S(2)}, u32[]{:S(2)}) collective-permute-start(bf16[4,128,128]{2,1,0:T(8,128)(2,1)} %get-tuple-element.51), channel_id=1, source_target_pairs={{0,64},{16,80},{32,96},{48,112},{64,0},{80,16},{96,32},{112,48},{1... | collective-permute-start | bytes 393224 | tf_op jit(solution)/shard_map/sum_over_z_lo/ppermute | solution.py:284
  117.1 10.8 %collective-permute-start.10 = (bf16[4,128,128]{2,1,0:T(8,128)(2,1)S(1)}, bf16[4,128,128]{2,1,0:T(8,128)(2,1)}, u32[]{:S(2)}, u32[]{:S(2)}) collective-permute-start(bf16[4,128,128]{2,1,0:T(8,128)(2,1)S(1)} %get-tuple-element.49), channel_id=1, source_target_pairs={{0,32},{16,48},{32,64},{48,80},{64,96},{80,112},{96,0},{112,16},{1... | collective-permute-start | bytes 393224 | tf_op jit(solution)/shard_map/sum_over_z_lo/ppermute | solution.py:284
  129.7 28.7 %collective-permute-start.13 = (bf16[128,128]{1,0:T(8,128)(2,1)}, bf16[128,128]{1,0:T(8,128)(2,1)}, u32[]{:S(2)}, u32[]{:S(2)}) collective-permute-start(bf16[128,128]{1,0:T(8,128)(2,1)} %get-tuple-element.55), channel_id=1, source_target_pairs={{0,0},{1,1},{2,2},{3,3},{4,128},{5,129},{6,130},{7,131},{8,256},{9... | collective-permute-start | bytes 98312 | tf_op jit(solution)/shard_map/sum_over_z_hi/ppermute | solution.py:289
  131.7 26.7 %collective-permute-start.14 = (bf16[128,128]{1,0:T(8,128)(2,1)}, bf16[128,128]{1,0:T(8,128)(2,1)}, u32[]{:S(2)}, u32[]{:S(2)}) collective-permute-start(bf16[128,128]{1,0:T(8,128)(2,1)} %get-tuple-element.54), channel_id=1, source_target_pairs={{0,4},{1,5},{2,6},{3,7},{4,132},{5,133},{6,134},{7,135},{8,260},{9... | collective-permute-start | bytes 98312 | tf_op jit(solution)/shard_map/sum_over_z_hi/ppermute | solution.py:289
  135.2 23.2 %collective-permute-start.15 = (bf16[128,128]{1,0:T(8,128)(2,1)}, bf16[128,128]{1,0:T(8,128)(2,1)}, u32[]{:S(2)}, u32[]{:S(2)}) collective-permute-start(bf16[128,128]{1,0:T(8,128)(2,1)} %get-tuple-element.53), channel_id=1, source_target_pairs={{0,8},{1,9},{2,10},{3,11},{4,136},{5,137},{6,138},{7,139},{8,264},... | collective-permute-start | bytes 98312 | tf_op jit(solution)/shard_map/sum_over_z_hi/ppermute | solution.py:289
  144.3 11.7 %copy-start.4 = (f32[256,128]{1,0:T(8,128)S(1)}, f32[256,128]{1,0:T(8,128)}, u32[]{:S(2)}) copy-start(f32[256,128]{1,0:T(8,128)} %get-tuple-element.59) | copy-start | bytes 393220
  144.3 16.9 %collective-permute-start.16 = (bf16[128,128]{1,0:T(8,128)(2,1)}, bf16[128,128]{1,0:T(8,128)(2,1)}, u32[]{:S(2)}, u32[]{:S(2)}) collective-permute-start(bf16[128,128]{1,0:T(8,128)(2,1)} %get-tuple-element.52), channel_id=1, source_target_pairs={{0,12},{1,13},{2,14},{3,15},{4,140},{5,141},{6,142},{7,143},{8,268... | collective-permute-start | bytes 98312 | tf_op jit(solution)/shard_map/sum_over_z_hi/ppermute | solution.py:289
  153.6 1.3 copy-start.3
  154.9 1.5 copy-start.5
  154.9 2.4 %copy-start.7 = (bf16[1,256,128]{2,1,0:T(8,128)(2,1)S(1)}, bf16[1,256,128]{2,1,0:T(8,128)(2,1)}, u32[]{:S(2)}) copy-start(bf16[1,256,128]{2,1,0:T(8,128)(2,1)} %param.8) | copy-start | bytes 196612

commit v8 on v6

--- a/solution.py
+++ b/solution.py
@@ -286,7 +286,8 @@
         summed_block = sum_f32(
             lax.all_to_all(near, "scene", 0, 0, axis_index_groups=z_hi_groups())
         )
-        d_wout = lax.ppermute(summed_block, ("scene", "mp"), swap_x_zh())
+        rounded = summed_block.astype(jnp.bfloat16)
+        d_wout = lax.ppermute(rounded, ("scene", "mp"), swap_x_zh()).astype(jnp.float32)
 
     with jax.named_scope("head_gradients"):
         upstream, w_other, _ = lax.optimization_barrier((upstream, w_other, near))

time: 160 us -> 160 us (level)
  no operation moved by 1% of the time
where the time goes in v8:
time: 160 us; the launch traced here: 159 us
  starting transfers between devices  96.2 us (60%)
  waiting for transfers between devices  42.4 us (26%)
  other arithmetic  6.12 us (4%)
  matrix products  5.8 us (4%)
  local copies, waits for them, and re-layouts  3.48 us (2%)
  Pallas kernels  3.33 us (2%)
  between operations  1.67 us (1%)
    all_to_all x1, starting transfers between devices, shards(): lax.all_to_all(w_spread, 'scene', 0, 0, axis_index_groups=z_hi_groups())  18.7 us
    all_to_all x1, waiting for transfers between devices, shards(): lax.all_to_all(w_spread, 'scene', 0, 0, axis_index_groups=z_hi_groups())  11.5 us
    ppermute x3, starting transfers between devices, shards(): lax.ppermute(block, 'mp', shift_x(-k))  11.5 us
    ppermute x3, starting transfers between devices, shards(): lax.ppermute(attended_rounded, 'mp', shift_x(-k))  11.4 us
    ppermute x1, waiting for transfers between devices, shards(): lax.ppermute(rounded, ('scene', 'mp'), swap_x_zh()).astype(jnp.float32)  10 us
    ppermute x3, starting transfers between devices, shards(): lax.ppermute(w_far, 'scene', shift_zl(-k))  9.64 us
    ppermute x3, starting transfers between devices, shards(): lax.ppermute(piece, 'mp', shift_x(k + 1))  8.86 us
    all_to_all x1, starting transfers between devices, shards(): lax.all_to_all(near, 'scene', 0, 0, axis_index_groups=z_hi_groups())  7.61 us
  transfers between devices with their start and end apart: 20, of which 10 were waited for; matrix products, arithmetic and copies ran while one was open for 7% of the time, Pallas kernels for 1%

profile of v8, /device:TPU:12, one launch (start us, length us, event | category | flops | bytes accessed | tf_op | source)
XLA Modules:
  0.0 159.0 jit_solution(11236247213992226852)
XLA Ops:
  0.7 1.5 dynamic-slice_bitcast_fusion
  2.2 3.1 %collective-permute-start = (bf16[256,1024]{1,0:T(8,128)(2,1)S(1)}, bf16[256,1024]{1,0:T(8,128)(2,1)S(1)}, u32[]{:S(2)}, u32[]{:S(2)}) collective-permute-start(bf16[256,1024]{1,0:T(8,128)(2,1)S(1)} %get-tuple-element.39), channel_id=1, source_target_pairs={{0,4},{1,5},{2,6},{3,7},{4,8},{5,9},{6,10},{7,11},{8,12},{9,13},{1... | collective-permute-start | bytes 1572872 | tf_op jit(solution)/shard_map/sum_over_x/ppermute | solution.py:229
  5.3 2.7 %collective-permute-start.1 = (bf16[256,1024]{1,0:T(8,128)(2,1)S(1)}, bf16[256,1024]{1,0:T(8,128)(2,1)S(1)}, u32[]{:S(2)}, u32[]{:S(2)}) collective-permute-start(bf16[256,1024]{1,0:T(8,128)(2,1)S(1)} %get-tuple-element.40), channel_id=1, source_target_pairs={{0,8},{1,9},{2,10},{3,11},{4,12},{5,13},{6,14},{7,15},{8,0},{9,1},... | collective-permute-start | bytes 1572872 | tf_op jit(solution)/shard_map/sum_over_x/ppermute | solution.py:229
  8.1 3.0 %collective-permute-start.2 = (bf16[256,1024]{1,0:T(8,128)(2,1)S(1)}, bf16[256,1024]{1,0:T(8,128)(2,1)S(1)}, u32[]{:S(2)}, u32[]{:S(2)}) collective-permute-start(bf16[256,1024]{1,0:T(8,128)(2,1)S(1)} %get-tuple-element.38), channel_id=1, source_target_pairs={{0,12},{1,13},{2,14},{3,15},{4,0},{5,1},{6,2},{7,3},{8,4},{9,5},{1... | collective-permute-start | bytes 1572872 | tf_op jit(solution)/shard_map/sum_over_x/ppermute | solution.py:229
  11.1 0.7 broadcast_in_dim.51
  11.8 18.7 %all-to-all-start = ((bf16[4,128,128]{2,1,0:T(8,128)(2,1)}), bf16[4,128,128]{2,1,0:T(8,128)(2,1)}, u32[]{:S(2)}, u32[]{:S(2)}) async-start(bf16[4,128,128]{2,1,0:T(8,128)(2,1)} %broadcast_in_dim.51), calls=%async_computation | async-start | bytes 262144 | tf_op jit(solution)/shard_map/gather_projection/all_to_all | solution.py:234
  30.6 0.3 broadcast_in_dim.48
  30.9 1.4 fusion.21
  32.3 0.3 fusion.9
  32.9 1.1 fusion.22
  34.0 1.1 add_own.1
  35.1 11.5 %all-to-all-done = bf16[4,128,128]{2,1,0:T(8,128)(2,1)} async-done(((bf16[4,128,128]{2,1,0:T(8,128)(2,1)}), bf16[4,128,128]{2,1,0:T(8,128)(2,1)}, u32[]{:S(2)}, u32[]{:S(2)}) %all-to-all-start) | async-done | bytes 131104 | tf_op jit(solution)/shard_map/gather_projection/all_to_all | solution.py:234
  46.6 7.5 %all-to-all-start.1 = ((bf16[8,32,1024]{2,1,0:T(8,128)(2,1)}), bf16[8,32,1024]{2,1,0:T(8,128)(2,1)S(1)}, u32[]{:S(2)}, u32[]{:S(2)}) async-start(bf16[8,32,1024]{2,1,0:T(8,128)(2,1)} %bitcast.13), calls=%async_computation.1 | async-start | bytes 1048576 | tf_op jit(solution)/shard_map/sum_over_y/all_to_all | solution.py:246
  54.8 4.1 %collective-permute-start.3 = (bf16[256,128]{1,0:T(8,128)(2,1)S(1)}, bf16[256,128]{1,0:T(8,128)(2,1)S(1)}, u32[]{:S(2)}, u32[]{:S(2)}) collective-permute-start(bf16[256,128]{1,0:T(8,128)(2,1)S(1)} %get-tuple-element.27.refs_0_), channel_id=1, source_target_pairs={{0,12},{1,13},{2,14},{3,15},{4,0},{5,1},{6,2},{7,3},{8,4},{9,5},{1... | collective-permute-start | bytes 196616 | tf_op jit(solution)/shard_map/gather_attended/ppermute | solution.py:254
  58.9 2.8 %collective-permute-start.4 = (bf16[256,128]{1,0:T(8,128)(2,1)S(1)}, bf16[256,128]{1,0:T(8,128)(2,1)S(1)}, u32[]{:S(2)}, u32[]{:S(2)}) collective-permute-start(bf16[256,128]{1,0:T(8,128)(2,1)S(1)} %get-tuple-element.27.refs_0_), channel_id=1, source_target_pairs={{0,8},{1,9},{2,10},{3,11},{4,12},{5,13},{6,14},{7,15},{8,0},{9,1},... | collective-permute-start | bytes 196616 | tf_op jit(solution)/shard_map/gather_attended/ppermute | solution.py:254
  61.7 4.5 %collective-permute-start.5 = (bf16[256,128]{1,0:T(8,128)(2,1)S(1)}, bf16[256,128]{1,0:T(8,128)(2,1)S(1)}, u32[]{:S(2)}, u32[]{:S(2)}) collective-permute-start(bf16[256,128]{1,0:T(8,128)(2,1)S(1)} %get-tuple-element.27.refs_0_), channel_id=1, source_target_pairs={{0,4},{1,5},{2,6},{3,7},{4,8},{5,9},{6,10},{7,11},{8,12},{9,13},{1... | collective-permute-start | bytes 196616 | tf_op jit(solution)/shard_map/gather_attended/ppermute | solution.py:254
  66.5 1.6 collective-permute-done.5.refs_3_
  68.1 0.9 broadcast_in_dim.53
  68.9 7.2 %all-to-all-start.2 = ((bf16[8,32,1024]{2,1,0:T(8,128)(2,1)}), bf16[8,32,1024]{2,1,0:T(8,128)(2,1)S(1)}, u32[]{:S(2)}, u32[]{:S(2)}) async-start(bf16[8,32,1024]{2,1,0:T(8,128)(2,1)} %broadcast_in_dim.53), calls=%async_computation.2 | async-start | bytes 1048576 | tf_op jit(solution)/shard_map/gather_over_y/all_to_all | solution.py:260
  76.2 3.3 %collective-permute-start.6 = (bf16[4,128,128]{2,1,0:T(8,128)(2,1)}, bf16[4,128,128]{2,1,0:T(8,128)(2,1)S(1)}, u32[]{:S(2)}, u32[]{:S(2)}) collective-permute-start(bf16[4,128,128]{2,1,0:T(8,128)(2,1)} %all-to-all-done), channel_id=1, source_target_pairs={{0,96},{16,112},{32,0},{48,16},{64,32},{80,48},{96,64},{112,80},{1... | collective-permute-start | bytes 393224 | tf_op jit(solution)/shard_map/gather_projection/ppermute | solution.py:264
  79.4 2.5 %collective-permute-start.7 = (bf16[4,128,128]{2,1,0:T(8,128)(2,1)}, bf16[4,128,128]{2,1,0:T(8,128)(2,1)S(1)}, u32[]{:S(2)}, u32[]{:S(2)}) collective-permute-start(bf16[4,128,128]{2,1,0:T(8,128)(2,1)} %all-to-all-done), channel_id=1, source_target_pairs={{0,64},{16,80},{32,96},{48,112},{64,0},{80,16},{96,32},{112,48},{1... | collective-permute-start | bytes 393224 | tf_op jit(solution)/shard_map/gather_projection/ppermute | solution.py:264
  81.9 3.9 %collective-permute-start.8 = (bf16[4,128,128]{2,1,0:T(8,128)(2,1)}, bf16[4,128,128]{2,1,0:T(8,128)(2,1)S(1)}, u32[]{:S(2)}, u32[]{:S(2)}) collective-permute-start(bf16[4,128,128]{2,1,0:T(8,128)(2,1)} %all-to-all-done), channel_id=1, source_target_pairs={{0,32},{16,48},{32,64},{48,80},{64,96},{80,112},{96,0},{112,16},{1... | collective-permute-start | bytes 393224 | tf_op jit(solution)/shard_map/gather_projection/ppermute | solution.py:264
  85.9 2.9 %collective-permute-done.7 = bf16[4,128,128]{2,1,0:T(8,128)(2,1)S(1)} collective-permute-done((bf16[4,128,128]{2,1,0:T(8,128)(2,1)}, bf16[4,128,128]{2,1,0:T(8,128)(2,1)S(1)}, u32[]{:S(2)}, u32[]{:S(2)}) %collective-permute-start.7) | collective-permute-done | bytes 131104 | tf_op jit(solution)/shard_map/gather_projection/ppermute | solution.py:264
  88.8 2.0 %collective-permute-done.8 = bf16[4,128,128]{2,1,0:T(8,128)(2,1)S(1)} collective-permute-done((bf16[4,128,128]{2,1,0:T(8,128)(2,1)}, bf16[4,128,128]{2,1,0:T(8,128)(2,1)S(1)}, u32[]{:S(2)}, u32[]{:S(2)}) %collective-permute-start.8) | collective-permute-done | bytes 131104 | tf_op jit(solution)/shard_map/gather_projection/ppermute | solution.py:264
  90.8 1.0 pad_maximum_fusion.w_own_ref
  91.7 1.0 weight_terms.1
  92.8 1.9 %collective-permute-start.13 = (bf16[4,4,128,128]{3,2,1,0:T(8,128)(2,1)S(1)}, bf16[4,4,128,128]{3,2,1,0:T(8,128)(2,1)S(1)}, u32[]{:S(2)}, u32[]{:S(2)}) collective-permute-start(bf16[4,4,128,128]{3,2,1,0:T(8,128)(2,1)S(1)} %get-tuple-element.32), channel_id=1, source_target_pairs={{0,16},{16,0},{32,48},{48,32},{64,80},{80,64},{96,112},{112,96},{1... | collective-permute-start | bytes 1572872 | tf_op jit(solution)/shard_map/sum_over_core/ppermute | solution.py:272
  94.7 1.9 %collective-permute-done.13 = bf16[4,4,128,128]{3,2,1,0:T(8,128)(2,1)S(1)} collective-permute-done((bf16[4,4,128,128]{3,2,1,0:T(8,128)(2,1)S(1)}, bf16[4,4,128,128]{3,2,1,0:T(8,128)(2,1)S(1)}, u32[]{:S(2)}, u32[]{:S(2)}) %collective-permute-start.13) | collective-permute-done | bytes 524320 | tf_op jit(solution)/shard_map/sum_over_core/ppermute | solution.py:272
  96.6 0.9 add_convert_fusion
  97.5 4.1 %all-to-all-start.3 = ((bf16[4,4,128,128]{3,2,1,0:T(8,128)(2,1)}), bf16[4,4,128,128]{3,2,1,0:T(8,128)(2,1)}, u32[]{:S(2)}, u32[]{:S(2)}) async-start(bf16[4,4,128,128]{3,2,1,0:T(8,128)(2,1)} %add_convert_fusion), calls=%async_computation.3 | async-start | bytes 1048576 | tf_op jit(solution)/shard_map/sum_over_z_lo/all_to_all | solution.py:282
  101.7 5.6 %collective-permute-start.10 = (bf16[256,1024]{1,0:T(8,128)(2,1)S(1)}, bf16[256,1024]{1,0:T(8,128)(2,1)S(1)}, u32[]{:S(2)}, u32[]{:S(2)}) collective-permute-start(bf16[256,1024]{1,0:T(8,128)(2,1)S(1)} %bitcast.61), channel_id=1, source_target_pairs={{0,8},{1,9},{2,10},{3,11},{4,12},{5,13},{6,14},{7,15},{8,0},{9,1},... | collective-permute-start | bytes 1572872 | tf_op jit(solution)/shard_map/gather_over_x/ppermute | solution.py:278
  107.3 1.9 %collective-permute-start.11 = (bf16[256,1024]{1,0:T(8,128)(2,1)S(1)}, bf16[256,1024]{1,0:T(8,128)(2,1)S(1)}, u32[]{:S(2)}, u32[]{:S(2)}) collective-permute-start(bf16[256,1024]{1,0:T(8,128)(2,1)S(1)} %bitcast.62), channel_id=1, source_target_pairs={{0,4},{1,5},{2,6},{3,7},{4,8},{5,9},{6,10},{7,11},{8,12},{9,13},{1... | collective-permute-start | bytes 1572872 | tf_op jit(solution)/shard_map/gather_over_x/ppermute | solution.py:278
  109.2 1.9 %collective-permute-start.12 = (bf16[4,4,128,128]{3,2,1,0:T(8,128)(2,1)S(1)}, bf16[4,4,128,128]{3,2,1,0:T(8,128)(2,1)S(1)}, u32[]{:S(2)}, u32[]{:S(2)}) collective-permute-start(bf16[4,4,128,128]{3,2,1,0:T(8,128)(2,1)S(1)} %pad_maximum_fusion.w_own_ref), channel_id=1, source_target_pairs={{0,16},{16,0},{32,48},{48,32},{64,80},{80,64},{96,112},{112,96},{1... | collective-permute-start | bytes 1572872 | tf_op jit(solution)/shard_map/gather_projection/ppermute | solution.py:275
  111.1 3.9 %collective-permute-start.9 = (bf16[256,1024]{1,0:T(8,128)(2,1)S(1)}, bf16[256,1024]{1,0:T(8,128)(2,1)S(1)}, u32[]{:S(2)}, u32[]{:S(2)}) collective-permute-start(bf16[256,1024]{1,0:T(8,128)(2,1)S(1)} %bitcast.63), channel_id=1, source_target_pairs={{0,12},{1,13},{2,14},{3,15},{4,0},{5,1},{6,2},{7,3},{8,4},{9,5},{1... | collective-permute-start | bytes 1572872 | tf_op jit(solution)/shard_map/gather_over_x/ppermute | solution.py:278
  115.1 1.7 %all-to-all-done.3 = bf16[4,4,128,128]{3,2,1,0:T(8,128)(2,1)} async-done(((bf16[4,4,128,128]{3,2,1,0:T(8,128)(2,1)}), bf16[4,4,128,128]{3,2,1,0:T(8,128)(2,1)}, u32[]{:S(2)}, u32[]{:S(2)}) %all-to-all-start.3) | async-done | bytes 524320 | tf_op jit(solution)/shard_map/sum_over_z_lo/all_to_all | solution.py:282
  116.8 1.8 %fusion.17 = bf16[4,128,128]{2,1,0:T(8,128)(2,1)} fusion(bf16[4,4,128,128]{3,2,1,0:T(8,128)(2,1)} %all-to-all-done.3), kind=kLoop, calls=%fused_computation.30 | loop fusion | flops 524288 | bytes 655360 | tf_op jit(solution)/shard_map/sum_over_z_lo/add | solution.py:209
  118.6 7.6 %all-to-all-start.4 = ((bf16[4,128,128]{2,1,0:T(8,128)(2,1)}), bf16[4,128,128]{2,1,0:T(8,128)(2,1)}, u32[]{:S(2)}, u32[]{:S(2)}) async-start(bf16[4,128,128]{2,1,0:T(8,128)(2,1)} %fusion.17), calls=%async_computation.4 | async-start | bytes 262144 | tf_op jit(solution)/shard_map/sum_over_z_hi/all_to_all | solution.py:287
  126.2 4.5 %collective-permute-done.11.refs_3_ = bf16[256,1024]{1,0:T(8,128)(2,1)S(1)} collective-permute-done((bf16[256,1024]{1,0:T(8,128)(2,1)S(1)}, bf16[256,1024]{1,0:T(8,128)(2,1)S(1)}, u32[]{:S(2)}, u32[]{:S(2)}) %collective-permute-start.11) | collective-permute-done | bytes 524320 | tf_op jit(solution)/shard_map/gather_over_x/ppermute | solution.py:278
  130.7 1.3 head_grad.1
  132.2 0.3 fusion.2
  132.5 0.9 fusion.7
  133.4 1.1 fusion.5
  134.5 6.1 %all-to-all-done.4 = bf16[4,128,128]{2,1,0:T(8,128)(2,1)} async-done(((bf16[4,128,128]{2,1,0:T(8,128)(2,1)}), bf16[4,128,128]{2,1,0:T(8,128)(2,1)}, u32[]{:S(2)}, u32[]{:S(2)}) %all-to-all-start.4) | async-done | bytes 131104 | tf_op jit(solution)/shard_map/sum_over_z_hi/all_to_all | solution.py:287
  140.6 0.8 fusion.20
  141.4 5.8 %collective-permute-start.14 = (bf16[128,128]{1,0:T(8,128)(2,1)S(1)}, bf16[128,128]{1,0:T(8,128)(2,1)S(1)}, u32[]{:S(2)}, u32[]{:S(2)}) collective-permute-start(bf16[128,128]{1,0:T(8,128)(2,1)S(1)} %fusion.20), channel_id=1, source_target_pairs={{0,0},{1,1},{2,2},{3,3},{4,128},{5,129},{6,130},{7,131},{8,256},{9... | collective-permute-start | bytes 98312 | tf_op jit(solution)/shard_map/sum_over_z_hi/ppermute | solution.py:290
  147.3 1.1 fusion.4
  148.3 10.0 %collective-permute-done.14 = bf16[128,128]{1,0:T(8,128)(2,1)S(1)} collective-permute-done((bf16[128,128]{1,0:T(8,128)(2,1)S(1)}, bf16[128,128]{1,0:T(8,128)(2,1)S(1)}, u32[]{:S(2)}, u32[]{:S(2)}) %collective-permute-start.14) | collective-permute-done | bytes 32800 | tf_op jit(solution)/shard_map/sum_over_z_hi/ppermute | solution.py:290
  158.4 0.6 convert_element_type.89
  (39 shorter events, 0.9 us)
Async XLA Ops:
  0.6 32.3 %copy-start = (bf16[1,1024,128]{2,1,0:T(8,128)(2,1)S(1)}, bf16[1,1024,128]{2,1,0:T(8,128)(2,1)}, u32[]{:S(2)}) copy-start(bf16[1,1024,128]{2,1,0:T(8,128)(2,1)} %param.10) | copy-start | bytes 786436
  0.6 10.5 %copy-start.8 = (bf16[128,128]{1,0:T(8,128)(2,1)S(1)}, bf16[128,128]{1,0:T(8,128)(2,1)}, u32[]{:S(2)}) copy-start(bf16[128,128]{1,0:T(8,128)(2,1)} %param.11) | copy-start | bytes 98308
  0.7 29.9 %copy-start.9 = (s32[1,2,8]{2,1,0:T(2,128)S(1)}, s32[1,2,8]{2,1,0:T(2,128)}, u32[]{:S(2)}) copy-start(s32[1,2,8]{2,1,0:T(2,128)} %param.12) | copy-start | bytes 196
  0.7 30.2 %copy-start.6 = (bf16[1,256,128]{2,1,0:T(8,128)(2,1)S(1)}, bf16[1,256,128]{2,1,0:T(8,128)(2,1)}, u32[]{:S(2)}) copy-start(bf16[1,256,128]{2,1,0:T(8,128)(2,1)} %param.8) | copy-start | bytes 196612
  2.2 31.8 %collective-permute-start = (bf16[256,1024]{1,0:T(8,128)(2,1)S(1)}, bf16[256,1024]{1,0:T(8,128)(2,1)S(1)}, u32[]{:S(2)}, u32[]{:S(2)}) collective-permute-start(bf16[256,1024]{1,0:T(8,128)(2,1)S(1)} %get-tuple-element.39), channel_id=1, source_target_pairs={{0,4},{1,5},{2,6},{3,7},{4,8},{5,9},{6,10},{7,11},{8,12},{9,13},{1... | collective-permute-start | bytes 1572872 | tf_op jit(solution)/shard_map/sum_over_x/ppermute | solution.py:229
  5.3 28.6 %collective-permute-start.1 = (bf16[256,1024]{1,0:T(8,128)(2,1)S(1)}, bf16[256,1024]{1,0:T(8,128)(2,1)S(1)}, u32[]{:S(2)}, u32[]{:S(2)}) collective-permute-start(bf16[256,1024]{1,0:T(8,128)(2,1)S(1)} %get-tuple-element.40), channel_id=1, source_target_pairs={{0,8},{1,9},{2,10},{3,11},{4,12},{5,13},{6,14},{7,15},{8,0},{9,1},... | collective-permute-start | bytes 1572872 | tf_op jit(solution)/shard_map/sum_over_x/ppermute | solution.py:229
  8.1 25.9 %collective-permute-start.2 = (bf16[256,1024]{1,0:T(8,128)(2,1)S(1)}, bf16[256,1024]{1,0:T(8,128)(2,1)S(1)}, u32[]{:S(2)}, u32[]{:S(2)}) collective-permute-start(bf16[256,1024]{1,0:T(8,128)(2,1)S(1)} %get-tuple-element.38), channel_id=1, source_target_pairs={{0,12},{1,13},{2,14},{3,15},{4,0},{5,1},{6,2},{7,3},{8,4},{9,5},{1... | collective-permute-start | bytes 1572872 | tf_op jit(solution)/shard_map/sum_over_x/ppermute | solution.py:229
  11.8 34.8 %all-to-all-start = ((bf16[4,128,128]{2,1,0:T(8,128)(2,1)}), bf16[4,128,128]{2,1,0:T(8,128)(2,1)}, u32[]{:S(2)}, u32[]{:S(2)}) async-start(bf16[4,128,128]{2,1,0:T(8,128)(2,1)} %broadcast_in_dim.51), calls=%async_computation | async-start | bytes 262144 | tf_op jit(solution)/shard_map/gather_projection/all_to_all | solution.py:234
  32.3 1.7 %copy-start.1 = (bf16[1,1,256,4096]{3,2,1,0:T(8,128)(2,1)S(1)}, bf16[1,1,256,4096]{3,2,1,0:T(8,128)(2,1)}, u32[]{:S(2)}) copy-start(bf16[1,1,256,4096]{3,2,1,0:T(8,128)(2,1)} %param.7) | copy-start | bytes 6291460
  32.9 1.1 copy-start.2
  46.6 19.6 %all-to-all-start.1 = ((bf16[8,32,1024]{2,1,0:T(8,128)(2,1)}), bf16[8,32,1024]{2,1,0:T(8,128)(2,1)S(1)}, u32[]{:S(2)}, u32[]{:S(2)}) async-start(bf16[8,32,1024]{2,1,0:T(8,128)(2,1)} %bitcast.13), calls=%async_computation.1 | async-start | bytes 1048576 | tf_op jit(solution)/shard_map/sum_over_y/all_to_all | solution.py:246
  54.8 11.6 %collective-permute-start.3 = (bf16[256,128]{1,0:T(8,128)(2,1)S(1)}, bf16[256,128]{1,0:T(8,128)(2,1)S(1)}, u32[]{:S(2)}, u32[]{:S(2)}) collective-permute-start(bf16[256,128]{1,0:T(8,128)(2,1)S(1)} %get-tuple-element.27.refs_0_), channel_id=1, source_target_pairs={{0,12},{1,13},{2,14},{3,15},{4,0},{5,1},{6,2},{7,3},{8,4},{9,5},{1... | collective-permute-start | bytes 196616 | tf_op jit(solution)/shard_map/gather_attended/ppermute | solution.py:254
  58.9 7.7 %collective-permute-start.4 = (bf16[256,128]{1,0:T(8,128)(2,1)S(1)}, bf16[256,128]{1,0:T(8,128)(2,1)S(1)}, u32[]{:S(2)}, u32[]{:S(2)}) collective-permute-start(bf16[256,128]{1,0:T(8,128)(2,1)S(1)} %get-tuple-element.27.refs_0_), channel_id=1, source_target_pairs={{0,8},{1,9},{2,10},{3,11},{4,12},{5,13},{6,14},{7,15},{8,0},{9,1},... | collective-permute-start | bytes 196616 | tf_op jit(solution)/shard_map/gather_attended/ppermute | solution.py:254
  61.7 6.4 %collective-permute-start.5 = (bf16[256,128]{1,0:T(8,128)(2,1)S(1)}, bf16[256,128]{1,0:T(8,128)(2,1)S(1)}, u32[]{:S(2)}, u32[]{:S(2)}) collective-permute-start(bf16[256,128]{1,0:T(8,128)(2,1)S(1)} %get-tuple-element.27.refs_0_), channel_id=1, source_target_pairs={{0,4},{1,5},{2,6},{3,7},{4,8},{5,9},{6,10},{7,11},{8,12},{9,13},{1... | collective-permute-start | bytes 196616 | tf_op jit(solution)/shard_map/gather_attended/ppermute | solution.py:254
  68.9 22.8 %all-to-all-start.2 = ((bf16[8,32,1024]{2,1,0:T(8,128)(2,1)}), bf16[8,32,1024]{2,1,0:T(8,128)(2,1)S(1)}, u32[]{:S(2)}, u32[]{:S(2)}) async-start(bf16[8,32,1024]{2,1,0:T(8,128)(2,1)} %broadcast_in_dim.53), calls=%async_computation.2 | async-start | bytes 1048576 | tf_op jit(solution)/shard_map/gather_over_y/all_to_all | solution.py:260
  76.2 9.8 %collective-permute-start.6 = (bf16[4,128,128]{2,1,0:T(8,128)(2,1)}, bf16[4,128,128]{2,1,0:T(8,128)(2,1)S(1)}, u32[]{:S(2)}, u32[]{:S(2)}) collective-permute-start(bf16[4,128,128]{2,1,0:T(8,128)(2,1)} %all-to-all-done), channel_id=1, source_target_pairs={{0,96},{16,112},{32,0},{48,16},{64,32},{80,48},{96,64},{112,80},{1... | collective-permute-start | bytes 393224 | tf_op jit(solution)/shard_map/gather_projection/ppermute | solution.py:264
  79.4 9.4 %collective-permute-start.7 = (bf16[4,128,128]{2,1,0:T(8,128)(2,1)}, bf16[4,128,128]{2,1,0:T(8,128)(2,1)S(1)}, u32[]{:S(2)}, u32[]{:S(2)}) collective-permute-start(bf16[4,128,128]{2,1,0:T(8,128)(2,1)} %all-to-all-done), channel_id=1, source_target_pairs={{0,64},{16,80},{32,96},{48,112},{64,0},{80,16},{96,32},{112,48},{1... | collective-permute-start | bytes 393224 | tf_op jit(solution)/shard_map/gather_projection/ppermute | solution.py:264
  81.9 8.9 %collective-permute-start.8 = (bf16[4,128,128]{2,1,0:T(8,128)(2,1)}, bf16[4,128,128]{2,1,0:T(8,128)(2,1)S(1)}, u32[]{:S(2)}, u32[]{:S(2)}) collective-permute-start(bf16[4,128,128]{2,1,0:T(8,128)(2,1)} %all-to-all-done), channel_id=1, source_target_pairs={{0,32},{16,48},{32,64},{48,80},{64,96},{80,112},{96,0},{112,16},{1... | collective-permute-start | bytes 393224 | tf_op jit(solution)/shard_map/gather_projection/ppermute | solution.py:264
  92.8 3.8 %collective-permute-start.13 = (bf16[4,4,128,128]{3,2,1,0:T(8,128)(2,1)S(1)}, bf16[4,4,128,128]{3,2,1,0:T(8,128)(2,1)S(1)}, u32[]{:S(2)}, u32[]{:S(2)}) collective-permute-start(bf16[4,4,128,128]{3,2,1,0:T(8,128)(2,1)S(1)} %get-tuple-element.32), channel_id=1, source_target_pairs={{0,16},{16,0},{32,48},{48,32},{64,80},{80,64},{96,112},{112,96},{1... | collective-permute-start | bytes 1572872 | tf_op jit(solution)/shard_map/sum_over_core/ppermute | solution.py:272
  97.5 19.3 %all-to-all-start.3 = ((bf16[4,4,128,128]{3,2,1,0:T(8,128)(2,1)}), bf16[4,4,128,128]{3,2,1,0:T(8,128)(2,1)}, u32[]{:S(2)}, u32[]{:S(2)}) async-start(bf16[4,4,128,128]{3,2,1,0:T(8,128)(2,1)} %add_convert_fusion), calls=%async_computation.3 | async-start | bytes 1048576 | tf_op jit(solution)/shard_map/sum_over_z_lo/all_to_all | solution.py:282
  101.7 30.4 %copy-start.4 = (f32[256,128]{1,0:T(8,128)S(1)}, f32[256,128]{1,0:T(8,128)}, u32[]{:S(2)}) copy-start(f32[256,128]{1,0:T(8,128)} %get-tuple-element.44) | copy-start | bytes 393220
  101.7 24.6 %collective-permute-start.10 = (bf16[256,1024]{1,0:T(8,128)(2,1)S(1)}, bf16[256,1024]{1,0:T(8,128)(2,1)S(1)}, u32[]{:S(2)}, u32[]{:S(2)}) collective-permute-start(bf16[256,1024]{1,0:T(8,128)(2,1)S(1)} %bitcast.61), channel_id=1, source_target_pairs={{0,8},{1,9},{2,10},{3,11},{4,12},{5,13},{6,14},{7,15},{8,0},{9,1},... | collective-permute-start | bytes 1572872 | tf_op jit(solution)/shard_map/gather_over_x/ppermute | solution.py:278
  107.3 23.4 %collective-permute-start.11 = (bf16[256,1024]{1,0:T(8,128)(2,1)S(1)}, bf16[256,1024]{1,0:T(8,128)(2,1)S(1)}, u32[]{:S(2)}, u32[]{:S(2)}) collective-permute-start(bf16[256,1024]{1,0:T(8,128)(2,1)S(1)} %bitcast.62), channel_id=1, source_target_pairs={{0,4},{1,5},{2,6},{3,7},{4,8},{5,9},{6,10},{7,11},{8,12},{9,13},{1... | collective-permute-start | bytes 1572872 | tf_op jit(solution)/shard_map/gather_over_x/ppermute | solution.py:278
  109.2 21.5 %collective-permute-start.12 = (bf16[4,4,128,128]{3,2,1,0:T(8,128)(2,1)S(1)}, bf16[4,4,128,128]{3,2,1,0:T(8,128)(2,1)S(1)}, u32[]{:S(2)}, u32[]{:S(2)}) collective-permute-start(bf16[4,4,128,128]{3,2,1,0:T(8,128)(2,1)S(1)} %pad_maximum_fusion.w_own_ref), channel_id=1, source_target_pairs={{0,16},{16,0},{32,48},{48,32},{64,80},{80,64},{96,112},{112,96},{1... | collective-permute-start | bytes 1572872 | tf_op jit(solution)/shard_map/gather_projection/ppermute | solution.py:275
  111.1 19.6 %collective-permute-start.9 = (bf16[256,1024]{1,0:T(8,128)(2,1)S(1)}, bf16[256,1024]{1,0:T(8,128)(2,1)S(1)}, u32[]{:S(2)}, u32[]{:S(2)}) collective-permute-start(bf16[256,1024]{1,0:T(8,128)(2,1)S(1)} %bitcast.63), channel_id=1, source_target_pairs={{0,12},{1,13},{2,14},{3,15},{4,0},{5,1},{6,2},{7,3},{8,4},{9,5},{1... | collective-permute-start | bytes 1572872 | tf_op jit(solution)/shard_map/gather_over_x/ppermute | solution.py:278
  118.6 22.0 %all-to-all-start.4 = ((bf16[4,128,128]{2,1,0:T(8,128)(2,1)}), bf16[4,128,128]{2,1,0:T(8,128)(2,1)}, u32[]{:S(2)}, u32[]{:S(2)}) async-start(bf16[4,128,128]{2,1,0:T(8,128)(2,1)} %fusion.17), calls=%async_computation.4 | async-start | bytes 262144 | tf_op jit(solution)/shard_map/sum_over_z_hi/all_to_all | solution.py:287
  126.2 5.9 %copy-start.3 = (f32[256,1024]{1,0:T(8,128)S(1)}, f32[256,1024]{1,0:T(8,128)}, u32[]{:S(2)}) copy-start(f32[256,1024]{1,0:T(8,128)} %copy-done.2) | copy-start | bytes 3145732
  126.2 6.3 %copy-start.5 = (bf16[1,1024,128]{2,1,0:T(8,128)(2,1)S(1)}, bf16[1,1024,128]{2,1,0:T(8,128)(2,1)}, u32[]{:S(2)}) copy-start(bf16[1,1024,128]{2,1,0:T(8,128)(2,1)} %param.9) | copy-start | bytes 786436
  132.1 15.1 %copy-start.7 = (bf16[1,256,128]{2,1,0:T(8,128)(2,1)S(1)}, bf16[1,256,128]{2,1,0:T(8,128)(2,1)}, u32[]{:S(2)}) copy-start(bf16[1,256,128]{2,1,0:T(8,128)(2,1)} %param.8) | copy-start | bytes 196612
  141.4 16.9 %collective-permute-start.14 = (bf16[128,128]{1,0:T(8,128)(2,1)S(1)}, bf16[128,128]{1,0:T(8,128)(2,1)S(1)}, u32[]{:S(2)}, u32[]{:S(2)}) collective-permute-start(bf16[128,128]{1,0:T(8,128)(2,1)S(1)} %fusion.20), channel_id=1, source_target_pairs={{0,0},{1,1},{2,2},{3,3},{4,128},{5,129},{6,130},{7,131},{8,256},{9... | collective-permute-start | bytes 98312 | tf_op jit(solution)/shard_map/sum_over_z_hi/ppermute | solution.py:290
